TPU v7x, 512 devices: a whole 4x4x16 slice. The times are simulated.
512 devices in a mesh: ctx: 32 (over y, z_lo, core), layer: 16 (over z_hi, x).
Axes of the slice: x: 4, y: 4, z: 16 (z_hi: 4, z_lo: 4; z = z_hi * 4 + z_lo), core: 2. Of those that a mesh axis runs over, the one named last changes fastest.
Arguments:
- acts: bfloat16 [16, 4096, 8192], P('layer', 'ctx'), may hold values from -6 to 6
- grads_out: bfloat16 [16, 4096, 8192], P('layer', 'ctx'), may hold values from -6 to 6
- proj_in: bfloat16 [16, 8192, 128], P('layer', 'ctx'), may hold values from -0.0625 to 0.0625
- proj_out: bfloat16 [16, 8192, 128], P('layer', 'ctx'), may hold values from -0.0625 to 0.0625
- basis_a: float32 [16, 128, 128], P('layer'), may hold values from -1 to 1, as said below
- basis_g: float32 [16, 128, 128], P('layer'), may hold values from -1 to 1, as said below
- eig_a: float32 [16, 128], P('layer'), may hold values from 0.3 to 3
- eig_g: float32 [16, 128], P('layer'), may hold values from 0.3 to 3
- train_grads: bfloat16 [16, 512, 16384], P('layer', 'ctx'), may hold values from -0.75 to 0.75
Outputs:
- scores: float32 [512], P('ctx')
Inputs may be any that keep to these rules, and one draw needn't show every extreme that they name: Each basis_a[l] is an orthogonal matrix up to float32 rounding. Each basis_g[l] is an orthogonal matrix up to float32 rounding.
All inputs are finite; a program needn't handle non-finite values.
Results may differ from a plain program's by a relative error of at most 0.0051.
Values may be sent and summed in bfloat16 or wider, within the bound.
No kernel may reach another device: no remote copies, remote signals or barrier semaphores. Data moves between devices by JAX's collectives and lax.ppermute only.
A program may use at most 64 MiB of HBM per device.

v0:
```python
import jax
import jax.numpy as jnp
from jax import lax
from jax.sharding import PartitionSpec as P


def taken_in(shard, axis, dim):
    return jax.tree.map(lambda part: lax.all_gather(part, axis, axis=dim, tiled=True), shard)


def body(acts, grads_out, proj_in, proj_out, basis_a, basis_g, eig_a, eig_g, train_grads):
    highest = lax.Precision.HIGHEST
    total_tokens = acts.shape[1] * lax.axis_size("ctx")
    inputs = acts[0]
    outgrad = grads_out[0]
    pieces = taken_in((proj_in[0], proj_out[0]), "ctx", 1 - 1)
    sum_acts = jnp.dot(inputs, pieces[0], preferred_element_type=jnp.float32)
    sum_grads = jnp.dot(outgrad, pieces[1], preferred_element_type=jnp.float32)
    proj_acts = sum_acts.astype(jnp.bfloat16)
    proj_grads = sum_grads.astype(jnp.bfloat16)
    partial_value = (
        jnp.dot(proj_grads.T, proj_acts, preferred_element_type=jnp.float32) / total_tokens
    )
    rot_a = basis_a[0]
    rot_g = basis_g[0]
    denom = eig_g[0][:, None] * eig_a[0][None, :]
    summed = lax.psum(partial_value, "ctx")
    rotated = jnp.dot(jnp.dot(rot_g.T, summed, precision=highest), rot_a, precision=highest)
    whitened = rotated / denom
    precond = jnp.dot(jnp.dot(rot_g, whitened, precision=highest), rot_a.T, precision=highest)
    flat = precond.astype(jnp.bfloat16).reshape(-1)
    score_part = jnp.dot(train_grads[0], flat, preferred_element_type=jnp.float32)
    return lax.psum(score_part, "layer")


def solution(mesh):
    return jax.shard_map(
        body,
        mesh=mesh,
        in_specs=(
            P("layer", "ctx", None),
            P("layer", "ctx", None),
            P("layer", "ctx", None),
            P("layer", "ctx", None),
            P("layer", None, None),
            P("layer", None, None),
            P("layer", None),
            P("layer", None),
            P("layer", "ctx", None),
        ),
        out_specs=P("ctx"),
        check_vma=False,
    )
```

profile of v0, /device:TPU:32, one launch (start us, length us, event | category | flops | bytes accessed | tf_op | source)
XLA Modules:
  0.0 465.1 jit_solution(13726294143275943784)
XLA Ops:
  6.5 0.0 copy-start
  6.5 0.0 all-gather.5.cloned.1.call-start
  6.5 0.7 all-gather.5.cloned.1.call-update
  7.3 0.0 all-gather.7.cloned.1.call-start
  7.3 0.7 all-gather.7.cloned.1.call-update
  8.0 0.0 all-reduce.2.cloned.1.call-start
  8.1 70.1 %all-gather.5.cloned.1.call-done = bf16[1,8192,128]{2,1,0:T(8,128)(2,1)} async-done(((bf16[1,256,128]{2,1,0:T(8,128)(2,1)}), bf16[1,8192,128]{2,1,0:T(8,128)(2,1)}) %all-gather.5.cloned.1.call-update) | async-done | bytes 2097168 | tf_op jit(solution)/shard_map/all_gather | solution.py:8
  78.2 0.0 copy-done
  78.2 2.3 fusion.6
  80.5 0.0 copy-start.1
  80.5 0.0 copy-start.2
  80.5 0.0 copy-start.4
  80.5 0.0 copy-start.5
  80.5 0.0 copy-start.3
  80.5 63.7 %all-gather.7.cloned.1.call-done = bf16[1,8192,128]{2,1,0:T(8,128)(2,1)} async-done(((bf16[1,256,128]{2,1,0:T(8,128)(2,1)}), bf16[1,8192,128]{2,1,0:T(8,128)(2,1)}) %all-gather.7.cloned.1.call-update) | async-done | bytes 2097168 | tf_op jit(solution)/shard_map/all_gather | solution.py:8
  144.2 3.7 convolution_multiply_fusion
  147.9 0.0 all-reduce.2.cloned.1.call-update
  147.9 254.0 %all-reduce.2.cloned.1.call-done = f32[128,128]{1,0:T(8,128)} async-done(((f32[128,128]{1,0:T(8,128)}), f32[128,128]{1,0:T(8,128)}) %all-reduce.2.cloned.1.call-update) | async-done | bytes 65552 | tf_op jit(solution)/shard_map/psum | solution.py:27
  401.8 0.0 copy-done.1
  401.8 1.1 fusion.26
  403.0 0.0 copy-done.2
  403.0 0.0 copy-done.4
  403.0 0.0 copy-done.5
  403.0 0.3 convolution_divide_fusion
  403.3 0.3 fusion.24
  403.6 0.3 fusion.16
  403.9 0.0 copy-done.3
  403.9 0.3 convolution_bitcast_fusion
  404.2 54.3 %psum.15 = f32[16]{0:T(128)} all-reduce(f32[16]{0:T(128)S(1)} %convolution_bitcast_fusion), channel_id=1, replica_groups=mesh['ctx'=32,'layer'=16] {'layer'}, use_global_device_ids=true, to_apply=%region_1.0 | all-reduce | flops 16 | bytes 128 | tf_op jit(solution)/shard_map/psum | solution.py:33
  (1 shorter events, 0.0 us)
Async XLA Ops:
  6.5 71.7 %copy-start = (bf16[1,128,8192]{2,1,0:T(8,128)(2,1)S(1)}, bf16[1,128,8192]{2,1,0:T(8,128)(2,1)}, u32[]{:S(2)}) copy-start(bf16[1,128,8192]{2,1,0:T(8,128)(2,1)} %param.10) | copy-start | bytes 6291460
  6.5 71.6 %all-gather.5.cloned.1.call-start = ((), (), s32[]{:S(2)}) async-start(), calls=%async_computation.1 | async-start | bytes 2162688 | tf_op jit(solution)/shard_map/all_gather | solution.py:8
  7.3 136.9 %all-gather.7.cloned.1.call-start = ((), (), s32[]{:S(2)}) async-start(), calls=%async_computation.2 | async-start | bytes 2162688 | tf_op jit(solution)/shard_map/all_gather | solution.py:8
  8.0 393.8 %all-reduce.2.cloned.1.call-start = ((), (), s32[]{:S(2)}) async-start(), calls=%async_computation | async-start | bytes 131072 | tf_op jit(solution)/shard_map/psum | solution.py:27
  80.5 321.4 %copy-start.1 = (f32[1,128,128]{2,1,0:T(8,128)S(1)}, f32[1,128,128]{2,1,0:T(8,128)}, u32[]{:S(2)}) copy-start(f32[1,128,128]{2,1,0:T(8,128)} %param.14) | copy-start | bytes 196612
  80.5 322.5 %copy-start.2 = (f32[1,128,128]{2,1,0:T(8,128)S(1)}, f32[1,128,128]{2,1,0:T(8,128)}, u32[]{:S(2)}) copy-start(f32[1,128,128]{2,1,0:T(8,128)} %param.13) | copy-start | bytes 196612
  80.5 322.5 %copy-start.4 = (f32[1,128]{1,0:T(1,128)S(1)}, f32[1,128]{1,0:T(1,128)}, u32[]{:S(2)}) copy-start(f32[1,128]{1,0:T(1,128)} %param.15) | copy-start | bytes 1540
  80.5 322.5 %copy-start.5 = (f32[1,128]{1,0:T(1,128)S(1)}, f32[1,128]{1,0:T(1,128)}, u32[]{:S(2)}) copy-start(f32[1,128]{1,0:T(1,128)} %param.16) | copy-start | bytes 1540
  80.5 323.4 %copy-start.3 = (bf16[1,16,16384]{2,1,0:T(8,128)(2,1)S(1)}, bf16[1,16,16384]{2,1,0:T(8,128)(2,1)}, u32[]{:S(2)}) copy-start(bf16[1,16,16384]{2,1,0:T(8,128)(2,1)} %param.17) | copy-start | bytes 1572868
Sparse Core Ops, SparseCore 0:
  9.5 68.6 all-gather.4
  80.3 63.8 all-gather.6
  148.0 253.7 all-reduce.1
where the time goes:
time: 465 us
  waiting for transfers between devices  389 us (84%)
  blocking collectives  54.3 us (12%)
  between operations  13.2 us (3%)
  matrix products  8.22 us (2%)
    psum x1, waiting for transfers between devices, body(): summed = lax.psum(partial_value, 'ctx')  254 us
    all_gather x2, waiting for transfers between devices, taken_in(): lax.all_gather(part, axis, axis=dim, tiled=True)  134 us
    psum x1, blocking collectives, body(): return lax.psum(score_part, 'layer')  54.3 us
  transfers between devices with their start and end apart: 3, of which 3 were waited for; matrix products, arithmetic and copies ran while one was open for 0% of the time, Pallas kernels for 0%

commit v1 on v0

v1 whole, which is shorter than its diff:
```python
import functools

import jax
import jax.numpy as jnp
from jax import lax
from jax.experimental import pallas as pl
from jax.experimental.pallas import tpu as pltpu
from jax.sharding import Mesh, PartitionSpec as P

F32 = jnp.float32
BF16 = jnp.bfloat16
HIGHEST = lax.Precision.HIGHEST

CTX = ("y", "zlo", "core")
LAYER = ("zhi", "x")
VMEM = pl.BlockSpec(memory_space=pltpu.VMEM)
SMEM = pl.BlockSpec(memory_space=pltpu.SMEM)


def half_products(parity, acts_ref, grads_ref, rows_ref, acc_a, acc_g):
    blocks, _, depth, _ = rows_ref.shape
    for b in range(blocks):
        start = pl.multiple_of((2 * b + parity) * depth, depth)
        cols = pl.ds(start, depth)
        acc_a = acc_a + jnp.dot(acts_ref[:, cols], rows_ref[b, 0], preferred_element_type=F32)
        acc_g = acc_g + jnp.dot(grads_ref[:, cols], rows_ref[b, 1], preferred_element_type=F32)
    return acc_a, acc_g


def first_half(core_ref, acts_ref, grads_ref, rows_ref, out_a, out_g):
    zero = jnp.zeros(out_a.shape, F32)
    out_a[...], out_g[...] = half_products(core_ref[0], acts_ref, grads_ref, rows_ref, zero, zero)


def second_half(tokens, core_ref, acts_ref, grads_ref, rows_ref, in_a, in_g, out):
    acc_a, acc_g = half_products(
        1 - core_ref[0], acts_ref, grads_ref, rows_ref, in_a[...], in_g[...]
    )
    proj_a, proj_g = acc_a.astype(BF16), acc_g.astype(BF16)
    outer = lax.dot_general(
        proj_g, proj_a, (((0,), (0,)), ((), ())), preferred_element_type=F32
    )
    out[...] = outer / tokens


def score(parts_ref, basis_a, basis_g, eig_a, eig_g, train_ref, out):
    grad = parts_ref[0]
    for k in range(1, parts_ref.shape[0]):
        grad = grad + parts_ref[k]
    rot_a, rot_g = basis_a[...], basis_g[...]
    dot = functools.partial(
        lax.dot_general, precision=HIGHEST, preferred_element_type=F32
    )
    nn, tn, nt = (((1,), (0,)), ((), ())), (((0,), (0,)), ((), ())), (((1,), (1,)), ((), ()))
    turned = dot(dot(rot_g, grad, tn), rot_a, nn)
    rank = turned.shape[0]
    eye = (
        lax.broadcasted_iota(jnp.int32, (rank, rank), 0)
        == lax.broadcasted_iota(jnp.int32, (rank, rank), 1)
    )
    row_eig = jnp.sum(jnp.where(eye, jnp.broadcast_to(eig_g[...], (rank, rank)), 0.0), 1, keepdims=True)
    whitened = turned / (row_eig * eig_a[...])
    precond = dot(dot(rot_g, whitened, nn), rot_a, nt).astype(BF16).astype(F32)
    total = jnp.zeros((train_ref.shape[0], rank), F32)
    for i in range(rank):
        total = total + train_ref[:, i * rank:(i + 1) * rank].astype(F32) * precond[i:i + 1, :]
    out[...] = dot(jnp.ones((out.shape[0], rank), F32), total, nt)


def to_all(x, axis):
    size = lax.axis_size(axis)
    return lax.all_to_all(jnp.broadcast_to(x, (size,) + x.shape), axis, 0, 0)


def body(acts, grads_out, proj_in, proj_out, basis_a, basis_g, eig_a, eig_g, train_grads):
    tokens = acts.shape[1] * lax.axis_size(CTX)
    n_layer = lax.axis_size(LAYER)
    rank = proj_in.shape[-1]
    depth = proj_in.shape[1]
    swap = [(0, 1), (1, 0)]
    core = lax.axis_index("core").astype(jnp.int32).reshape(1)
    acts2, grads2 = acts[0], grads_out[0]
    n_tok = acts2.shape[0]

    mine = jnp.concatenate([proj_in, proj_out], 0)
    rows = to_all(to_all(mine, "zlo"), "y").reshape(-1, 2, depth, rank)
    theirs = lax.ppermute(rows, "core", swap)

    small = jax.ShapeDtypeStruct((n_tok, rank), F32)
    flops = 2 * n_tok * acts2.shape[1] * rank
    cost = pl.CostEstimate(flops=flops, bytes_accessed=6 << 20, transcendentals=0)
    acc = pl.pallas_call(
        first_half,
        out_shape=(small, small),
        in_specs=[SMEM, VMEM, VMEM, VMEM],
        out_specs=(VMEM, VMEM),
        cost_estimate=cost,
        name="first_half",
    )(core, acts2, grads2, rows)
    grad = pl.pallas_call(
        functools.partial(second_half, float(tokens)),
        out_shape=jax.ShapeDtypeStruct((rank, rank), F32),
        in_specs=[SMEM] + [VMEM] * 5,
        out_specs=VMEM,
        cost_estimate=cost,
        name="second_half",
    )(core, acts2, grads2, theirs, *acc)

    grad = grad + lax.ppermute(grad, "core", swap)
    grad = jnp.sum(to_all(grad, "y"), 0)
    parts = to_all(grad, "zlo")
    sent = pl.pallas_call(
        score,
        out_shape=jax.ShapeDtypeStruct((n_layer, train_grads.shape[1]), F32),
        in_specs=[VMEM] * 6,
        out_specs=VMEM,
        name="score",
    )(parts, basis_a[0], basis_g[0], eig_a, eig_g, train_grads[0])
    return jnp.sum(lax.all_to_all(sent, LAYER, 0, 0), 0)


def solution(mesh):
    devices = mesh.devices.reshape(4, 4, 2, 4, 4)
    fine = Mesh(devices, CTX + LAYER)
    return jax.shard_map(
        body,
        mesh=fine,
        in_specs=(
            P(LAYER, CTX, None),
            P(LAYER, CTX, None),
            P(LAYER, CTX, None),
            P(LAYER, CTX, None),
            P(LAYER, None, None),
            P(LAYER, None, None),
            P(LAYER, None),
            P(LAYER, None),
            P(LAYER, CTX, None),
        ),
        out_specs=P(CTX),
        check_vma=False,
    )
```

time: 465 us -> 121 us (0.26)
  the two profiles are of different devices: /device:TPU:32 before, /device:TPU:2 now
where the time goes in v1:
time: 121 us; the launch traced here: 120 us
  blocking collectives  100 us (83%)
  Pallas kernels  11.7 us (10%)
  starting transfers between devices  4.28 us (4%)
  other arithmetic  2.29 us (2%)
    all_to_all x4, blocking collectives, to_all(): return lax.all_to_all(jnp.broadcast_to(x, (size,) + x.shape), axis, 0, 0)  71.3 us
    all_to_all x1, blocking collectives, body(): return jnp.sum(lax.all_to_all(sent, LAYER, 0, 0), 0)  28.8 us
    pallas_call x1, Pallas kernels, body(): pl.pallas_call(functools.partial(second_half, float(tokens)), out_shape=j...  4.39 us
    pallas_call x1, Pallas kernels, body(): pl.pallas_call(first_half, out_shape=(small, small), in_specs=[SMEM, VMEM...  4.21 us
    pallas_call x1, Pallas kernels, body(): pl.pallas_call(score, out_shape=jax.ShapeDtypeStruct((n_layer, train_grad...  3.06 us
  transfers between devices with their start and end apart: 2, of which 1 were waited for; matrix products, arithmetic and copies ran while one was open for 0% of the time, Pallas kernels for 4%

profile of v1, /device:TPU:2, one launch (start us, length us, event | category | flops | bytes accessed | tf_op | source)
XLA Modules:
  0.0 120.1 jit_solution(6423353367727726033)
XLA Ops:
  0.0 0.9 pad_maximum_fusion
  0.9 0.1 broadcast_in_dim.12
  1.0 20.2 %all_to_all.29 = bf16[4,2,256,128]{3,2,1,0:T(8,128)(2,1)S(1)} all-to-all(bf16[4,2,256,128]{3,2,1,0:T(8,128)(2,1)S(1)} %broadcast_in_dim.12), channel_id=1, replica_groups=mesh['y'=4,'zlo'=4,'core'=2,'zhi'=4,'x'=4] {'zlo'}, dimensions={0} | all-to-all | bytes 1048576 | tf_op jit(solution)/shard_map/all_to_all | solution.py:72
  21.2 0.5 broadcast_in_dim.13
  21.6 29.5 %all_to_all.30 = bf16[4,4,2,256,128]{4,3,2,1,0:T(8,128)(2,1)S(1)} all-to-all(bf16[4,4,2,256,128]{4,3,2,1,0:T(8,128)(2,1)S(1)} %broadcast_in_dim.13), channel_id=1, replica_groups=mesh['y'=4,'zlo'=4,'core'=2,'zhi'=4,'x'=4] {'y'}, dimensions={0} | all-to-all | bytes 4194304 | tf_op jit(solution)/shard_map/all_to_all | solution.py:72
  51.1 0.0 copy-start
  51.1 1.9 %collective-permute-start = (bf16[16,2,256,128]{3,2,1,0:T(8,128)(2,1)S(1)}, bf16[16,2,256,128]{3,2,1,0:T(8,128)(2,1)}, u32[]{:S(2)}, u32[]{:S(2)}) collective-permute-start(bf16[16,2,256,128]{3,2,1,0:T(8,128)(2,1)S(1)} %bitcast.14), channel_id=1, source_target_pairs={{0,16},{16,0},{1,17},{17,1},{2,18},{18,2},{3,19},{19,3},{4,20},{20... | collective-permute-start | bytes 6291464 | tf_op jit(solution)/shard_map/ppermute | solution.py:87
  53.1 0.0 copy-done
  53.1 4.2 %first_half.1 = (f32[128,128]{1,0:T(8,128)}, f32[128,128]{1,0:T(8,128)}) custom-call(s32[1]{0:T(128)} %bitcast.core_ref, bf16[128,8192]{1,0:T(8,128)(2,1)} %bitcast.10, bf16[128,8192]{1,0:T(8,128)(2,1)} %bitcast.12, bf16[16,2,256,128]{3,2,1,0:T(8,128)(2,1)} %bitcast.15), custom_call_target="tpu_custom_call" | custom-call | flops 268435456 | bytes 6291456 | tf_op jit(solution)/shard_map/first_half/pallas_call | solution.py:92
  57.3 0.0 collective-permute-done.rows_ref
  57.3 4.4 %second_half.1 = f32[128,128]{1,0:T(8,128)} custom-call(s32[1]{0:T(128)} %bitcast.core_ref, bf16[128,8192]{1,0:T(8,128)(2,1)} %bitcast.11, bf16[128,8192]{1,0:T(8,128)(2,1)} %bitcast.13, bf16[16,2,256,128]{3,2,1,0:T(8,128)(2,1)} %collective-permute-done.rows_ref, f32[128,128]{1,0:T(8,128)} %get-tuple-element.7.in_a, f32[128,128]{1,0:T(8,128)} %get-tuple-element.8.in_g), custom_call_target="tpu_custom_call" | custom-call | flops 268435456 | bytes 6291456 | tf_op jit(solution)/shard_map/second_half/pallas_call | solution.py:100
  61.7 2.4 %collective-permute-start.1 = (f32[128,128]{1,0:T(8,128)}, f32[128,128]{1,0:T(8,128)S(1)}, u32[]{:S(2)}, u32[]{:S(2)}) collective-permute-start(f32[128,128]{1,0:T(8,128)} %second_half.1), channel_id=1, source_target_pairs={{0,16},{16,0},{1,17},{17,1},{2,18},{18,2},{3,19},{19,3},{4,20},{20... | collective-permute-start | bytes 196616 | tf_op jit(solution)/shard_map/ppermute | solution.py:109
  64.1 1.1 collective-permute-done.1
  65.2 0.8 add.3
  66.0 9.9 %all_to_all.31 = f32[4,128,128]{2,1,0:T(8,128)S(1)} all-to-all(f32[4,128,128]{2,1,0:T(8,128)S(1)} %broadcast_in_dim.14), channel_id=1, replica_groups=mesh['y'=4,'zlo'=4,'core'=2,'zhi'=4,'x'=4] {'y'}, dimensions={0} | all-to-all | bytes 524288 | tf_op jit(solution)/shard_map/all_to_all | solution.py:72
  75.9 11.7 %all_to_all.32.parts_ref = f32[4,128,128]{2,1,0:T(8,128)} all-to-all(f32[4,128,128]{2,1,0:T(8,128)S(1)} %broadcast_in_dim.15), channel_id=1, replica_groups=mesh['y'=4,'zlo'=4,'core'=2,'zhi'=4,'x'=4] {'zlo'}, dimensions={0} | all-to-all | bytes 524288 | tf_op jit(solution)/shard_map/all_to_all | solution.py:72
  87.6 3.1 %score.1 = f32[16,16]{1,0:T(8,128)} custom-call(f32[4,128,128]{2,1,0:T(8,128)} %all_to_all.32.parts_ref, f32[128,128]{1,0:T(8,128)} %bitcast.17, f32[128,128]{1,0:T(8,128)} %bitcast.18, f32[1,128]{1,0:T(1,128)} %eig_a.1, f32[1,128]{1,0:T(1,128)} %eig_g.1, bf16[16,16384]{1,0:T(8,128)(2,1)} %bitcast.16), custom_call_target="tpu_custom_call" | custom-call | tf_op jit(solution)/shard_map/score/pallas_call | solution.py:112
  90.7 28.8 %all_to_all.33 = f32[16,1,16]{2,1,0:T(1,128)S(1)} all-to-all(f32[16,1,16]{2,1,0:T(1,128)} %bitcast.19), channel_id=1, replica_groups=mesh['y'=4,'zlo'=4,'core'=2,'zhi'=4,'x'=4] {'zhi','x'}, dimensions={0} | all-to-all | bytes 2048 | tf_op jit(solution)/shard_map/all_to_all | solution.py:119
  119.5 0.5 reduce_sum.19
  (3 shorter events, 0.1 us)
Async XLA Ops:
  51.1 1.9 %copy-start = (bf16[4,4,2,256,128]{4,3,2,1,0:T(8,128)(2,1)}, bf16[4,4,2,256,128]{4,3,2,1,0:T(8,128)(2,1)S(1)}, u32[]{:S(2)}) copy-start(bf16[4,4,2,256,128]{4,3,2,1,0:T(8,128)(2,1)S(1)} %all_to_all.30) | copy-start | bytes 6291460
  51.1 6.2 %collective-permute-start = (bf16[16,2,256,128]{3,2,1,0:T(8,128)(2,1)S(1)}, bf16[16,2,256,128]{3,2,1,0:T(8,128)(2,1)}, u32[]{:S(2)}, u32[]{:S(2)}) collective-permute-start(bf16[16,2,256,128]{3,2,1,0:T(8,128)(2,1)S(1)} %bitcast.14), channel_id=1, source_target_pairs={{0,16},{16,0},{1,17},{17,1},{2,18},{18,2},{3,19},{19,3},{4,20},{20... | collective-permute-start | bytes 6291464 | tf_op jit(solution)/shard_map/ppermute | solution.py:87
  61.7 3.5 %collective-permute-start.1 = (f32[128,128]{1,0:T(8,128)}, f32[128,128]{1,0:T(8,128)S(1)}, u32[]{:S(2)}, u32[]{:S(2)}) collective-permute-start(f32[128,128]{1,0:T(8,128)} %second_half.1), channel_id=1, source_target_pairs={{0,16},{16,0},{1,17},{17,1},{2,18},{18,2},{3,19},{19,3},{4,20},{20... | collective-permute-start | bytes 196616 | tf_op jit(solution)/shard_map/ppermute | solution.py:109

commit v2 on v1

v2 whole, which is shorter than its diff:
```python
import functools

import jax
import jax.numpy as jnp
from jax import lax
from jax.experimental import pallas as pl
from jax.experimental.pallas import tpu as pltpu
from jax.sharding import Mesh, PartitionSpec as P


F32 = jnp.float32
BF16 = jnp.bfloat16
HIGHEST = lax.Precision.HIGHEST

CTX = ("y", "zlo", "core")
LAYER = ("zhi", "x")
VMEM = pl.BlockSpec(memory_space=pltpu.VMEM)
SMEM = pl.BlockSpec(memory_space=pltpu.SMEM)


def products(pieces, here_ref, acts_ref, grads_ref, row_refs, acc_a, acc_g):
    n_y, n_z = here_ref[2], here_ref[3]
    for (blocks, flip), rows_ref in zip(pieces, row_refs):
        depth = rows_ref.shape[2]
        core = 1 - here_ref[1] if flip else here_ref[1]
        for k, (step, z) in enumerate(blocks):
            line = lax.rem(here_ref[0] + step, n_y) * n_z
            start = pl.multiple_of(((line + z) * 2 + core) * depth, depth)
            cols = pl.ds(start, depth)
            acc_a = acc_a + jnp.dot(acts_ref[:, cols], rows_ref[k, 0], preferred_element_type=F32)
            acc_g = acc_g + jnp.dot(grads_ref[:, cols], rows_ref[k, 1], preferred_element_type=F32)
    return acc_a, acc_g


def begin(pieces, here_ref, acts_ref, grads_ref, *refs):
    rows, (out_a, out_g) = refs[:-2], refs[-2:]
    zero = jnp.zeros(out_a.shape, F32)
    out_a[...], out_g[...] = products(pieces, here_ref, acts_ref, grads_ref, rows, zero, zero)


def go_on(pieces, here_ref, acts_ref, grads_ref, *refs):
    rows, (in_a, in_g, out_a, out_g) = refs[:-4], refs[-4:]
    out_a[...], out_g[...] = products(
        pieces, here_ref, acts_ref, grads_ref, rows, in_a[...], in_g[...]
    )


def finish(tokens, pieces, here_ref, acts_ref, grads_ref, *refs):
    rows, (in_a, in_g, out) = refs[:-3], refs[-3:]
    acc_a, acc_g = products(pieces, here_ref, acts_ref, grads_ref, rows, in_a[...], in_g[...])
    proj_a, proj_g = acc_a.astype(BF16), acc_g.astype(BF16)
    outer = lax.dot_general(
        proj_g, proj_a, (((0,), (0,)), ((), ())), preferred_element_type=F32
    )
    out[...] = outer / tokens


def score(parts_ref, basis_a, basis_g, eig_a, eig_g, train_ref, out):
    grad = parts_ref[0]
    for k in range(1, parts_ref.shape[0]):
        grad = grad + parts_ref[k]
    rot_a, rot_g = basis_a[...], basis_g[...]
    dot = functools.partial(
        lax.dot_general, precision=HIGHEST, preferred_element_type=F32
    )
    nn, tn, nt = (((1,), (0,)), ((), ())), (((0,), (0,)), ((), ())), (((1,), (1,)), ((), ()))
    turned = dot(dot(rot_g, grad, tn), rot_a, nn)
    rank = turned.shape[0]
    eye = (
        lax.broadcasted_iota(jnp.int32, (rank, rank), 0)
        == lax.broadcasted_iota(jnp.int32, (rank, rank), 1)
    )
    row_eig = jnp.sum(jnp.where(eye, jnp.broadcast_to(eig_g[...], (rank, rank)), 0.0), 1, keepdims=True)
    whitened = turned / (row_eig * eig_a[...])
    precond = dot(dot(rot_g, whitened, nn), rot_a, nt).astype(BF16).astype(F32)
    total = jnp.zeros((train_ref.shape[0], rank), F32)
    for i in range(rank):
        total = total + train_ref[:, i * rank:(i + 1) * rank].astype(F32) * precond[i:i + 1, :]
    out[...] = dot(jnp.ones((out.shape[0], rank), F32), total, nt)


def to_all(x, axis):
    size = lax.axis_size(axis)
    return lax.all_to_all(jnp.broadcast_to(x, (size,) + x.shape), axis, 0, 0)


def ring(size, step):
    return [(i, (i + step) % size) for i in range(size)]


def body(acts, grads_out, proj_in, proj_out, basis_a, basis_g, eig_a, eig_g, train_grads):
    tokens = acts.shape[1] * lax.axis_size(CTX)
    n_layer = lax.axis_size(LAYER)
    n_y, n_z = lax.axis_size("y"), lax.axis_size("zlo")
    rank = proj_in.shape[-1]
    half = n_z // 2
    acts2, grads2 = acts[0], grads_out[0]
    n_tok = acts2.shape[0]
    here = jnp.stack(
        [lax.axis_index("y"), lax.axis_index("core"), jnp.int32(n_y), jnp.int32(n_z)]
    ).astype(jnp.int32)

    def up(x):
        return lax.ppermute(x, "y", ring(n_y, 1))

    def down(x):
        return lax.ppermute(x, "y", ring(n_y, -1))

    def swap(x):
        return lax.ppermute(x, "core", ring(2, 1))

    def call(kernel, rows, acc, out_shape):
        count = sum(r.shape[0] for r in rows)
        flops = 4 * n_tok * count * rows[0].shape[2] * rank
        return pl.pallas_call(
            kernel,
            out_shape=out_shape,
            in_specs=[SMEM] + [VMEM] * (2 + len(rows) + len(acc)),
            out_specs=jax.tree.map(lambda _: VMEM, out_shape),
            cost_estimate=pl.CostEstimate(flops=flops, bytes_accessed=count << 17, transcendentals=0),
            compiler_params=pltpu.CompilerParams(vmem_limit_bytes=20 << 20),
        )(here, acts2, grads2, *rows, *acc)

    mine = jnp.concatenate([proj_in, proj_out], 0)
    line = to_all(mine, "zlo")
    low, high = line[:half], line[half:]
    from_below_low = up(low)
    from_above_high = down(high)
    from_below_high = up(high)
    from_above_low = down(low)
    other_line = swap(line)
    far_low = up(from_below_low)
    far_high = down(from_above_high)
    near = jnp.concatenate([from_below_low, from_below_high, from_above_low, from_above_high], 0)
    other_near = swap(near)
    far = jnp.concatenate([far_low, far_high], 0)
    other_far = swap(far)

    def row(step):
        return [(step, z) for z in range(n_z)]

    below, above, opposite = n_y - 1, 1, n_y // 2
    small = jax.ShapeDtypeStruct((n_tok, rank), F32)
    acc = call(
        functools.partial(begin, [
            (row(0), False),
            (row(below)[:half], False),
            (row(below)[half:], False),
            (row(above)[:half], False),
            (row(above)[half:], False),
        ]),
        [line, from_below_low, from_below_high, from_above_low, from_above_high],
        (), (small, small),
    )
    acc = call(
        functools.partial(go_on, [
            (row(0), True),
            (row(below) + row(above), True),
            (row(opposite), False),
        ]),
        [other_line, other_near, far], acc, (small, small),
    )
    grad = call(
        functools.partial(finish, float(tokens), [(row(opposite), True)]),
        [other_far], acc, jax.ShapeDtypeStruct((rank, rank), F32),
    )

    grad = grad + swap(grad)
    grad = jnp.sum(to_all(grad, "y"), 0)
    parts = to_all(grad, "zlo")
    sent = pl.pallas_call(
        score,
        out_shape=jax.ShapeDtypeStruct((n_layer, train_grads.shape[1]), F32),
        in_specs=[VMEM] * 6,
        out_specs=VMEM,
        compiler_params=pltpu.CompilerParams(vmem_limit_bytes=20 << 20),
        name="score",
    )(parts, basis_a[0], basis_g[0], eig_a, eig_g, train_grads[0])
    return jnp.sum(lax.all_to_all(sent, LAYER, 0, 0), 0)


def solution(mesh):
    devices = mesh.devices.reshape(4, 4, 2, 4, 4)
    fine = Mesh(devices, CTX + LAYER)
    return jax.shard_map(
        body,
        mesh=fine,
        in_specs=(
            P(LAYER, CTX, None),
            P(LAYER, CTX, None),
            P(LAYER, CTX, None),
            P(LAYER, CTX, None),
            P(LAYER, None, None),
            P(LAYER, None, None),
            P(LAYER, None),
            P(LAYER, None),
            P(LAYER, CTX, None),
        ),
        out_specs=P(CTX),
        check_vma=False,
    )
```

time: 121 us -> 125 us (1.033)
  blocking collectives: 100 us -> 72 us
  starting transfers between devices: 4.28 us -> 30.2 us
  waiting for transfers between devices: 1.12 us -> 8.76 us
  Pallas kernels: 11.7 us -> 5.98 us
  local copies, waits for them, and re-layouts: 0.57 us -> 4.69 us
    all_to_all x4 -> x3, blocking collectives: 71.3 us -> 43.4 us  [to_all(): return lax.all_to_all(jnp.broadcast_to(x, (size,) + x.shape), axis, 0, 0)]
    ppermute x2 -> x10, starting transfers between devices: 4.28 us -> 30.2 us  [the longest x3 12.7 us: down(): return lax.ppermute(x, 'y', ring(n_y, -1))]
    ppermute x2 -> x10, waiting for transfers between devices: 1.12 us -> 8.76 us  [the longest x3 5.35 us: up(): return lax.ppermute(x, 'y', ring(n_y, 1))]
    unnamed x2 -> x27, local copies, waits for them, and re-layouts: 0.01 us -> 4.51 us
    pallas_call x2 -> x3, Pallas kernels: 8.6 us -> 4.74 us  [call(): pl.pallas_call(kernel, out_shape=out_shape, in_specs=[SMEM] + [VMEM] * (2...]
    pallas_call x1, Pallas kernels: 3.06 us -> 1.24 us  [body(): pl.pallas_call(score, out_shape=jax.ShapeDtypeStruct((n_layer, train_grad...]
  transfers between devices with their start and end apart: 2 -> 10, of which waited for: 1 -> 5; matrix products, arithmetic and copies ran while one was open for 0% -> 0% of each run, Pallas kernels for 4% -> 3%
where the time goes in v2:
time: 125 us
  blocking collectives  72 us (58%)
  starting transfers between devices  30.2 us (24%)
  waiting for transfers between devices  8.76 us (7%)
  Pallas kernels  5.98 us (5%)
  local copies, waits for them, and re-layouts  4.69 us (4%)
  other arithmetic  2.66 us (2%)
    all_to_all x3, blocking collectives, to_all(): return lax.all_to_all(jnp.broadcast_to(x, (size,) + x.shape), axis, 0, 0)  43.4 us
    all_to_all x1, blocking collectives, body(): return jnp.sum(lax.all_to_all(sent, LAYER, 0, 0), 0)  28.6 us
    ppermute x3, starting transfers between devices, down(): return lax.ppermute(x, 'y', ring(n_y, -1))  12.7 us
    ppermute x3, starting transfers between devices, up(): return lax.ppermute(x, 'y', ring(n_y, 1))  9.06 us
    ppermute x4, starting transfers between devices, swap(): return lax.ppermute(x, 'core', ring(2, 1))  8.49 us
    ppermute x3, waiting for transfers between devices, up(): return lax.ppermute(x, 'y', ring(n_y, 1))  5.35 us
    pallas_call x3, Pallas kernels, call(): pl.pallas_call(kernel, out_shape=out_shape, in_specs=[SMEM] + [VMEM] * (2...  4.74 us
    unnamed x27, local copies, waits for them, and re-layouts  4.51 us
  transfers between devices with their start and end apart: 10, of which 5 were waited for; matrix products, arithmetic and copies ran while one was open for 0% of the time, Pallas kernels for 3%

profile of v2, /device:TPU:2, one launch (start us, length us, event | category | flops | bytes accessed | tf_op | source)
XLA Modules:
  0.0 124.7 jit_solution(16369861803524151106)
XLA Ops:
  0.0 0.9 pad_maximum_fusion.1
  0.9 0.1 broadcast_in_dim.9
  1.0 20.2 %all_to_all.24.refs_0_ = bf16[4,2,256,128]{3,2,1,0:T(8,128)(2,1)S(1)} all-to-all(bf16[4,2,256,128]{3,2,1,0:T(8,128)(2,1)S(1)} %broadcast_in_dim.9), channel_id=1, replica_groups=mesh['y'=4,'zlo'=4,'core'=2,'zhi'=4,'x'=4] {'zlo'}, dimensions={0} | all-to-all | bytes 1048576 | tf_op jit(solution)/shard_map/all_to_all | solution.py:84
  21.2 3.6 %collective-permute-start = (bf16[2,2,256,128]{3,2,1,0:T(8,128)(2,1)S(1)}, bf16[2,2,256,128]{3,2,1,0:T(8,128)(2,1)S(1)}, u32[]{:S(2)}, u32[]{:S(2)}) collective-permute-start(bf16[2,2,256,128]{3,2,1,0:T(8,128)(2,1)S(1)} %get-tuple-element.14), channel_id=1, source_target_pairs={{0,128},{128,256},{256,384},{384,0},{1,129},{129,257},{257,385},{3... | collective-permute-start | bytes 786440 | tf_op jit(solution)/shard_map/ppermute | solution.py:104
  24.8 3.6 %collective-permute-start.2 = (bf16[2,2,256,128]{3,2,1,0:T(8,128)(2,1)S(1)}, bf16[2,2,256,128]{3,2,1,0:T(8,128)(2,1)S(1)}, u32[]{:S(2)}, u32[]{:S(2)}) collective-permute-start(bf16[2,2,256,128]{3,2,1,0:T(8,128)(2,1)S(1)} %get-tuple-element.13), channel_id=1, source_target_pairs={{0,384},{128,0},{256,128},{384,256},{1,385},{129,1},{257,129},{385... | collective-permute-start | bytes 786440 | tf_op jit(solution)/shard_map/ppermute | solution.py:107
  28.4 2.3 %collective-permute-start.6 = (bf16[2,2,256,128]{3,2,1,0:T(8,128)(2,1)S(1)}, bf16[2,2,256,128]{3,2,1,0:T(8,128)(2,1)S(1)}, u32[]{:S(2)}, u32[]{:S(2)}) collective-permute-start(bf16[2,2,256,128]{3,2,1,0:T(8,128)(2,1)S(1)} %get-tuple-element.13), channel_id=1, source_target_pairs={{0,128},{128,256},{256,384},{384,0},{1,129},{129,257},{257,385},{3... | collective-permute-start | bytes 786440 | tf_op jit(solution)/shard_map/ppermute | solution.py:104
  30.7 4.8 %collective-permute-start.7 = (bf16[2,2,256,128]{3,2,1,0:T(8,128)(2,1)S(1)}, bf16[2,2,256,128]{3,2,1,0:T(8,128)(2,1)S(1)}, u32[]{:S(2)}, u32[]{:S(2)}) collective-permute-start(bf16[2,2,256,128]{3,2,1,0:T(8,128)(2,1)S(1)} %get-tuple-element.14), channel_id=1, source_target_pairs={{0,384},{128,0},{256,128},{384,256},{1,385},{129,1},{257,129},{385... | collective-permute-start | bytes 786440 | tf_op jit(solution)/shard_map/ppermute | solution.py:107
  35.5 0.0 collective-permute-done.refs_1_
  35.5 0.0 collective-permute-done.2.refs_4_
  35.5 0.0 copy-start.2
  35.5 2.5 %collective-permute-done.6.refs_2_ = bf16[2,2,256,128]{3,2,1,0:T(8,128)(2,1)S(1)} collective-permute-done((bf16[2,2,256,128]{3,2,1,0:T(8,128)(2,1)S(1)}, bf16[2,2,256,128]{3,2,1,0:T(8,128)(2,1)S(1)}, u32[]{:S(2)}, u32[]{:S(2)}) %collective-permute-start.6) | collective-permute-done | bytes 262176 | tf_op jit(solution)/shard_map/ppermute | solution.py:104
  38.0 1.4 %collective-permute-done.7.refs_3_ = bf16[2,2,256,128]{3,2,1,0:T(8,128)(2,1)S(1)} collective-permute-done((bf16[2,2,256,128]{3,2,1,0:T(8,128)(2,1)S(1)}, bf16[2,2,256,128]{3,2,1,0:T(8,128)(2,1)S(1)}, u32[]{:S(2)}, u32[]{:S(2)}) %collective-permute-start.7) | collective-permute-done | bytes 262176 | tf_op jit(solution)/shard_map/ppermute | solution.py:107
  39.3 1.1 pad_maximum_fusion
  40.5 1.9 %collective-permute-start.8 = (bf16[8,2,256,128]{3,2,1,0:T(8,128)(2,1)}, bf16[8,2,256,128]{3,2,1,0:T(8,128)(2,1)}, u32[]{:S(2)}, u32[]{:S(2)}) collective-permute-start(bf16[8,2,256,128]{3,2,1,0:T(8,128)(2,1)} %pad_maximum_fusion), channel_id=1, source_target_pairs={{0,16},{16,0},{1,17},{17,1},{2,18},{18,2},{3,19},{19,3},{4,20},{20... | collective-permute-start | bytes 3145736 | tf_op jit(solution)/shard_map/ppermute | solution.py:110
  42.4 3.2 %collective-permute-start.1 = (bf16[2,2,256,128]{3,2,1,0:T(8,128)(2,1)S(1)}, bf16[2,2,256,128]{3,2,1,0:T(8,128)(2,1)S(1)}, u32[]{:S(2)}, u32[]{:S(2)}) collective-permute-start(bf16[2,2,256,128]{3,2,1,0:T(8,128)(2,1)S(1)} %collective-permute-done.refs_1_), channel_id=1, source_target_pairs={{0,128},{128,256},{256,384},{384,0},{1,129},{129,257},{257,385},{3... | collective-permute-start | bytes 786440 | tf_op jit(solution)/shard_map/ppermute | solution.py:104
  45.6 4.4 %collective-permute-start.3 = (bf16[2,2,256,128]{3,2,1,0:T(8,128)(2,1)S(1)}, bf16[2,2,256,128]{3,2,1,0:T(8,128)(2,1)S(1)}, u32[]{:S(2)}, u32[]{:S(2)}) collective-permute-start(bf16[2,2,256,128]{3,2,1,0:T(8,128)(2,1)S(1)} %collective-permute-done.2.refs_4_), channel_id=1, source_target_pairs={{0,384},{128,0},{256,128},{384,256},{1,385},{129,1},{257,129},{385... | collective-permute-start | bytes 786440 | tf_op jit(solution)/shard_map/ppermute | solution.py:107
  49.9 2.1 %collective-permute-start.5 = (bf16[4,2,256,128]{3,2,1,0:T(8,128)(2,1)S(1)}, bf16[4,2,256,128]{3,2,1,0:T(8,128)(2,1)}, u32[]{:S(2)}, u32[]{:S(2)}) collective-permute-start(bf16[4,2,256,128]{3,2,1,0:T(8,128)(2,1)S(1)} %all_to_all.24.refs_0_), channel_id=1, source_target_pairs={{0,16},{16,0},{1,17},{17,1},{2,18},{18,2},{3,19},{19,3},{4,20},{20... | collective-permute-start | bytes 1572872 | tf_op jit(solution)/shard_map/ppermute | solution.py:110
  52.0 0.0 copy-done.4
  52.1 0.0 copy-done.6
  52.1 2.9 %collective-permute-done.1 = bf16[2,2,256,128]{3,2,1,0:T(8,128)(2,1)S(1)} collective-permute-done((bf16[2,2,256,128]{3,2,1,0:T(8,128)(2,1)S(1)}, bf16[2,2,256,128]{3,2,1,0:T(8,128)(2,1)S(1)}, u32[]{:S(2)}, u32[]{:S(2)}) %collective-permute-start.1) | collective-permute-done | bytes 262176 | tf_op jit(solution)/shard_map/ppermute | solution.py:104
  55.0 1.2 collective-permute-done.3
  56.2 0.0 copy-done.2
  56.2 1.9 %collective-permute-start.4 = (bf16[4,2,256,128]{3,2,1,0:T(8,128)(2,1)S(1)}, bf16[4,2,256,128]{3,2,1,0:T(8,128)(2,1)}, u32[]{:S(2)}, u32[]{:S(2)}) collective-permute-start(bf16[4,2,256,128]{3,2,1,0:T(8,128)(2,1)S(1)} %constant_dynamic-update-slice_fusion.refs_2_), channel_id=1, source_target_pairs={{0,16},{16,0},{1,17},{17,1},{2,18},{18,2},{3,19},{19,3},{4,20},{20... | collective-permute-start | bytes 1572872 | tf_op jit(solution)/shard_map/ppermute | solution.py:110
  58.1 0.1 pad_add_fusion.here_ref
  58.2 0.0 copy-done
  58.2 1.6 %copy-done.1 = bf16[1,128,8192]{2,1,0:T(8,128)(2,1)S(1)} copy-done((bf16[1,128,8192]{2,1,0:T(8,128)(2,1)S(1)}, bf16[1,128,8192]{2,1,0:T(8,128)(2,1)}, u32[]{:S(2)}) %copy-start.1) | copy-done | bytes 2097176
  59.8 0.9 copy-done.3
  60.7 0.9 copy-done.5
  61.7 0.9 copy-done.7
  62.6 1.1 shard_map.91
  63.8 0.0 collective-permute-done.5.refs_0_
  63.8 0.0 collective-permute-done.8.refs_1_
  63.8 2.1 %shard_map.92 = (f32[128,128]{1,0:T(8,128)S(1)}, f32[128,128]{1,0:T(8,128)S(1)}) custom-call(s32[4]{0:T(128)S(1)} %pad_add_fusion.here_ref, bf16[128,8192]{1,0:T(8,128)(2,1)S(1)} %bitcast.11, bf16[128,8192]{1,0:T(8,128)(2,1)S(1)} %bitcast.14, bf16[4,2,256,128]{3,2,1,0:T(8,128)(2,1)} %collective-permute-done.5.refs_0_, ...), custom_call_target="tpu_custom_call" | custom-call | flops 268435456 | bytes 2097152 | tf_op jit(solution)/shard_map/pallas_call | solution.py:115
  65.9 0.0 collective-permute-done.4.refs_0_
  65.9 1.5 %shard_map.93 = f32[128,128]{1,0:T(8,128)S(1)} custom-call(s32[4]{0:T(128)S(1)} %pad_add_fusion.here_ref, bf16[128,8192]{1,0:T(8,128)(2,1)S(1)} %bitcast.12, bf16[128,8192]{1,0:T(8,128)(2,1)S(1)} %bitcast.15, bf16[4,2,256,128]{3,2,1,0:T(8,128)(2,1)} %collective-permute-done.4.refs_0_, f32[128,128]{1,0:T(8,128)S(1)} %get-tuple-element.11.refs_1_, ...), custom_call_target="tpu_custom_call" | custom-call | flops 67108864 | bytes 524288 | tf_op jit(solution)/shard_map/pallas_call | solution.py:115
  67.4 0.0 copy-start.8
  67.5 0.0 copy-start.9
  67.5 0.0 copy-start.10
  67.5 0.0 copy-start.11
  67.5 0.0 copy-start.12
  67.5 2.5 %collective-permute-start.9 = (f32[128,128]{1,0:T(8,128)S(1)}, f32[128,128]{1,0:T(8,128)S(1)}, u32[]{:S(2)}, u32[]{:S(2)}) collective-permute-start(f32[128,128]{1,0:T(8,128)S(1)} %shard_map.93), channel_id=1, source_target_pairs={{0,16},{16,0},{1,17},{17,1},{2,18},{18,2},{3,19},{19,3},{4,20},{20... | collective-permute-start | bytes 196616 | tf_op jit(solution)/shard_map/ppermute | solution.py:110
  70.0 0.9 collective-permute-done.9
  71.0 11.9 %all_to_all.25 = f32[4,128,128]{2,1,0:T(8,128)S(1)} all-to-all(f32[4,128,128]{2,1,0:T(8,128)S(1)} %broadcast_in_dim.10), channel_id=1, replica_groups=mesh['y'=4,'zlo'=4,'core'=2,'zhi'=4,'x'=4] {'y'}, dimensions={0} | all-to-all | bytes 524288 | tf_op jit(solution)/shard_map/all_to_all | solution.py:84
  83.0 11.3 %all_to_all.26.parts_ref = f32[4,128,128]{2,1,0:T(8,128)S(1)} all-to-all(f32[4,128,128]{2,1,0:T(8,128)S(1)} %broadcast_in_dim.11), channel_id=1, replica_groups=mesh['y'=4,'zlo'=4,'core'=2,'zhi'=4,'x'=4] {'zlo'}, dimensions={0} | all-to-all | bytes 524288 | tf_op jit(solution)/shard_map/all_to_all | solution.py:84
  94.2 0.0 copy-done.9
  94.2 1.2 score.1
  95.5 28.6 %all_to_all.27 = f32[16,1,16]{2,1,0:T(1,128)S(1)} all-to-all(f32[16,1,16]{2,1,0:T(1,128)S(1)} %bitcast.19), channel_id=1, replica_groups=mesh['y'=4,'zlo'=4,'core'=2,'zhi'=4,'x'=4] {'zhi','x'}, dimensions={0} | all-to-all | bytes 2048 | tf_op jit(solution)/shard_map/all_to_all | solution.py:179
  124.1 0.5 reduce_sum.19
  (19 shorter events, 0.2 us)
Async XLA Ops:
  21.2 37.0 %copy-start = (bf16[1,128,8192]{2,1,0:T(8,128)(2,1)S(1)}, bf16[1,128,8192]{2,1,0:T(8,128)(2,1)}, u32[]{:S(2)}) copy-start(bf16[1,128,8192]{2,1,0:T(8,128)(2,1)} %param.9) | copy-start | bytes 6291460
  21.2 14.3 %collective-permute-start = (bf16[2,2,256,128]{3,2,1,0:T(8,128)(2,1)S(1)}, bf16[2,2,256,128]{3,2,1,0:T(8,128)(2,1)S(1)}, u32[]{:S(2)}, u32[]{:S(2)}) collective-permute-start(bf16[2,2,256,128]{3,2,1,0:T(8,128)(2,1)S(1)} %get-tuple-element.14), channel_id=1, source_target_pairs={{0,128},{128,256},{256,384},{384,0},{1,129},{129,257},{257,385},{3... | collective-permute-start | bytes 786440 | tf_op jit(solution)/shard_map/ppermute | solution.py:104
  24.8 10.7 %collective-permute-start.2 = (bf16[2,2,256,128]{3,2,1,0:T(8,128)(2,1)S(1)}, bf16[2,2,256,128]{3,2,1,0:T(8,128)(2,1)S(1)}, u32[]{:S(2)}, u32[]{:S(2)}) collective-permute-start(bf16[2,2,256,128]{3,2,1,0:T(8,128)(2,1)S(1)} %get-tuple-element.13), channel_id=1, source_target_pairs={{0,384},{128,0},{256,128},{384,256},{1,385},{129,1},{257,129},{385... | collective-permute-start | bytes 786440 | tf_op jit(solution)/shard_map/ppermute | solution.py:107
  28.4 9.6 %collective-permute-start.6 = (bf16[2,2,256,128]{3,2,1,0:T(8,128)(2,1)S(1)}, bf16[2,2,256,128]{3,2,1,0:T(8,128)(2,1)S(1)}, u32[]{:S(2)}, u32[]{:S(2)}) collective-permute-start(bf16[2,2,256,128]{3,2,1,0:T(8,128)(2,1)S(1)} %get-tuple-element.13), channel_id=1, source_target_pairs={{0,128},{128,256},{256,384},{384,0},{1,129},{129,257},{257,385},{3... | collective-permute-start | bytes 786440 | tf_op jit(solution)/shard_map/ppermute | solution.py:104
  30.7 8.7 %collective-permute-start.7 = (bf16[2,2,256,128]{3,2,1,0:T(8,128)(2,1)S(1)}, bf16[2,2,256,128]{3,2,1,0:T(8,128)(2,1)S(1)}, u32[]{:S(2)}, u32[]{:S(2)}) collective-permute-start(bf16[2,2,256,128]{3,2,1,0:T(8,128)(2,1)S(1)} %get-tuple-element.14), channel_id=1, source_target_pairs={{0,384},{128,0},{256,128},{384,256},{1,385},{129,1},{257,129},{385... | collective-permute-start | bytes 786440 | tf_op jit(solution)/shard_map/ppermute | solution.py:107
  35.5 20.7 %copy-start.2 = (bf16[2,2,256,128]{3,2,1,0:T(8,128)(2,1)}, bf16[2,2,256,128]{3,2,1,0:T(8,128)(2,1)S(1)}, u32[]{:S(2)}) copy-start(bf16[2,2,256,128]{3,2,1,0:T(8,128)(2,1)S(1)} %collective-permute-done.2.refs_4_) | copy-start | bytes 786436
  38.0 14.1 %copy-start.4 = (bf16[2,2,256,128]{3,2,1,0:T(8,128)(2,1)}, bf16[2,2,256,128]{3,2,1,0:T(8,128)(2,1)S(1)}, u32[]{:S(2)}) copy-start(bf16[2,2,256,128]{3,2,1,0:T(8,128)(2,1)S(1)} %collective-permute-done.6.refs_2_) | copy-start | bytes 786436
  39.3 12.7 %copy-start.6 = (bf16[2,2,256,128]{3,2,1,0:T(8,128)(2,1)}, bf16[2,2,256,128]{3,2,1,0:T(8,128)(2,1)S(1)}, u32[]{:S(2)}) copy-start(bf16[2,2,256,128]{3,2,1,0:T(8,128)(2,1)S(1)} %collective-permute-done.7.refs_3_) | copy-start | bytes 786436
  40.5 23.3 %collective-permute-start.8 = (bf16[8,2,256,128]{3,2,1,0:T(8,128)(2,1)}, bf16[8,2,256,128]{3,2,1,0:T(8,128)(2,1)}, u32[]{:S(2)}, u32[]{:S(2)}) collective-permute-start(bf16[8,2,256,128]{3,2,1,0:T(8,128)(2,1)} %pad_maximum_fusion), channel_id=1, source_target_pairs={{0,16},{16,0},{1,17},{17,1},{2,18},{18,2},{3,19},{19,3},{4,20},{20... | collective-permute-start | bytes 3145736 | tf_op jit(solution)/shard_map/ppermute | solution.py:110
  42.4 12.6 %collective-permute-start.1 = (bf16[2,2,256,128]{3,2,1,0:T(8,128)(2,1)S(1)}, bf16[2,2,256,128]{3,2,1,0:T(8,128)(2,1)S(1)}, u32[]{:S(2)}, u32[]{:S(2)}) collective-permute-start(bf16[2,2,256,128]{3,2,1,0:T(8,128)(2,1)S(1)} %collective-permute-done.refs_1_), channel_id=1, source_target_pairs={{0,128},{128,256},{256,384},{384,0},{1,129},{129,257},{257,385},{3... | collective-permute-start | bytes 786440 | tf_op jit(solution)/shard_map/ppermute | solution.py:104
  45.6 10.6 %collective-permute-start.3 = (bf16[2,2,256,128]{3,2,1,0:T(8,128)(2,1)S(1)}, bf16[2,2,256,128]{3,2,1,0:T(8,128)(2,1)S(1)}, u32[]{:S(2)}, u32[]{:S(2)}) collective-permute-start(bf16[2,2,256,128]{3,2,1,0:T(8,128)(2,1)S(1)} %collective-permute-done.2.refs_4_), channel_id=1, source_target_pairs={{0,384},{128,0},{256,128},{384,256},{1,385},{129,1},{257,129},{385... | collective-permute-start | bytes 786440 | tf_op jit(solution)/shard_map/ppermute | solution.py:107
  49.9 13.8 %collective-permute-start.5 = (bf16[4,2,256,128]{3,2,1,0:T(8,128)(2,1)S(1)}, bf16[4,2,256,128]{3,2,1,0:T(8,128)(2,1)}, u32[]{:S(2)}, u32[]{:S(2)}) collective-permute-start(bf16[4,2,256,128]{3,2,1,0:T(8,128)(2,1)S(1)} %all_to_all.24.refs_0_), channel_id=1, source_target_pairs={{0,16},{16,0},{1,17},{17,1},{2,18},{18,2},{3,19},{19,3},{4,20},{20... | collective-permute-start | bytes 1572872 | tf_op jit(solution)/shard_map/ppermute | solution.py:110
  56.2 9.7 %collective-permute-start.4 = (bf16[4,2,256,128]{3,2,1,0:T(8,128)(2,1)S(1)}, bf16[4,2,256,128]{3,2,1,0:T(8,128)(2,1)}, u32[]{:S(2)}, u32[]{:S(2)}) collective-permute-start(bf16[4,2,256,128]{3,2,1,0:T(8,128)(2,1)S(1)} %constant_dynamic-update-slice_fusion.refs_2_), channel_id=1, source_target_pairs={{0,16},{16,0},{1,17},{17,1},{2,18},{18,2},{3,19},{19,3},{4,20},{20... | collective-permute-start | bytes 1572872 | tf_op jit(solution)/shard_map/ppermute | solution.py:110
  58.2 1.6 %copy-start.1 = (bf16[1,128,8192]{2,1,0:T(8,128)(2,1)S(1)}, bf16[1,128,8192]{2,1,0:T(8,128)(2,1)}, u32[]{:S(2)}) copy-start(bf16[1,128,8192]{2,1,0:T(8,128)(2,1)} %param.10) | copy-start | bytes 6291460
  59.8 0.9 copy-start.3
  60.7 0.9 copy-start.5
  61.7 0.9 copy-start.7
  67.4 26.8 %copy-start.8 = (bf16[1,16,16384]{2,1,0:T(8,128)(2,1)S(1)}, bf16[1,16,16384]{2,1,0:T(8,128)(2,1)}, u32[]{:S(2)}) copy-start(bf16[1,16,16384]{2,1,0:T(8,128)(2,1)} %param.17) | copy-start | bytes 1572868
  67.5 26.8 %copy-start.9 = (f32[1,128,128]{2,1,0:T(8,128)S(1)}, f32[1,128,128]{2,1,0:T(8,128)}, u32[]{:S(2)}) copy-start(f32[1,128,128]{2,1,0:T(8,128)} %param.13) | copy-start | bytes 196612
  67.5 26.8 %copy-start.10 = (f32[1,128,128]{2,1,0:T(8,128)S(1)}, f32[1,128,128]{2,1,0:T(8,128)}, u32[]{:S(2)}) copy-start(f32[1,128,128]{2,1,0:T(8,128)} %param.14) | copy-start | bytes 196612
  67.5 26.8 %copy-start.11 = (f32[1,128]{1,0:T(1,128)S(1)}, f32[1,128]{1,0:T(1,128)}, u32[]{:S(2)}) copy-start(f32[1,128]{1,0:T(1,128)} %eig_a.1) | copy-start | bytes 1540
  67.5 26.8 %copy-start.12 = (f32[1,128]{1,0:T(1,128)S(1)}, f32[1,128]{1,0:T(1,128)}, u32[]{:S(2)}) copy-start(f32[1,128]{1,0:T(1,128)} %eig_g.1) | copy-start | bytes 1540
  67.5 3.4 %collective-permute-start.9 = (f32[128,128]{1,0:T(8,128)S(1)}, f32[128,128]{1,0:T(8,128)S(1)}, u32[]{:S(2)}, u32[]{:S(2)}) collective-permute-start(f32[128,128]{1,0:T(8,128)S(1)} %shard_map.93), channel_id=1, source_target_pairs={{0,16},{16,0},{1,17},{17,1},{2,18},{18,2},{3,19},{19,3},{4,20},{20... | collective-permute-start | bytes 196616 | tf_op jit(solution)/shard_map/ppermute | solution.py:110

commit v3 on v1

v3 whole, which is shorter than its diff:
```python
import functools

import jax
import jax.numpy as jnp
from jax import lax
from jax.experimental import pallas as pl
from jax.experimental.pallas import tpu as pltpu
from jax.sharding import Mesh, PartitionSpec as P

F32 = jnp.float32
BF16 = jnp.bfloat16
HIGHEST = lax.Precision.HIGHEST

CTX = ("y", "zlo", "core")
LAYER = ("zhi", "x")
VMEM = pl.BlockSpec(memory_space=pltpu.VMEM)
SMEM = pl.BlockSpec(memory_space=pltpu.SMEM)


def deal(core_ref, acts_ref, grads_ref, keep_ref, send_ref, sems):
    def copies(keep_from, send_from):
        one = pltpu.make_async_copy(send_from, send_ref, sems.at[0])
        two = pltpu.make_async_copy(keep_from, keep_ref, sems.at[1])
        one.start()
        two.start()
        one.wait()
        two.wait()

    @pl.when(core_ref[0] == 0)
    def _():
        copies(acts_ref, grads_ref)

    @pl.when(core_ref[0] != 0)
    def _():
        copies(grads_ref, acts_ref)


def project(keep_ref, got_ref, rows_ref, out):
    depth = rows_ref.shape[1]
    n_tok = keep_ref.shape[0]
    mine = jnp.zeros((n_tok, rows_ref.shape[2]), F32)
    other = mine
    for b in range(rows_ref.shape[0]):
        cols = pl.ds(b * depth, depth)
        mine = mine + jnp.dot(keep_ref[:, cols], rows_ref[b], preferred_element_type=F32)
        other = other + jnp.dot(got_ref[:, cols], rows_ref[b], preferred_element_type=F32)
    out[0] = mine.astype(BF16)
    out[1] = other.astype(BF16)


def outer(tokens, core_ref, mine_ref, got_ref, out):
    even = core_ref[0] == 0
    total = jnp.zeros(out.shape[1:], F32)
    for k in range(2):
        mine, got = mine_ref[k].astype(F32), got_ref[1 - k].astype(F32)
        proj_g = jnp.where(even, got, mine).astype(BF16)
        proj_a = jnp.where(even, mine, got).astype(BF16)
        total = total + lax.dot_general(
            proj_g, proj_a, (((0,), (0,)), ((), ())), preferred_element_type=F32
        )
    total = total / tokens
    for k in range(out.shape[0]):
        out[k] = total


def score(parts_ref, basis_a, basis_g, eig_a, eig_g, train_ref, out):
    grad = parts_ref[0]
    for k in range(1, parts_ref.shape[0]):
        grad = grad + parts_ref[k]
    rot_a, rot_g = basis_a[...], basis_g[...]
    dot = functools.partial(
        lax.dot_general, precision=HIGHEST, preferred_element_type=F32
    )
    nn, tn, nt = (((1,), (0,)), ((), ())), (((0,), (0,)), ((), ())), (((1,), (1,)), ((), ()))
    turned = dot(dot(rot_g, grad, tn), rot_a, nn)
    rank = turned.shape[0]
    eye = (
        lax.broadcasted_iota(jnp.int32, (rank, rank), 0)
        == lax.broadcasted_iota(jnp.int32, (rank, rank), 1)
    )
    row_eig = jnp.sum(jnp.where(eye, jnp.broadcast_to(eig_g[...], (rank, rank)), 0.0), 1, keepdims=True)
    whitened = turned / (row_eig * eig_a[...])
    precond = dot(dot(rot_g, whitened, nn), rot_a, nt).astype(BF16).astype(F32)
    total = jnp.zeros((train_ref.shape[0], rank), F32)
    for i in range(rank):
        total = total + train_ref[:, i * rank:(i + 1) * rank].astype(F32) * precond[i:i + 1, :]
    out[...] = dot(jnp.ones((out.shape[0], rank), F32), total, nt)


def to_all(x, axis):
    size = lax.axis_size(axis)
    return lax.all_to_all(jnp.broadcast_to(x, (size,) + x.shape), axis, 0, 0)


def body(acts, grads_out, proj_in, proj_out, basis_a, basis_g, eig_a, eig_g, train_grads):
    tokens = acts.shape[1] * lax.axis_size(CTX)
    n_layer, n_y = lax.axis_size(LAYER), lax.axis_size("y")
    depth, rank = proj_in.shape[1:]
    core = lax.axis_index("core").astype(jnp.int32).reshape(1)
    local = acts[0]
    n_tok = local.shape[0]
    params = pltpu.CompilerParams(vmem_limit_bytes=20 << 20)

    def swap(x):
        return lax.ppermute(x, "core", [(0, 1), (1, 0)])

    piece = jax.ShapeDtypeStruct(local.shape, BF16)
    keep, send = pl.pallas_call(
        deal,
        out_shape=(piece, piece),
        in_specs=[SMEM, pl.BlockSpec(memory_space=pl.ANY), pl.BlockSpec(memory_space=pl.ANY)],
        out_specs=(VMEM, VMEM),
        scratch_shapes=[pltpu.SemaphoreType.DMA((2,))],
        compiler_params=params,
        name="deal",
    )(core, local, grads_out[0])
    got = swap(send)

    both = jnp.concatenate([proj_in, proj_out], 0)
    both = jnp.broadcast_to(both, (lax.axis_size("zlo"),) + both.shape)
    line = lax.all_to_all(both.reshape(-1, depth, rank), ("zlo", "core"), 0, 0, tiled=True)
    rows = to_all(line, "y").reshape(-1, depth, rank)

    mine = pl.pallas_call(
        project,
        out_shape=jax.ShapeDtypeStruct((2, n_tok, rank), BF16),
        in_specs=[VMEM] * 3,
        out_specs=VMEM,
        compiler_params=params,
        name="project",
    )(keep, got, rows)
    grad = pl.pallas_call(
        functools.partial(outer, float(tokens)),
        out_shape=jax.ShapeDtypeStruct((n_y, rank, rank), F32),
        in_specs=[SMEM, VMEM, VMEM],
        out_specs=VMEM,
        compiler_params=params,
        name="outer",
    )(core, mine, swap(mine))

    grad = jnp.sum(lax.all_to_all(grad, "y", 0, 0), 0)
    parts = to_all(grad, "zlo")
    sent = pl.pallas_call(
        score,
        out_shape=jax.ShapeDtypeStruct((n_layer, train_grads.shape[1]), F32),
        in_specs=[VMEM] * 6,
        out_specs=VMEM,
        compiler_params=params,
        name="score",
    )(parts, basis_a[0], basis_g[0], eig_a, eig_g, train_grads[0])
    return jnp.sum(lax.all_to_all(sent, LAYER, 0, 0), 0)


def solution(mesh):
    devices = mesh.devices.reshape(4, 4, 2, 4, 4)
    fine = Mesh(devices, CTX + LAYER)
    return jax.shard_map(
        body,
        mesh=fine,
        in_specs=(
            P(LAYER, CTX, None),
            P(LAYER, CTX, None),
            P(LAYER, CTX, None),
            P(LAYER, CTX, None),
            P(LAYER, None, None),
            P(LAYER, None, None),
            P(LAYER, None),
            P(LAYER, None),
            P(LAYER, CTX, None),
        ),
        out_specs=P(CTX),
        check_vma=False,
    )
```

time: 121 us -> 116 us (0.959)
  blocking collectives: 100 us -> 49.7 us
  waiting for transfers between devices: 1.12 us -> 34 us
  starting transfers between devices: 4.28 us -> 14.8 us
  local copies, waits for them, and re-layouts: 0.57 us -> 8.9 us
  Pallas kernels: 11.7 us -> 5.9 us
    all_to_all x4 -> x1, blocking collectives: 71.3 us -> 11.2 us  [to_all(): return lax.all_to_all(jnp.broadcast_to(x, (size,) + x.shape), axis, 0, 0)]
    all_to_all x0 -> x2, waiting for transfers between devices: none -> 32.8 us  [the longest x1 26 us: to_all(): return lax.all_to_all(jnp.broadcast_to(x, (size,) + x.shape), axis, 0, 0)]
    all_to_all x0 -> x2, starting transfers between devices: none -> 10.4 us  [the longest x1 5.9 us: body(): lax.all_to_all(both.reshape(-1, depth, rank), ('zlo', 'core'), 0, 0, tile...]
    all_to_all x0 -> x1, blocking collectives: none -> 9.65 us  [body(): grad = jnp.sum(lax.all_to_all(grad, 'y', 0, 0), 0)]
    unnamed x2 -> x18, local copies, waits for them, and re-layouts: 0.01 us -> 6.13 us
    pallas_call x2 -> x3, Pallas kernels: 8.6 us -> 4.66 us  [the longest x1 2.83 us: body(): pl.pallas_call(project, out_shape=jax.ShapeDtypeStruct((2, n_tok, rank),...]
    pallas_call x1, Pallas kernels: 3.06 us -> 1.24 us  [body(): pl.pallas_call(score, out_shape=jax.ShapeDtypeStruct((n_layer, train_grad...]
    broadcast_in_dim x4 -> x2, local copies, waits for them, and re-layouts: 0.57 us -> 1.88 us  [to_all(): return lax.all_to_all(jnp.broadcast_to(x, (size,) + x.shape), axis, 0, 0)]
  transfers between devices with their start and end apart: 2 -> 4, of which waited for: 1 -> 3; matrix products, arithmetic and copies ran while one was open for 0% -> 2% of each run, Pallas kernels for 4% -> 1%
where the time goes in v3:
time: 116 us; the launch traced here: 115 us
  blocking collectives  49.7 us (43%)
  waiting for transfers between devices  34 us (29%)
  starting transfers between devices  14.8 us (13%)
  local copies, waits for them, and re-layouts  8.9 us (8%)
  Pallas kernels  5.9 us (5%)
  other arithmetic  1.44 us (1%)
    all_to_all x1, blocking collectives, body(): return jnp.sum(lax.all_to_all(sent, LAYER, 0, 0), 0)  28.8 us
    all_to_all x1, waiting for transfers between devices, to_all(): return lax.all_to_all(jnp.broadcast_to(x, (size,) + x.shape), axis, 0, 0)  26 us
    all_to_all x1, blocking collectives, to_all(): return lax.all_to_all(jnp.broadcast_to(x, (size,) + x.shape), axis, 0, 0)  11.2 us
    all_to_all x1, blocking collectives, body(): grad = jnp.sum(lax.all_to_all(grad, 'y', 0, 0), 0)  9.65 us
    all_to_all x1, waiting for transfers between devices, body(): lax.all_to_all(both.reshape(-1, depth, rank), ('zlo', 'core'), 0, 0, tile...  6.76 us
    unnamed x18, local copies, waits for them, and re-layouts  6.13 us
    all_to_all x1, starting transfers between devices, body(): lax.all_to_all(both.reshape(-1, depth, rank), ('zlo', 'core'), 0, 0, tile...  5.9 us
    all_to_all x1, starting transfers between devices, to_all(): return lax.all_to_all(jnp.broadcast_to(x, (size,) + x.shape), axis, 0, 0)  4.46 us
  transfers between devices with their start and end apart: 4, of which 3 were waited for; matrix products, arithmetic and copies ran while one was open for 2% of the time, Pallas kernels for 1%

profile of v3, /device:TPU:2, one launch (start us, length us, event | category | flops | bytes accessed | tf_op | source)
XLA Modules:
  0.0 114.9 jit_solution(8524529270349845642)
XLA Ops:
  0.0 0.9 pad_maximum_fusion
  0.9 0.9 broadcast_in_dim.9
  1.8 5.9 %all-to-all-start = ((bf16[8,256,128]{2,1,0:T(8,128)(2,1)}), bf16[8,256,128]{2,1,0:T(8,128)(2,1)S(1)}, u32[]{:S(2)}, u32[]{:S(2)}) async-start(bf16[8,256,128]{2,1,0:T(8,128)(2,1)} %bitcast.3), calls=%async_computation | async-start | bytes 1048576 | tf_op jit(solution)/shard_map/all_to_all | solution.py:121
  7.7 0.0 copy-start.2
  7.7 1.6 %copy-done.2 = bf16[1,128,8192]{2,1,0:T(8,128)(2,1)S(1)} copy-done((bf16[1,128,8192]{2,1,0:T(8,128)(2,1)S(1)}, bf16[1,128,8192]{2,1,0:T(8,128)(2,1)}, u32[]{:S(2)}) %copy-start.2) | copy-done | bytes 2097176
  9.3 0.0 copy-start.3
  9.3 1.6 %copy-done.3 = bf16[1,128,8192]{2,1,0:T(8,128)(2,1)S(1)} copy-done((bf16[1,128,8192]{2,1,0:T(8,128)(2,1)S(1)}, bf16[1,128,8192]{2,1,0:T(8,128)(2,1)}, u32[]{:S(2)}) %copy-start.3) | copy-done | bytes 2097176
  10.9 1.6 %deal.1 = (bf16[128,8192]{1,0:T(8,128)(2,1)S(1)}, bf16[128,8192]{1,0:T(8,128)(2,1)}) custom-call(s32[1]{0:T(128)} %bitcast.core_ref, bf16[128,8192]{1,0:T(8,128)(2,1)S(1)} %bitcast.12, bf16[128,8192]{1,0:T(8,128)(2,1)S(1)} %bitcast.13), custom_call_target="tpu_custom_call" | custom-call | tf_op jit(solution)/shard_map/deal/pallas_call | solution.py:108
  12.5 0.0 copy-start
  12.5 1.3 %copy-done = bf16[128,8192]{1,0:T(8,128)(2,1)} copy-done((bf16[128,8192]{1,0:T(8,128)(2,1)}, bf16[128,8192]{1,0:T(8,128)(2,1)S(1)}, u32[]{:S(2)}) %copy-start) | copy-done | bytes 2097176
  13.8 2.4 %collective-permute-start = (bf16[128,8192]{1,0:T(8,128)(2,1)}, bf16[128,8192]{1,0:T(8,128)(2,1)}, u32[]{:S(2)}, u32[]{:S(2)}) collective-permute-start(bf16[128,8192]{1,0:T(8,128)(2,1)} %get-tuple-element.8), channel_id=1, source_target_pairs={{0,16},{16,0},{1,17},{17,1},{2,18},{18,2},{3,19},{19,3},{4,20},{20... | collective-permute-start | bytes 6291464 | tf_op jit(solution)/shard_map/ppermute | solution.py:105
  16.2 6.8 %all-to-all-done = bf16[8,256,128]{2,1,0:T(8,128)(2,1)S(1)} async-done(((bf16[8,256,128]{2,1,0:T(8,128)(2,1)}), bf16[8,256,128]{2,1,0:T(8,128)(2,1)S(1)}, u32[]{:S(2)}, u32[]{:S(2)}) %all-to-all-start) | async-done | bytes 524320 | tf_op jit(solution)/shard_map/all_to_all | solution.py:121
  23.0 1.9 %broadcast_in_dim.10 = bf16[4,8,256,128]{3,2,1,0:T(8,128)(2,1)} broadcast(bf16[8,256,128]{2,1,0:T(8,128)(2,1)S(1)} %all-to-all-done), dimensions={1,2,3} | broadcast | bytes 2621440 | tf_op jit(solution)/shard_map/broadcast_in_dim | solution.py:92
  24.9 4.5 %all-to-all-start.1 = ((bf16[4,8,256,128]{3,2,1,0:T(8,128)(2,1)}), bf16[4,8,256,128]{3,2,1,0:T(8,128)(2,1)S(1)}, u32[]{:S(2)}, u32[]{:S(2)}) async-start(bf16[4,8,256,128]{3,2,1,0:T(8,128)(2,1)} %broadcast_in_dim.10), calls=%async_computation.1 | async-start | bytes 4194304 | tf_op jit(solution)/shard_map/all_to_all | solution.py:92
  29.3 0.0 collective-permute-done.got_ref
  29.3 26.0 %all-to-all-done.1 = bf16[4,8,256,128]{3,2,1,0:T(8,128)(2,1)S(1)} async-done(((bf16[4,8,256,128]{3,2,1,0:T(8,128)(2,1)}), bf16[4,8,256,128]{3,2,1,0:T(8,128)(2,1)S(1)}, u32[]{:S(2)}, u32[]{:S(2)}) %all-to-all-start.1) | async-done | bytes 2097184 | tf_op jit(solution)/shard_map/all_to_all | solution.py:92
  55.4 0.0 copy-start.1
  55.4 1.6 %copy-done.1 = bf16[128,8192]{1,0:T(8,128)(2,1)S(1)} copy-done((bf16[128,8192]{1,0:T(8,128)(2,1)S(1)}, bf16[128,8192]{1,0:T(8,128)(2,1)}, u32[]{:S(2)}) %copy-start.1) | copy-done | bytes 2097176
  57.0 2.8 %project.1.mine_ref = bf16[2,128,128]{2,1,0:T(8,128)(2,1)S(1)} custom-call(bf16[128,8192]{1,0:T(8,128)(2,1)S(1)} %copy-done.1, bf16[128,8192]{1,0:T(8,128)(2,1)} %collective-permute-done.got_ref, bf16[32,256,128]{2,1,0:T(8,128)(2,1)S(1)} %bitcast.11), custom_call_target="tpu_custom_call" | custom-call | tf_op jit(solution)/shard_map/project/pallas_call | solution.py:124
  59.8 0.0 copy-start.4
  59.8 0.0 copy-start.5
  59.8 0.0 copy-start.6
  59.8 0.0 copy-start.7
  59.8 0.0 copy-start.8
  59.9 2.1 %collective-permute-start.1 = (bf16[2,128,128]{2,1,0:T(8,128)(2,1)S(1)}, bf16[2,128,128]{2,1,0:T(8,128)(2,1)S(1)}, u32[]{:S(2)}, u32[]{:S(2)}) collective-permute-start(bf16[2,128,128]{2,1,0:T(8,128)(2,1)S(1)} %project.1.mine_ref), channel_id=1, source_target_pairs={{0,16},{16,0},{1,17},{17,1},{2,18},{18,2},{3,19},{19,3},{4,20},{20... | collective-permute-start | bytes 196616 | tf_op jit(solution)/shard_map/ppermute | solution.py:105
  61.9 1.2 %collective-permute-done.1.got_ref = bf16[2,128,128]{2,1,0:T(8,128)(2,1)S(1)} collective-permute-done((bf16[2,128,128]{2,1,0:T(8,128)(2,1)S(1)}, bf16[2,128,128]{2,1,0:T(8,128)(2,1)S(1)}, u32[]{:S(2)}, u32[]{:S(2)}) %collective-permute-start.1) | collective-permute-done | bytes 65568 | tf_op jit(solution)/shard_map/ppermute | solution.py:105
  63.1 0.2 outer.1
  63.3 9.7 %all_to_all.29 = f32[4,128,128]{2,1,0:T(8,128)S(1)} all-to-all(f32[4,128,128]{2,1,0:T(8,128)S(1)} %outer.1), channel_id=1, replica_groups=mesh['y'=4,'zlo'=4,'core'=2,'zhi'=4,'x'=4] {'y'}, dimensions={0} | all-to-all | bytes 524288 | tf_op jit(solution)/shard_map/all_to_all | solution.py:141
  73.0 11.2 %all_to_all.30.parts_ref = f32[4,128,128]{2,1,0:T(8,128)S(1)} all-to-all(f32[4,128,128]{2,1,0:T(8,128)S(1)} %broadcast_in_dim.11), channel_id=1, replica_groups=mesh['y'=4,'zlo'=4,'core'=2,'zhi'=4,'x'=4] {'zlo'}, dimensions={0} | all-to-all | bytes 524288 | tf_op jit(solution)/shard_map/all_to_all | solution.py:92
  84.3 0.0 copy-done.4
  84.3 0.0 copy-done.5
  84.3 0.0 copy-done.6
  84.3 0.0 copy-done.7
  84.3 0.0 copy-done.8
  84.3 1.2 %score.1 = f32[16,16]{1,0:T(8,128)S(1)} custom-call(f32[4,128,128]{2,1,0:T(8,128)S(1)} %all_to_all.30.parts_ref, f32[128,128]{1,0:T(8,128)S(1)} %bitcast.15, f32[128,128]{1,0:T(8,128)S(1)} %bitcast.16, f32[1,128]{1,0:T(1,128)S(1)} %copy-done.7, f32[1,128]{1,0:T(1,128)S(1)} %copy-done.8, bf16[16,16384]{1,0:T(8,128)(2,1)S(1)} %bitcast.14), custom_call_target="tpu_custom_call" | custom-call | tf_op jit(solution)/shard_map/score/pallas_call | solution.py:143
  85.5 28.8 %all_to_all.31 = f32[16,1,16]{2,1,0:T(1,128)S(1)} all-to-all(f32[16,1,16]{2,1,0:T(1,128)S(1)} %bitcast.17), channel_id=1, replica_groups=mesh['y'=4,'zlo'=4,'core'=2,'zhi'=4,'x'=4] {'zhi','x'}, dimensions={0} | all-to-all | bytes 2048 | tf_op jit(solution)/shard_map/all_to_all | solution.py:151
  114.4 0.5 reduce_sum.19
  (2 shorter events, 0.0 us)
Async XLA Ops:
  1.8 21.2 %all-to-all-start = ((bf16[8,256,128]{2,1,0:T(8,128)(2,1)}), bf16[8,256,128]{2,1,0:T(8,128)(2,1)S(1)}, u32[]{:S(2)}, u32[]{:S(2)}) async-start(bf16[8,256,128]{2,1,0:T(8,128)(2,1)} %bitcast.3), calls=%async_computation | async-start | bytes 1048576 | tf_op jit(solution)/shard_map/all_to_all | solution.py:121
  7.7 1.6 %copy-start.2 = (bf16[1,128,8192]{2,1,0:T(8,128)(2,1)S(1)}, bf16[1,128,8192]{2,1,0:T(8,128)(2,1)}, u32[]{:S(2)}) copy-start(bf16[1,128,8192]{2,1,0:T(8,128)(2,1)} %param.9) | copy-start | bytes 6291460
  9.3 1.6 %copy-start.3 = (bf16[1,128,8192]{2,1,0:T(8,128)(2,1)S(1)}, bf16[1,128,8192]{2,1,0:T(8,128)(2,1)}, u32[]{:S(2)}) copy-start(bf16[1,128,8192]{2,1,0:T(8,128)(2,1)} %param.10) | copy-start | bytes 6291460
  12.5 1.3 %copy-start = (bf16[128,8192]{1,0:T(8,128)(2,1)}, bf16[128,8192]{1,0:T(8,128)(2,1)S(1)}, u32[]{:S(2)}) copy-start(bf16[128,8192]{1,0:T(8,128)(2,1)S(1)} %get-tuple-element.7.keep_ref) | copy-start | bytes 6291460
  13.8 15.5 %collective-permute-start = (bf16[128,8192]{1,0:T(8,128)(2,1)}, bf16[128,8192]{1,0:T(8,128)(2,1)}, u32[]{:S(2)}, u32[]{:S(2)}) collective-permute-start(bf16[128,8192]{1,0:T(8,128)(2,1)} %get-tuple-element.8), channel_id=1, source_target_pairs={{0,16},{16,0},{1,17},{17,1},{2,18},{18,2},{3,19},{19,3},{4,20},{20... | collective-permute-start | bytes 6291464 | tf_op jit(solution)/shard_map/ppermute | solution.py:105
  24.9 30.5 %all-to-all-start.1 = ((bf16[4,8,256,128]{3,2,1,0:T(8,128)(2,1)}), bf16[4,8,256,128]{3,2,1,0:T(8,128)(2,1)S(1)}, u32[]{:S(2)}, u32[]{:S(2)}) async-start(bf16[4,8,256,128]{3,2,1,0:T(8,128)(2,1)} %broadcast_in_dim.10), calls=%async_computation.1 | async-start | bytes 4194304 | tf_op jit(solution)/shard_map/all_to_all | solution.py:92
  55.4 1.6 %copy-start.1 = (bf16[128,8192]{1,0:T(8,128)(2,1)S(1)}, bf16[128,8192]{1,0:T(8,128)(2,1)}, u32[]{:S(2)}) copy-start(bf16[128,8192]{1,0:T(8,128)(2,1)} %copy-done) | copy-start | bytes 6291460
  59.8 24.5 %copy-start.4 = (bf16[1,16,16384]{2,1,0:T(8,128)(2,1)S(1)}, bf16[1,16,16384]{2,1,0:T(8,128)(2,1)}, u32[]{:S(2)}) copy-start(bf16[1,16,16384]{2,1,0:T(8,128)(2,1)} %param.17) | copy-start | bytes 1572868
  59.8 24.5 %copy-start.5 = (f32[1,128,128]{2,1,0:T(8,128)S(1)}, f32[1,128,128]{2,1,0:T(8,128)}, u32[]{:S(2)}) copy-start(f32[1,128,128]{2,1,0:T(8,128)} %param.13) | copy-start | bytes 196612
  59.8 24.4 %copy-start.6 = (f32[1,128,128]{2,1,0:T(8,128)S(1)}, f32[1,128,128]{2,1,0:T(8,128)}, u32[]{:S(2)}) copy-start(f32[1,128,128]{2,1,0:T(8,128)} %param.14) | copy-start | bytes 196612
  59.8 24.4 %copy-start.7 = (f32[1,128]{1,0:T(1,128)S(1)}, f32[1,128]{1,0:T(1,128)}, u32[]{:S(2)}) copy-start(f32[1,128]{1,0:T(1,128)} %eig_a.1) | copy-start | bytes 1540
  59.8 24.4 %copy-start.8 = (f32[1,128]{1,0:T(1,128)S(1)}, f32[1,128]{1,0:T(1,128)}, u32[]{:S(2)}) copy-start(f32[1,128]{1,0:T(1,128)} %eig_g.1) | copy-start | bytes 1540
  59.9 3.3 %collective-permute-start.1 = (bf16[2,128,128]{2,1,0:T(8,128)(2,1)S(1)}, bf16[2,128,128]{2,1,0:T(8,128)(2,1)S(1)}, u32[]{:S(2)}, u32[]{:S(2)}) collective-permute-start(bf16[2,128,128]{2,1,0:T(8,128)(2,1)S(1)} %project.1.mine_ref), channel_id=1, source_target_pairs={{0,16},{16,0},{1,17},{17,1},{2,18},{18,2},{3,19},{19,3},{4,20},{20... | collective-permute-start | bytes 196616 | tf_op jit(solution)/shard_map/ppermute | solution.py:105

commit v4 on v1

v4 whole, which is shorter than its diff:
```python
import functools

import jax
import jax.numpy as jnp
from jax import lax
from jax.experimental import pallas as pl
from jax.experimental.pallas import tpu as pltpu
from jax.sharding import Mesh, PartitionSpec as P


F32 = jnp.float32
BF16 = jnp.bfloat16
HIGHEST = lax.Precision.HIGHEST

CTX = ("y", "zlo", "core")
LAYER = ("zhi", "x")
VMEM = pl.BlockSpec(memory_space=pltpu.VMEM)
SMEM = pl.BlockSpec(memory_space=pltpu.SMEM)


def pack(in_ref, out_ref, out):
    for k in range(out.shape[0]):
        out[k, 0] = in_ref[...]
        out[k, 1] = out_ref[...]


def deal(here_ref, acts_ref, grads_ref, send_ref, sem):
    @pl.when(here_ref[1] == 0)
    def _():
        copy = pltpu.make_async_copy(grads_ref, send_ref, sem)
        copy.start()
        copy.wait()

    @pl.when(here_ref[1] != 0)
    def _():
        copy = pltpu.make_async_copy(acts_ref, send_ref, sem)
        copy.start()
        copy.wait()


def products(pieces, here_ref, acts_ref, grads_ref, got_ref, row_refs, mine, other):
    even = here_ref[1] == 0
    for (step, first), rows_ref in zip(pieces, row_refs):
        count, depth, _ = rows_ref.shape
        line = lax.rem(here_ref[0] + step, here_ref[2]) * here_ref[3]
        for k in range(count):
            cols = pl.ds(pl.multiple_of((line + (first + k)) * depth, depth), depth)
            keep = jnp.where(even, acts_ref[:, cols], grads_ref[:, cols])
            mine = mine + jnp.dot(keep, rows_ref[k], preferred_element_type=F32)
            other = other + jnp.dot(got_ref[:, cols], rows_ref[k], preferred_element_type=F32)
    return mine, other


def begin(pieces, here_ref, acts_ref, grads_ref, got_ref, *refs):
    rows, out = refs[:-1], refs[-1]
    zero = jnp.zeros(out.shape[1:], F32)
    out[0], out[1] = products(
        pieces, here_ref, acts_ref, grads_ref, got_ref, rows, zero, zero
    )


def finish(pieces, here_ref, acts_ref, grads_ref, got_ref, *refs):
    rows, (acc, out) = refs[:-2], refs[-2:]
    mine, other = products(
        pieces, here_ref, acts_ref, grads_ref, got_ref, rows, acc[0], acc[1]
    )
    out[0], out[1] = mine.astype(out.dtype), other.astype(out.dtype)


def outer(tokens, here_ref, mine_ref, got_ref, out):
    even = here_ref[1] == 0
    total = jnp.zeros(out.shape[1:], F32)
    for k in range(2):
        mine, got = mine_ref[k].astype(F32), got_ref[1 - k].astype(F32)
        proj_g = jnp.where(even, got, mine).astype(BF16)
        proj_a = jnp.where(even, mine, got).astype(BF16)
        total = total + lax.dot_general(
            proj_g, proj_a, (((0,), (0,)), ((), ())), preferred_element_type=F32
        )
    total = (total / tokens).astype(out.dtype)
    for k in range(out.shape[0]):
        out[k] = total


def add_up(parts_ref, out):
    total = parts_ref[0].astype(F32)
    for k in range(1, parts_ref.shape[0]):
        total = total + parts_ref[k].astype(F32)
    total = total.astype(out.dtype)
    for k in range(out.shape[0]):
        out[k] = total


def score(parts_ref, basis_a, basis_g, eig_a, eig_g, train_ref, out):
    grad = parts_ref[0].astype(F32)
    for k in range(1, parts_ref.shape[0]):
        grad = grad + parts_ref[k].astype(F32)
    rot_a, rot_g = basis_a[...], basis_g[...]
    dot = functools.partial(
        lax.dot_general, precision=HIGHEST, preferred_element_type=F32
    )
    nn, tn, nt = (((1,), (0,)), ((), ())), (((0,), (0,)), ((), ())), (((1,), (1,)), ((), ()))
    turned = dot(dot(rot_g, grad, tn), rot_a, nn)
    rank = turned.shape[0]
    eye = (
        lax.broadcasted_iota(jnp.int32, (rank, rank), 0)
        == lax.broadcasted_iota(jnp.int32, (rank, rank), 1)
    )
    row_eig = jnp.sum(jnp.where(eye, jnp.broadcast_to(eig_g[...], (rank, rank)), 0.0), 1, keepdims=True)
    whitened = turned / (row_eig * eig_a[...])
    precond = dot(dot(rot_g, whitened, nn), rot_a, nt).astype(BF16).astype(F32)
    total = jnp.zeros((train_ref.shape[0], rank), F32)
    for i in range(rank):
        total = total + train_ref[:, i * rank:(i + 1) * rank].astype(F32) * precond[i:i + 1, :]
    out[...] = dot(jnp.ones((out.shape[0], rank), F32), total, nt)


def body(acts, grads_out, proj_in, proj_out, basis_a, basis_g, eig_a, eig_g, train_grads):
    tokens = acts.shape[1] * lax.axis_size(CTX)
    n_layer = lax.axis_size(LAYER)
    n_y, n_z = lax.axis_size("y"), lax.axis_size("zlo")
    depth, rank = proj_in.shape[1:]
    line_blocks = 2 * n_z
    half = n_z
    local, local_g = acts[0], grads_out[0]
    n_tok = local.shape[0]
    hbm = pl.BlockSpec(memory_space=pltpu.HBM)
    here = jnp.stack(
        [lax.axis_index("y"), lax.axis_index("core"), jnp.int32(n_y), jnp.int32(line_blocks)]
    ).astype(jnp.int32)

    def call(kernel, shape, in_specs, *args, **more):
        return pl.pallas_call(
            kernel,
            out_shape=shape,
            in_specs=in_specs,
            out_specs=VMEM,
            compiler_params=pltpu.CompilerParams(vmem_limit_bytes=20 << 20),
            **more,
        )(*args)

    def shape(*dims, dtype=BF16):
        return jax.ShapeDtypeStruct(dims, dtype)

    def all_to_all(x, axis):
        return lax.all_to_all(x, axis, 0, 0, tiled=True)

    def permute(x, axis, step):
        size = lax.axis_size(axis)
        return lax.ppermute(x, axis, [(i, (i + step) % size) for i in range(size)])

    both = call(pack, shape(n_z, 2, depth, rank), [VMEM] * 2, proj_in[0], proj_out[0])
    line = all_to_all(both.reshape(line_blocks, depth, rank), ("zlo", "core"))
    send = call(
        deal, shape(*local.shape), [SMEM, hbm, hbm], here, local, local_g,
        scratch_shapes=[pltpu.SemaphoreType.DMA],
    )
    got = permute(send, "core", 1)

    low, high = line[:half], line[half:]
    below_low = permute(low, "y", 1)
    above_high = permute(high, "y", -1)
    below_high = permute(high, "y", 1)
    above_low = permute(low, "y", -1)
    far_low = permute(below_low, "y", 1)
    far_high = permute(above_high, "y", -1)

    below, above, far = n_y - 1, 1, n_y // 2
    near = {(0, 0): line, (below, 0): below_low, (below, half): below_high,
            (above, 0): above_low, (above, half): above_high}
    cost = pl.CostEstimate(
        flops=4 * n_tok * rank * local.shape[1] * 3 // 4, bytes_accessed=6 << 20, transcendentals=0
    )
    acc = call(
        functools.partial(begin, tuple(near)), shape(2, n_tok, rank, dtype=F32),
        [SMEM] + [VMEM] * (3 + len(near)),
        here, local, local_g, got, *near.values(), cost_estimate=cost,
    )
    mine = call(
        functools.partial(finish, ((far, 0), (far, half))), shape(2, n_tok, rank),
        [SMEM] + [VMEM] * 6,
        here, local, local_g, got, far_low, far_high, acc,
    )
    grad = call(
        functools.partial(outer, float(tokens)), shape(n_y, rank, rank),
        [SMEM, VMEM, VMEM], here, mine, permute(mine, "core", 1),
    )
    grad = call(add_up, shape(n_z, rank, rank), [VMEM], all_to_all(grad, "y"))
    sent = call(
        score, shape(n_layer, train_grads.shape[1], dtype=F32), [VMEM] * 6,
        all_to_all(grad, "zlo"), basis_a[0], basis_g[0], eig_a, eig_g, train_grads[0],
    )
    return jnp.sum(lax.all_to_all(sent, LAYER, 0, 0), 0)


def solution(mesh):
    devices = mesh.devices.reshape(4, 4, 2, 4, 4)
    fine = Mesh(devices, CTX + LAYER)
    return jax.shard_map(
        body,
        mesh=fine,
        in_specs=(
            P(LAYER, CTX, None),
            P(LAYER, CTX, None),
            P(LAYER, CTX, None),
            P(LAYER, CTX, None),
            P(LAYER, None, None),
            P(LAYER, None, None),
            P(LAYER, None),
            P(LAYER, None),
            P(LAYER, CTX, None),
        ),
        out_specs=P(CTX),
        check_vma=False,
    )
```

time: 121 us -> 106 us (0.88)
  the two profiles are of different devices: /device:TPU:2 before, /device:TPU:32 now
where the time goes in v4:
time: 106 us; the launch traced here: 105 us
  blocking collectives  48.4 us (46%)
  starting transfers between devices  34 us (32%)
  Pallas kernels  9.59 us (9%)
  local copies, waits for them, and re-layouts  6.52 us (6%)
  waiting for transfers between devices  6.02 us (6%)
    all_to_all x1, blocking collectives, body(): return jnp.sum(lax.all_to_all(sent, LAYER, 0, 0), 0)  27 us
    ppermute x8, starting transfers between devices, permute(): return lax.ppermute(x, axis, [(i, (i + step) % size) for i in range(size)])  25.1 us
    all_to_all x2, blocking collectives, all_to_all(): return lax.all_to_all(x, axis, 0, 0, tiled=True)  21.4 us
    pallas_call x7, Pallas kernels, call(): pl.pallas_call(kernel, out_shape=shape, in_specs=in_specs, out_specs=VMEM...  9.59 us
    all_to_all x1, starting transfers between devices, all_to_all(): return lax.all_to_all(x, axis, 0, 0, tiled=True)  8.85 us
    unnamed x22, local copies, waits for them, and re-layouts  6.48 us
    all_to_all x1, waiting for transfers between devices, all_to_all(): return lax.all_to_all(x, axis, 0, 0, tiled=True)  4.78 us
  transfers between devices with their start and end apart: 9, of which 2 were waited for; matrix products, arithmetic and copies ran while one was open for 0% of the time, Pallas kernels for 4%

profile of v4, /device:TPU:32, one launch (start us, length us, event | category | flops | bytes accessed | tf_op | source)
XLA Modules:
  0.0 105.4 jit_solution(1279881098609296439)
XLA Ops:
  0.0 0.0 copy-start.5
  0.0 0.8 copy-done.5
  0.8 0.0 copy-start.6
  0.8 0.8 copy-done.6
  1.7 0.9 shard_map.92
  2.5 8.9 %all-to-all-start = ((bf16[8,256,128]{2,1,0:T(8,128)(2,1)}), bf16[8,256,128]{2,1,0:T(8,128)(2,1)S(1)}, u32[]{:S(2)}, u32[]{:S(2)}) async-start(bf16[8,256,128]{2,1,0:T(8,128)(2,1)} %bitcast.6), calls=%async_computation | async-start | bytes 1048576 | tf_op jit(solution)/shard_map/all_to_all | solution.py:146
  11.4 0.1 pad_add_fusion.here_ref
  11.5 1.6 %copy-done = bf16[1,128,8192]{2,1,0:T(8,128)(2,1)S(1)} copy-done((bf16[1,128,8192]{2,1,0:T(8,128)(2,1)S(1)}, bf16[1,128,8192]{2,1,0:T(8,128)(2,1)}, u32[]{:S(2)}) %copy-start) | copy-done | bytes 2097176
  13.1 1.6 %copy-done.2 = bf16[1,128,8192]{2,1,0:T(8,128)(2,1)S(1)} copy-done((bf16[1,128,8192]{2,1,0:T(8,128)(2,1)S(1)}, bf16[1,128,8192]{2,1,0:T(8,128)(2,1)}, u32[]{:S(2)}) %copy-start.2) | copy-done | bytes 2097176
  14.7 2.0 %shard_map.91 = bf16[128,8192]{1,0:T(8,128)(2,1)} custom-call(s32[4]{0:T(128)S(1)} %pad_add_fusion.here_ref, bf16[128,8192]{1,0:T(8,128)(2,1)S(1)} %bitcast.13, bf16[128,8192]{1,0:T(8,128)(2,1)S(1)} %bitcast.16), custom_call_target="tpu_custom_call" | custom-call | tf_op jit(solution)/shard_map/pallas_call | solution.py:133
  16.7 2.0 %collective-permute-start = (bf16[128,8192]{1,0:T(8,128)(2,1)}, bf16[128,8192]{1,0:T(8,128)(2,1)}, u32[]{:S(2)}, u32[]{:S(2)}) collective-permute-start(bf16[128,8192]{1,0:T(8,128)(2,1)} %shard_map.91), channel_id=1, source_target_pairs={{0,16},{16,0},{1,17},{17,1},{2,18},{18,2},{3,19},{19,3},{4,20},{20... | collective-permute-start | bytes 6291464 | tf_op jit(solution)/shard_map/ppermute | solution.py:150
  18.8 4.8 %all-to-all-done.refs_0_ = bf16[8,256,128]{2,1,0:T(8,128)(2,1)S(1)} async-done(((bf16[8,256,128]{2,1,0:T(8,128)(2,1)}), bf16[8,256,128]{2,1,0:T(8,128)(2,1)S(1)}, u32[]{:S(2)}, u32[]{:S(2)}) %all-to-all-start) | async-done | bytes 524320 | tf_op jit(solution)/shard_map/all_to_all | solution.py:146
  23.6 1.9 %collective-permute-start.1 = (bf16[4,256,128]{2,1,0:T(8,128)(2,1)S(1)}, bf16[4,256,128]{2,1,0:T(8,128)(2,1)S(1)}, u32[]{:S(2)}, u32[]{:S(2)}) collective-permute-start(bf16[4,256,128]{2,1,0:T(8,128)(2,1)S(1)} %get-tuple-element.6), channel_id=1, source_target_pairs={{0,128},{128,256},{256,384},{384,0},{1,129},{129,257},{257,385},{3... | collective-permute-start | bytes 786440 | tf_op jit(solution)/shard_map/ppermute | solution.py:150
  25.5 5.1 %collective-permute-start.3 = (bf16[4,256,128]{2,1,0:T(8,128)(2,1)S(1)}, bf16[4,256,128]{2,1,0:T(8,128)(2,1)S(1)}, u32[]{:S(2)}, u32[]{:S(2)}) collective-permute-start(bf16[4,256,128]{2,1,0:T(8,128)(2,1)S(1)} %get-tuple-element.5), channel_id=1, source_target_pairs={{0,384},{128,0},{256,128},{384,256},{1,385},{129,1},{257,129},{385... | collective-permute-start | bytes 786440 | tf_op jit(solution)/shard_map/ppermute | solution.py:150
  30.6 1.9 %collective-permute-start.5 = (bf16[4,256,128]{2,1,0:T(8,128)(2,1)S(1)}, bf16[4,256,128]{2,1,0:T(8,128)(2,1)S(1)}, u32[]{:S(2)}, u32[]{:S(2)}) collective-permute-start(bf16[4,256,128]{2,1,0:T(8,128)(2,1)S(1)} %get-tuple-element.5), channel_id=1, source_target_pairs={{0,128},{128,256},{256,384},{384,0},{1,129},{129,257},{257,385},{3... | collective-permute-start | bytes 786440 | tf_op jit(solution)/shard_map/ppermute | solution.py:150
  32.6 5.1 %collective-permute-start.6 = (bf16[4,256,128]{2,1,0:T(8,128)(2,1)S(1)}, bf16[4,256,128]{2,1,0:T(8,128)(2,1)S(1)}, u32[]{:S(2)}, u32[]{:S(2)}) collective-permute-start(bf16[4,256,128]{2,1,0:T(8,128)(2,1)S(1)} %get-tuple-element.6), channel_id=1, source_target_pairs={{0,384},{128,0},{256,128},{384,256},{1,385},{129,1},{257,129},{385... | collective-permute-start | bytes 786440 | tf_op jit(solution)/shard_map/ppermute | solution.py:150
  37.7 0.0 collective-permute-done.1.refs_1_
  37.7 1.9 %collective-permute-start.2 = (bf16[4,256,128]{2,1,0:T(8,128)(2,1)S(1)}, bf16[4,256,128]{2,1,0:T(8,128)(2,1)S(1)}, u32[]{:S(2)}, u32[]{:S(2)}) collective-permute-start(bf16[4,256,128]{2,1,0:T(8,128)(2,1)S(1)} %collective-permute-done.1.refs_1_), channel_id=1, source_target_pairs={{0,128},{128,256},{256,384},{384,0},{1,129},{129,257},{257,385},{3... | collective-permute-start | bytes 786440 | tf_op jit(solution)/shard_map/ppermute | solution.py:150
  39.6 0.0 collective-permute-done.3.refs_4_
  39.7 5.1 %collective-permute-start.4 = (bf16[4,256,128]{2,1,0:T(8,128)(2,1)S(1)}, bf16[4,256,128]{2,1,0:T(8,128)(2,1)S(1)}, u32[]{:S(2)}, u32[]{:S(2)}) collective-permute-start(bf16[4,256,128]{2,1,0:T(8,128)(2,1)S(1)} %collective-permute-done.3.refs_4_), channel_id=1, source_target_pairs={{0,384},{128,0},{256,128},{384,256},{1,385},{129,1},{257,129},{385... | collective-permute-start | bytes 786440 | tf_op jit(solution)/shard_map/ppermute | solution.py:150
  44.8 0.0 collective-permute-done.got_ref
  44.8 0.0 collective-permute-done.5.refs_2_
  44.8 0.0 collective-permute-done.6.refs_3_
  44.8 0.0 copy-done.1
  44.8 0.0 copy-start.3
  44.9 1.6 %copy-done.3 = bf16[1,128,8192]{2,1,0:T(8,128)(2,1)S(1)} copy-done((bf16[1,128,8192]{2,1,0:T(8,128)(2,1)S(1)}, bf16[1,128,8192]{2,1,0:T(8,128)(2,1)}, u32[]{:S(2)}) %copy-start.3) | copy-done | bytes 2097176
  46.4 2.6 %shard_map.93.refs_2_ = f32[2,128,128]{2,1,0:T(8,128)S(1)} custom-call(s32[4]{0:T(128)S(1)} %pad_add_fusion.here_ref, bf16[128,8192]{1,0:T(8,128)(2,1)S(1)} %bitcast.14, bf16[128,8192]{1,0:T(8,128)(2,1)S(1)} %bitcast.17, bf16[128,8192]{1,0:T(8,128)(2,1)} %collective-permute-done.got_ref, bf16[8,256,128]{2,1,0:T(8,128)(2,1)S(1)} %all-to-all-done.refs_0_, ...), custom_call_target="tpu_custom_call" | custom-call | flops 402653184 | bytes 6291456 | tf_op jit(solution)/shard_map/pallas_call | solution.py:133
  49.0 0.0 copy-start.4
  49.0 0.0 copy-start.7
  49.1 0.0 copy-start.8
  49.1 0.0 copy-start.9
  49.1 0.0 copy-start.10
  49.1 0.0 collective-permute-done.2.refs_0_
  49.1 0.0 collective-permute-done.4.refs_1_
  49.1 2.1 %shard_map.94.mine_ref = bf16[2,128,128]{2,1,0:T(8,128)(2,1)S(1)} custom-call(s32[4]{0:T(128)S(1)} %pad_add_fusion.here_ref, bf16[128,8192]{1,0:T(8,128)(2,1)S(1)} %bitcast.15, bf16[128,8192]{1,0:T(8,128)(2,1)S(1)} %bitcast.18, bf16[128,8192]{1,0:T(8,128)(2,1)} %collective-permute-done.got_ref, bf16[4,256,128]{2,1,0:T(8,128)(2,1)S(1)} %collective-permute-done.2.refs_0_, ...), custom_call_target="tpu_custom_call" | custom-call | tf_op jit(solution)/shard_map/pallas_call | solution.py:133
  51.2 1.9 %collective-permute-start.7 = (bf16[2,128,128]{2,1,0:T(8,128)(2,1)S(1)}, bf16[2,128,128]{2,1,0:T(8,128)(2,1)S(1)}, u32[]{:S(2)}, u32[]{:S(2)}) collective-permute-start(bf16[2,128,128]{2,1,0:T(8,128)(2,1)S(1)} %shard_map.94.mine_ref), channel_id=1, source_target_pairs={{0,16},{16,0},{1,17},{17,1},{2,18},{18,2},{3,19},{19,3},{4,20},{20... | collective-permute-start | bytes 196616 | tf_op jit(solution)/shard_map/ppermute | solution.py:150
  53.1 1.2 %collective-permute-done.7.got_ref = bf16[2,128,128]{2,1,0:T(8,128)(2,1)S(1)} collective-permute-done((bf16[2,128,128]{2,1,0:T(8,128)(2,1)S(1)}, bf16[2,128,128]{2,1,0:T(8,128)(2,1)S(1)}, u32[]{:S(2)}, u32[]{:S(2)}) %collective-permute-start.7) | collective-permute-done | bytes 65568 | tf_op jit(solution)/shard_map/ppermute | solution.py:150
  54.4 0.7 shard_map.95
  55.1 10.5 %all_to_all.24.parts_ref = bf16[4,128,128]{2,1,0:T(8,128)(2,1)S(1)} all-to-all(bf16[4,128,128]{2,1,0:T(8,128)(2,1)S(1)} %shard_map.95), channel_id=1, replica_groups=mesh['y'=4,'zlo'=4,'core'=2,'zhi'=4,'x'=4] {'y'}, dimensions={0} | all-to-all | bytes 262144 | tf_op jit(solution)/shard_map/all_to_all | solution.py:146
  65.6 11.0 %all_to_all.25.parts_ref = bf16[4,128,128]{2,1,0:T(8,128)(2,1)S(1)} all-to-all(bf16[4,128,128]{2,1,0:T(8,128)(2,1)S(1)} %shard_map.96), channel_id=1, replica_groups=mesh['y'=4,'zlo'=4,'core'=2,'zhi'=4,'x'=4] {'zlo'}, dimensions={0} | all-to-all | bytes 262144 | tf_op jit(solution)/shard_map/all_to_all | solution.py:146
  76.6 0.0 copy-done.4
  76.6 0.0 copy-done.7
  76.6 0.0 copy-done.8
  76.6 0.0 copy-done.9
  76.6 0.0 copy-done.10
  76.6 1.2 %shard_map.97 = f32[16,16]{1,0:T(8,128)S(1)} custom-call(bf16[4,128,128]{2,1,0:T(8,128)(2,1)S(1)} %all_to_all.25.parts_ref, f32[128,128]{1,0:T(8,128)S(1)} %bitcast.22, f32[128,128]{1,0:T(8,128)S(1)} %bitcast.23, f32[1,128]{1,0:T(1,128)S(1)} %copy-done.9, f32[1,128]{1,0:T(1,128)S(1)} %copy-done.10, bf16[16,16384]{1,0:T(8,128)(2,1)S(1)} %bitcast.19), custom_call_target="tpu_custom_call" | custom-call | tf_op jit(solution)/shard_map/pallas_call | solution.py:133
  77.8 27.0 %all_to_all.26 = f32[16,1,16]{2,1,0:T(1,128)S(1)} all-to-all(f32[16,1,16]{2,1,0:T(1,128)S(1)} %bitcast.24), channel_id=1, replica_groups=mesh['y'=4,'zlo'=4,'core'=2,'zhi'=4,'x'=4] {'zhi','x'}, dimensions={0} | all-to-all | bytes 2048 | tf_op jit(solution)/shard_map/all_to_all | solution.py:193
  104.8 0.5 reduce_sum.9
  (5 shorter events, 0.1 us)
Async XLA Ops:
  0.0 0.8 copy-start.5
  0.8 0.8 copy-start.6
  2.5 21.0 %all-to-all-start = ((bf16[8,256,128]{2,1,0:T(8,128)(2,1)}), bf16[8,256,128]{2,1,0:T(8,128)(2,1)S(1)}, u32[]{:S(2)}, u32[]{:S(2)}) async-start(bf16[8,256,128]{2,1,0:T(8,128)(2,1)} %bitcast.6), calls=%async_computation | async-start | bytes 1048576 | tf_op jit(solution)/shard_map/all_to_all | solution.py:146
  11.5 1.6 %copy-start = (bf16[1,128,8192]{2,1,0:T(8,128)(2,1)S(1)}, bf16[1,128,8192]{2,1,0:T(8,128)(2,1)}, u32[]{:S(2)}) copy-start(bf16[1,128,8192]{2,1,0:T(8,128)(2,1)} %param.9) | copy-start | bytes 6291460
  13.1 1.6 %copy-start.2 = (bf16[1,128,8192]{2,1,0:T(8,128)(2,1)S(1)}, bf16[1,128,8192]{2,1,0:T(8,128)(2,1)}, u32[]{:S(2)}) copy-start(bf16[1,128,8192]{2,1,0:T(8,128)(2,1)} %param.10) | copy-start | bytes 6291460
  14.7 30.2 %copy-start.1 = (bf16[1,128,8192]{2,1,0:T(8,128)(2,1)S(1)}, bf16[1,128,8192]{2,1,0:T(8,128)(2,1)}, u32[]{:S(2)}) copy-start(bf16[1,128,8192]{2,1,0:T(8,128)(2,1)} %param.9) | copy-start | bytes 6291460
  16.7 28.1 %collective-permute-start = (bf16[128,8192]{1,0:T(8,128)(2,1)}, bf16[128,8192]{1,0:T(8,128)(2,1)}, u32[]{:S(2)}, u32[]{:S(2)}) collective-permute-start(bf16[128,8192]{1,0:T(8,128)(2,1)} %shard_map.91), channel_id=1, source_target_pairs={{0,16},{16,0},{1,17},{17,1},{2,18},{18,2},{3,19},{19,3},{4,20},{20... | collective-permute-start | bytes 6291464 | tf_op jit(solution)/shard_map/ppermute | solution.py:150
  23.6 14.1 %collective-permute-start.1 = (bf16[4,256,128]{2,1,0:T(8,128)(2,1)S(1)}, bf16[4,256,128]{2,1,0:T(8,128)(2,1)S(1)}, u32[]{:S(2)}, u32[]{:S(2)}) collective-permute-start(bf16[4,256,128]{2,1,0:T(8,128)(2,1)S(1)} %get-tuple-element.6), channel_id=1, source_target_pairs={{0,128},{128,256},{256,384},{384,0},{1,129},{129,257},{257,385},{3... | collective-permute-start | bytes 786440 | tf_op jit(solution)/shard_map/ppermute | solution.py:150
  25.5 14.2 %collective-permute-start.3 = (bf16[4,256,128]{2,1,0:T(8,128)(2,1)S(1)}, bf16[4,256,128]{2,1,0:T(8,128)(2,1)S(1)}, u32[]{:S(2)}, u32[]{:S(2)}) collective-permute-start(bf16[4,256,128]{2,1,0:T(8,128)(2,1)S(1)} %get-tuple-element.5), channel_id=1, source_target_pairs={{0,384},{128,0},{256,128},{384,256},{1,385},{129,1},{257,129},{385... | collective-permute-start | bytes 786440 | tf_op jit(solution)/shard_map/ppermute | solution.py:150
  30.6 14.2 %collective-permute-start.5 = (bf16[4,256,128]{2,1,0:T(8,128)(2,1)S(1)}, bf16[4,256,128]{2,1,0:T(8,128)(2,1)S(1)}, u32[]{:S(2)}, u32[]{:S(2)}) collective-permute-start(bf16[4,256,128]{2,1,0:T(8,128)(2,1)S(1)} %get-tuple-element.5), channel_id=1, source_target_pairs={{0,128},{128,256},{256,384},{384,0},{1,129},{129,257},{257,385},{3... | collective-permute-start | bytes 786440 | tf_op jit(solution)/shard_map/ppermute | solution.py:150
  32.6 12.3 %collective-permute-start.6 = (bf16[4,256,128]{2,1,0:T(8,128)(2,1)S(1)}, bf16[4,256,128]{2,1,0:T(8,128)(2,1)S(1)}, u32[]{:S(2)}, u32[]{:S(2)}) collective-permute-start(bf16[4,256,128]{2,1,0:T(8,128)(2,1)S(1)} %get-tuple-element.6), channel_id=1, source_target_pairs={{0,384},{128,0},{256,128},{384,256},{1,385},{129,1},{257,129},{385... | collective-permute-start | bytes 786440 | tf_op jit(solution)/shard_map/ppermute | solution.py:150
  37.7 11.4 %collective-permute-start.2 = (bf16[4,256,128]{2,1,0:T(8,128)(2,1)S(1)}, bf16[4,256,128]{2,1,0:T(8,128)(2,1)S(1)}, u32[]{:S(2)}, u32[]{:S(2)}) collective-permute-start(bf16[4,256,128]{2,1,0:T(8,128)(2,1)S(1)} %collective-permute-done.1.refs_1_), channel_id=1, source_target_pairs={{0,128},{128,256},{256,384},{384,0},{1,129},{129,257},{257,385},{3... | collective-permute-start | bytes 786440 | tf_op jit(solution)/shard_map/ppermute | solution.py:150
  39.7 9.4 %collective-permute-start.4 = (bf16[4,256,128]{2,1,0:T(8,128)(2,1)S(1)}, bf16[4,256,128]{2,1,0:T(8,128)(2,1)S(1)}, u32[]{:S(2)}, u32[]{:S(2)}) collective-permute-start(bf16[4,256,128]{2,1,0:T(8,128)(2,1)S(1)} %collective-permute-done.3.refs_4_), channel_id=1, source_target_pairs={{0,384},{128,0},{256,128},{384,256},{1,385},{129,1},{257,129},{385... | collective-permute-start | bytes 786440 | tf_op jit(solution)/shard_map/ppermute | solution.py:150
  44.8 1.6 %copy-start.3 = (bf16[1,128,8192]{2,1,0:T(8,128)(2,1)S(1)}, bf16[1,128,8192]{2,1,0:T(8,128)(2,1)}, u32[]{:S(2)}) copy-start(bf16[1,128,8192]{2,1,0:T(8,128)(2,1)} %param.10) | copy-start | bytes 6291460
  49.0 27.5 %copy-start.4 = (bf16[1,16,16384]{2,1,0:T(8,128)(2,1)S(1)}, bf16[1,16,16384]{2,1,0:T(8,128)(2,1)}, u32[]{:S(2)}) copy-start(bf16[1,16,16384]{2,1,0:T(8,128)(2,1)} %param.17) | copy-start | bytes 1572868
  49.0 27.5 %copy-start.7 = (f32[1,128,128]{2,1,0:T(8,128)S(1)}, f32[1,128,128]{2,1,0:T(8,128)}, u32[]{:S(2)}) copy-start(f32[1,128,128]{2,1,0:T(8,128)} %param.13) | copy-start | bytes 196612
  49.1 27.5 %copy-start.8 = (f32[1,128,128]{2,1,0:T(8,128)S(1)}, f32[1,128,128]{2,1,0:T(8,128)}, u32[]{:S(2)}) copy-start(f32[1,128,128]{2,1,0:T(8,128)} %param.14) | copy-start | bytes 196612
  49.1 27.5 %copy-start.9 = (f32[1,128]{1,0:T(1,128)S(1)}, f32[1,128]{1,0:T(1,128)}, u32[]{:S(2)}) copy-start(f32[1,128]{1,0:T(1,128)} %eig_a.1) | copy-start | bytes 1540
  49.1 27.5 %copy-start.10 = (f32[1,128]{1,0:T(1,128)S(1)}, f32[1,128]{1,0:T(1,128)}, u32[]{:S(2)}) copy-start(f32[1,128]{1,0:T(1,128)} %eig_g.1) | copy-start | bytes 1540
  51.2 3.1 %collective-permute-start.7 = (bf16[2,128,128]{2,1,0:T(8,128)(2,1)S(1)}, bf16[2,128,128]{2,1,0:T(8,128)(2,1)S(1)}, u32[]{:S(2)}, u32[]{:S(2)}) collective-permute-start(bf16[2,128,128]{2,1,0:T(8,128)(2,1)S(1)} %shard_map.94.mine_ref), channel_id=1, source_target_pairs={{0,16},{16,0},{1,17},{17,1},{2,18},{18,2},{3,19},{19,3},{4,20},{20... | collective-permute-start | bytes 196616 | tf_op jit(solution)/shard_map/ppermute | solution.py:150

commit v5 on v4

--- a/solution.py
+++ b/solution.py
@@ -51,19 +51,29 @@
     return mine, other
 
 
-def begin(pieces, here_ref, acts_ref, grads_ref, got_ref, *refs):
-    rows, out = refs[:-1], refs[-1]
+def begin(pieces, far, here_ref, acts_ref, grads_ref, got_ref, *refs):
+    rows, (out, ahead) = refs[:-2], refs[-2:]
     zero = jnp.zeros(out.shape[1:], F32)
     out[0], out[1] = products(
         pieces, here_ref, acts_ref, grads_ref, got_ref, rows, zero, zero
     )
-
-
-def finish(pieces, here_ref, acts_ref, grads_ref, got_ref, *refs):
-    rows, (acc, out) = refs[:-2], refs[-2:]
-    mine, other = products(
-        pieces, here_ref, acts_ref, grads_ref, got_ref, rows, acc[0], acc[1]
-    )
+    width = ahead.shape[2]
+    line = lax.rem(here_ref[0] + far, here_ref[2])
+    cols = pl.ds(pl.multiple_of(line * width, width), width)
+    ahead[0] = jnp.where(here_ref[1] == 0, acts_ref[:, cols], grads_ref[:, cols])
+    ahead[1] = got_ref[:, cols]
+
+
+def finish(ahead_ref, low_ref, high_ref, acc_ref, out):
+    mine, other = acc_ref[0], acc_ref[1]
+    depth = low_ref.shape[1]
+    done = 0
+    for rows_ref in (low_ref, high_ref):
+        for k in range(rows_ref.shape[0]):
+            cols = pl.ds((done + k) * depth, depth)
+            mine = mine + jnp.dot(ahead_ref[0, :, cols], rows_ref[k], preferred_element_type=F32)
+            other = other + jnp.dot(ahead_ref[1, :, cols], rows_ref[k], preferred_element_type=F32)
+        done += rows_ref.shape[0]
     out[0], out[1] = mine.astype(out.dtype), other.astype(out.dtype)
 
 
@@ -121,7 +131,7 @@
     n_y, n_z = lax.axis_size("y"), lax.axis_size("zlo")
     depth, rank = proj_in.shape[1:]
     line_blocks = 2 * n_z
-    half = n_z
+    part = 5 * line_blocks // 8
     local, local_g = acts[0], grads_out[0]
     n_tok = local.shape[0]
     hbm = pl.BlockSpec(memory_space=pltpu.HBM)
@@ -129,13 +139,13 @@
         [lax.axis_index("y"), lax.axis_index("core"), jnp.int32(n_y), jnp.int32(line_blocks)]
     ).astype(jnp.int32)
 
-    def call(kernel, shape, in_specs, *args, **more):
+    def call(kernel, shape, in_specs, *args, grant=20 << 20, **more):
         return pl.pallas_call(
             kernel,
             out_shape=shape,
             in_specs=in_specs,
-            out_specs=VMEM,
-            compiler_params=pltpu.CompilerParams(vmem_limit_bytes=20 << 20),
+            out_specs=jax.tree.map(lambda _: VMEM, shape),
+            compiler_params=pltpu.CompilerParams(vmem_limit_bytes=grant),
             **more,
         )(*args)
 
@@ -149,7 +159,7 @@
         size = lax.axis_size(axis)
         return lax.ppermute(x, axis, [(i, (i + step) % size) for i in range(size)])
 
-    both = call(pack, shape(n_z, 2, depth, rank), [VMEM] * 2, proj_in[0], proj_out[0])
+    both = call(pack, shape(n_z, 2, depth, rank), [VMEM] * 2, proj_in[0], proj_out[0], grant=None)
     line = all_to_all(both.reshape(line_blocks, depth, rank), ("zlo", "core"))
     send = call(
         deal, shape(*local.shape), [SMEM, hbm, hbm], here, local, local_g,
@@ -157,7 +167,7 @@
     )
     got = permute(send, "core", 1)
 
-    low, high = line[:half], line[half:]
+    low, high = line[:part], line[part:]
     below_low = permute(low, "y", 1)
     above_high = permute(high, "y", -1)
     below_high = permute(high, "y", 1)
@@ -166,21 +176,18 @@
     far_high = permute(above_high, "y", -1)
 
     below, above, far = n_y - 1, 1, n_y // 2
-    near = {(0, 0): line, (below, 0): below_low, (below, half): below_high,
-            (above, 0): above_low, (above, half): above_high}
+    near = {(0, 0): line, (below, 0): below_low, (below, part): below_high,
+            (above, 0): above_low, (above, part): above_high}
     cost = pl.CostEstimate(
         flops=4 * n_tok * rank * local.shape[1] * 3 // 4, bytes_accessed=6 << 20, transcendentals=0
     )
-    acc = call(
-        functools.partial(begin, tuple(near)), shape(2, n_tok, rank, dtype=F32),
+    acc, ahead = call(
+        functools.partial(begin, tuple(near), far),
+        (shape(2, n_tok, rank, dtype=F32), shape(2, n_tok, line_blocks * depth)),
         [SMEM] + [VMEM] * (3 + len(near)),
         here, local, local_g, got, *near.values(), cost_estimate=cost,
     )
-    mine = call(
-        functools.partial(finish, ((far, 0), (far, half))), shape(2, n_tok, rank),
-        [SMEM] + [VMEM] * 6,
-        here, local, local_g, got, far_low, far_high, acc,
-    )
+    mine = call(finish, shape(2, n_tok, rank), [VMEM] * 4, ahead, far_low, far_high, acc)
     grad = call(
         functools.partial(outer, float(tokens)), shape(n_y, rank, rank),
         [SMEM, VMEM, VMEM], here, mine, permute(mine, "core", 1),

time: 106 us -> 109 us (1.028)
  waiting for transfers between devices: 6.02 us -> 16.4 us
  starting transfers between devices: 34 us -> 30.7 us
  blocking collectives: 48.4 us -> 46.6 us
  local copies, waits for them, and re-layouts: 6.52 us -> 4.84 us
    ppermute x8, waiting for transfers between devices: 1.24 us -> 11.6 us  [permute(): return lax.ppermute(x, axis, [(i, (i + step) % size) for i in range(size)])]
    ppermute x8, starting transfers between devices: 25.1 us -> 21.9 us  [permute(): return lax.ppermute(x, axis, [(i, (i + step) % size) for i in range(size)])]
    all_to_all x2, blocking collectives: 21.4 us -> 19.6 us  [all_to_all(): return lax.all_to_all(x, axis, 0, 0, tiled=True)]
    unnamed x22 -> x18, local copies, waits for them, and re-layouts: 6.48 us -> 4.8 us
  transfers between devices with their start and end apart: 9 -> 9, of which waited for: 2 -> 4; matrix products, arithmetic and copies ran while one was open for 0% -> 0% of each run, Pallas kernels for 4% -> 4%
where the time goes in v5:
time: 109 us; the launch traced here: 108 us
  blocking collectives  46.6 us (43%)
  starting transfers between devices  30.7 us (28%)
  waiting for transfers between devices  16.4 us (15%)
  Pallas kernels  8.86 us (8%)
  local copies, waits for them, and re-layouts  4.84 us (4%)
    all_to_all x1, blocking collectives, body(): return jnp.sum(lax.all_to_all(sent, LAYER, 0, 0), 0)  27 us
    ppermute x8, starting transfers between devices, permute(): return lax.ppermute(x, axis, [(i, (i + step) % size) for i in range(size)])  21.9 us
    all_to_all x2, blocking collectives, all_to_all(): return lax.all_to_all(x, axis, 0, 0, tiled=True)  19.6 us
    ppermute x8, waiting for transfers between devices, permute(): return lax.ppermute(x, axis, [(i, (i + step) % size) for i in range(size)])  11.6 us
    pallas_call x7, Pallas kernels, call(): pl.pallas_call(kernel, out_shape=shape, in_specs=in_specs, out_specs=jax....  8.86 us
    all_to_all x1, starting transfers between devices, all_to_all(): return lax.all_to_all(x, axis, 0, 0, tiled=True)  8.85 us
    unnamed x18, local copies, waits for them, and re-layouts  4.8 us
    all_to_all x1, waiting for transfers between devices, all_to_all(): return lax.all_to_all(x, axis, 0, 0, tiled=True)  4.78 us
  transfers between devices with their start and end apart: 9, of which 4 were waited for; matrix products, arithmetic and copies ran while one was open for 0% of the time, Pallas kernels for 4%

profile of v5, /device:TPU:32, one launch (start us, length us, event | category | flops | bytes accessed | tf_op | source)
XLA Modules:
  0.0 108.3 jit_solution(12580666388855600599)
XLA Ops:
  0.0 1.7 %shard_map.92 = bf16[4,2,256,128]{3,2,1,0:T(8,128)(2,1)} custom-call(bf16[256,128]{1,0:T(8,128)(2,1)} %bitcast.22, bf16[256,128]{1,0:T(8,128)(2,1)} %bitcast.23), custom_call_target="tpu_custom_call" | custom-call | tf_op jit(solution)/shard_map/pallas_call | solution.py:143
  1.7 8.9 %all-to-all-start = ((bf16[8,256,128]{2,1,0:T(8,128)(2,1)}), bf16[8,256,128]{2,1,0:T(8,128)(2,1)S(1)}, u32[]{:S(2)}, u32[]{:S(2)}) async-start(bf16[8,256,128]{2,1,0:T(8,128)(2,1)} %bitcast.21), calls=%async_computation | async-start | bytes 1048576 | tf_op jit(solution)/shard_map/all_to_all | solution.py:156
  10.6 0.1 pad_add_fusion.here_ref
  10.7 0.0 copy-start
  10.7 1.6 %copy-done = bf16[1,128,8192]{2,1,0:T(8,128)(2,1)S(1)} copy-done((bf16[1,128,8192]{2,1,0:T(8,128)(2,1)S(1)}, bf16[1,128,8192]{2,1,0:T(8,128)(2,1)}, u32[]{:S(2)}) %copy-start) | copy-done | bytes 2097176
  12.3 0.0 copy-start.2
  12.3 1.6 %copy-done.2 = bf16[1,128,8192]{2,1,0:T(8,128)(2,1)S(1)} copy-done((bf16[1,128,8192]{2,1,0:T(8,128)(2,1)S(1)}, bf16[1,128,8192]{2,1,0:T(8,128)(2,1)}, u32[]{:S(2)}) %copy-start.2) | copy-done | bytes 2097176
  13.9 0.0 copy-start.1
  13.9 2.0 %shard_map.91 = bf16[128,8192]{1,0:T(8,128)(2,1)} custom-call(s32[4]{0:T(128)S(1)} %pad_add_fusion.here_ref, bf16[128,8192]{1,0:T(8,128)(2,1)S(1)} %bitcast.13, bf16[128,8192]{1,0:T(8,128)(2,1)S(1)} %bitcast.15), custom_call_target="tpu_custom_call" | custom-call | tf_op jit(solution)/shard_map/pallas_call | solution.py:143
  15.9 2.0 %collective-permute-start = (bf16[128,8192]{1,0:T(8,128)(2,1)}, bf16[128,8192]{1,0:T(8,128)(2,1)}, u32[]{:S(2)}, u32[]{:S(2)}) collective-permute-start(bf16[128,8192]{1,0:T(8,128)(2,1)} %shard_map.91), channel_id=1, source_target_pairs={{0,16},{16,0},{1,17},{17,1},{2,18},{18,2},{3,19},{19,3},{4,20},{20... | collective-permute-start | bytes 6291464 | tf_op jit(solution)/shard_map/ppermute | solution.py:160
  17.9 4.8 %all-to-all-done.refs_0_ = bf16[8,256,128]{2,1,0:T(8,128)(2,1)S(1)} async-done(((bf16[8,256,128]{2,1,0:T(8,128)(2,1)}), bf16[8,256,128]{2,1,0:T(8,128)(2,1)S(1)}, u32[]{:S(2)}, u32[]{:S(2)}) %all-to-all-start) | async-done | bytes 524320 | tf_op jit(solution)/shard_map/all_to_all | solution.py:156
  22.8 1.9 %collective-permute-start.1 = (bf16[5,256,128]{2,1,0:T(8,128)(2,1)S(1)}, bf16[5,256,128]{2,1,0:T(8,128)(2,1)S(1)}, u32[]{:S(2)}, u32[]{:S(2)}) collective-permute-start(bf16[5,256,128]{2,1,0:T(8,128)(2,1)S(1)} %slice.8), channel_id=1, source_target_pairs={{0,128},{128,256},{256,384},{384,0},{1,129},{129,257},{257,385},{3... | collective-permute-start | bytes 983048 | tf_op jit(solution)/shard_map/ppermute | solution.py:160
  24.7 5.1 %collective-permute-start.4 = (bf16[3,256,128]{2,1,0:T(8,128)(2,1)S(1)}, bf16[3,256,128]{2,1,0:T(8,128)(2,1)S(1)}, u32[]{:S(2)}, u32[]{:S(2)}) collective-permute-start(bf16[3,256,128]{2,1,0:T(8,128)(2,1)S(1)} %slice.9), channel_id=1, source_target_pairs={{0,384},{128,0},{256,128},{384,256},{1,385},{129,1},{257,129},{385... | collective-permute-start | bytes 589832 | tf_op jit(solution)/shard_map/ppermute | solution.py:160
  29.8 1.9 %collective-permute-start.3 = (bf16[5,256,128]{2,1,0:T(8,128)(2,1)S(1)}, bf16[5,256,128]{2,1,0:T(8,128)(2,1)S(1)}, u32[]{:S(2)}, u32[]{:S(2)}) collective-permute-start(bf16[5,256,128]{2,1,0:T(8,128)(2,1)S(1)} %slice.8), channel_id=1, source_target_pairs={{0,384},{128,0},{256,128},{384,256},{1,385},{129,1},{257,129},{385... | collective-permute-start | bytes 983048 | tf_op jit(solution)/shard_map/ppermute | solution.py:160
  31.8 3.5 %collective-permute-done.1.refs_1_ = bf16[5,256,128]{2,1,0:T(8,128)(2,1)S(1)} collective-permute-done((bf16[5,256,128]{2,1,0:T(8,128)(2,1)S(1)}, bf16[5,256,128]{2,1,0:T(8,128)(2,1)S(1)}, u32[]{:S(2)}, u32[]{:S(2)}) %collective-permute-start.1) | collective-permute-done | bytes 327712 | tf_op jit(solution)/shard_map/ppermute | solution.py:160
  35.3 1.9 %collective-permute-start.5 = (bf16[5,256,128]{2,1,0:T(8,128)(2,1)S(1)}, bf16[5,256,128]{2,1,0:T(8,128)(2,1)S(1)}, u32[]{:S(2)}, u32[]{:S(2)}) collective-permute-start(bf16[5,256,128]{2,1,0:T(8,128)(2,1)S(1)} %collective-permute-done.1.refs_1_), channel_id=1, source_target_pairs={{0,128},{128,256},{256,384},{384,0},{1,129},{129,257},{257,385},{3... | collective-permute-start | bytes 983048 | tf_op jit(solution)/shard_map/ppermute | solution.py:160
  37.2 1.9 %collective-permute-start.2 = (bf16[3,256,128]{2,1,0:T(8,128)(2,1)S(1)}, bf16[3,256,128]{2,1,0:T(8,128)(2,1)S(1)}, u32[]{:S(2)}, u32[]{:S(2)}) collective-permute-start(bf16[3,256,128]{2,1,0:T(8,128)(2,1)S(1)} %slice.9), channel_id=1, source_target_pairs={{0,128},{128,256},{256,384},{384,0},{1,129},{129,257},{257,385},{3... | collective-permute-start | bytes 589832 | tf_op jit(solution)/shard_map/ppermute | solution.py:160
  39.1 0.0 collective-permute-done.4.refs_4_
  39.1 5.1 %collective-permute-start.6 = (bf16[3,256,128]{2,1,0:T(8,128)(2,1)S(1)}, bf16[3,256,128]{2,1,0:T(8,128)(2,1)S(1)}, u32[]{:S(2)}, u32[]{:S(2)}) collective-permute-start(bf16[3,256,128]{2,1,0:T(8,128)(2,1)S(1)} %collective-permute-done.4.refs_4_), channel_id=1, source_target_pairs={{0,384},{128,0},{256,128},{384,256},{1,385},{129,1},{257,129},{385... | collective-permute-start | bytes 589832 | tf_op jit(solution)/shard_map/ppermute | solution.py:160
  44.3 6.9 %collective-permute-done.2.refs_2_ = bf16[3,256,128]{2,1,0:T(8,128)(2,1)S(1)} collective-permute-done((bf16[3,256,128]{2,1,0:T(8,128)(2,1)S(1)}, bf16[3,256,128]{2,1,0:T(8,128)(2,1)S(1)}, u32[]{:S(2)}, u32[]{:S(2)}) %collective-permute-start.2) | collective-permute-done | bytes 196640 | tf_op jit(solution)/shard_map/ppermute | solution.py:160
  51.1 0.0 collective-permute-done.got_ref
  51.1 0.0 collective-permute-done.3.refs_3_
  51.2 0.0 copy-done.1
  51.2 0.0 copy-start.3
  51.2 1.6 %copy-done.3 = bf16[1,128,8192]{2,1,0:T(8,128)(2,1)S(1)} copy-done((bf16[1,128,8192]{2,1,0:T(8,128)(2,1)S(1)}, bf16[1,128,8192]{2,1,0:T(8,128)(2,1)}, u32[]{:S(2)}) %copy-start.3) | copy-done | bytes 2097176
  52.8 2.7 %shard_map.93 = (f32[2,128,128]{2,1,0:T(8,128)S(1)}, bf16[2,128,2048]{2,1,0:T(8,128)(2,1)S(1)}) custom-call(s32[4]{0:T(128)S(1)} %pad_add_fusion.here_ref, bf16[128,8192]{1,0:T(8,128)(2,1)S(1)} %bitcast.14, bf16[128,8192]{1,0:T(8,128)(2,1)S(1)} %bitcast.16, bf16[128,8192]{1,0:T(8,128)(2,1)} %collective-permute-done.got_ref, ...), custom_call_target="tpu_custom_call" | custom-call | flops 402653184 | bytes 6291456 | tf_op jit(solution)/shard_map/pallas_call | solution.py:143
  55.4 0.0 copy-start.4
  55.4 0.0 copy-start.5
  55.4 0.0 copy-start.6
  55.5 0.0 copy-start.7
  55.5 0.0 copy-start.8
  55.5 0.0 collective-permute-done.6.high_ref
  55.5 0.0 collective-permute-done.5.low_ref
  55.5 0.4 shard_map.94.mine_ref
  55.9 1.9 %collective-permute-start.7 = (bf16[2,128,128]{2,1,0:T(8,128)(2,1)S(1)}, bf16[2,128,128]{2,1,0:T(8,128)(2,1)S(1)}, u32[]{:S(2)}, u32[]{:S(2)}) collective-permute-start(bf16[2,128,128]{2,1,0:T(8,128)(2,1)S(1)} %shard_map.94.mine_ref), channel_id=1, source_target_pairs={{0,16},{16,0},{1,17},{17,1},{2,18},{18,2},{3,19},{19,3},{4,20},{20... | collective-permute-start | bytes 196616 | tf_op jit(solution)/shard_map/ppermute | solution.py:160
  57.9 1.2 %collective-permute-done.7.got_ref = bf16[2,128,128]{2,1,0:T(8,128)(2,1)S(1)} collective-permute-done((bf16[2,128,128]{2,1,0:T(8,128)(2,1)S(1)}, bf16[2,128,128]{2,1,0:T(8,128)(2,1)S(1)}, u32[]{:S(2)}, u32[]{:S(2)}) %collective-permute-start.7) | collective-permute-done | bytes 65568 | tf_op jit(solution)/shard_map/ppermute | solution.py:160
  59.1 0.7 shard_map.95
  59.8 8.4 %all_to_all.24.parts_ref = bf16[4,128,128]{2,1,0:T(8,128)(2,1)S(1)} all-to-all(bf16[4,128,128]{2,1,0:T(8,128)(2,1)S(1)} %shard_map.95), channel_id=1, replica_groups=mesh['y'=4,'zlo'=4,'core'=2,'zhi'=4,'x'=4] {'y'}, dimensions={0} | all-to-all | bytes 262144 | tf_op jit(solution)/shard_map/all_to_all | solution.py:156
  68.2 11.2 %all_to_all.25.parts_ref = bf16[4,128,128]{2,1,0:T(8,128)(2,1)S(1)} all-to-all(bf16[4,128,128]{2,1,0:T(8,128)(2,1)S(1)} %shard_map.96), channel_id=1, replica_groups=mesh['y'=4,'zlo'=4,'core'=2,'zhi'=4,'x'=4] {'zlo'}, dimensions={0} | all-to-all | bytes 262144 | tf_op jit(solution)/shard_map/all_to_all | solution.py:156
  79.4 0.0 copy-done.4
  79.4 0.0 copy-done.5
  79.4 0.0 copy-done.6
  79.4 0.0 copy-done.7
  79.5 0.0 copy-done.8
  79.5 1.2 %shard_map.97 = f32[16,16]{1,0:T(8,128)S(1)} custom-call(bf16[4,128,128]{2,1,0:T(8,128)(2,1)S(1)} %all_to_all.25.parts_ref, f32[128,128]{1,0:T(8,128)S(1)} %bitcast.18, f32[128,128]{1,0:T(8,128)S(1)} %bitcast.19, f32[1,128]{1,0:T(1,128)S(1)} %copy-done.7, f32[1,128]{1,0:T(1,128)S(1)} %copy-done.8, bf16[16,16384]{1,0:T(8,128)(2,1)S(1)} %bitcast.17), custom_call_target="tpu_custom_call" | custom-call | tf_op jit(solution)/shard_map/pallas_call | solution.py:143
  80.7 27.0 %all_to_all.26 = f32[16,1,16]{2,1,0:T(1,128)S(1)} all-to-all(f32[16,1,16]{2,1,0:T(1,128)S(1)} %bitcast.20), channel_id=1, replica_groups=mesh['y'=4,'zlo'=4,'core'=2,'zhi'=4,'x'=4] {'zhi','x'}, dimensions={0} | all-to-all | bytes 2048 | tf_op jit(solution)/shard_map/all_to_all | solution.py:200
  107.7 0.5 reduce_sum.9
  (3 shorter events, 0.1 us)
Async XLA Ops:
  1.7 21.0 %all-to-all-start = ((bf16[8,256,128]{2,1,0:T(8,128)(2,1)}), bf16[8,256,128]{2,1,0:T(8,128)(2,1)S(1)}, u32[]{:S(2)}, u32[]{:S(2)}) async-start(bf16[8,256,128]{2,1,0:T(8,128)(2,1)} %bitcast.21), calls=%async_computation | async-start | bytes 1048576 | tf_op jit(solution)/shard_map/all_to_all | solution.py:156
  10.7 1.6 %copy-start = (bf16[1,128,8192]{2,1,0:T(8,128)(2,1)S(1)}, bf16[1,128,8192]{2,1,0:T(8,128)(2,1)}, u32[]{:S(2)}) copy-start(bf16[1,128,8192]{2,1,0:T(8,128)(2,1)} %param.9) | copy-start | bytes 6291460
  12.3 1.6 %copy-start.2 = (bf16[1,128,8192]{2,1,0:T(8,128)(2,1)S(1)}, bf16[1,128,8192]{2,1,0:T(8,128)(2,1)}, u32[]{:S(2)}) copy-start(bf16[1,128,8192]{2,1,0:T(8,128)(2,1)} %param.10) | copy-start | bytes 6291460
  13.9 37.3 %copy-start.1 = (bf16[1,128,8192]{2,1,0:T(8,128)(2,1)S(1)}, bf16[1,128,8192]{2,1,0:T(8,128)(2,1)}, u32[]{:S(2)}) copy-start(bf16[1,128,8192]{2,1,0:T(8,128)(2,1)} %param.9) | copy-start | bytes 6291460
  15.9 35.2 %collective-permute-start = (bf16[128,8192]{1,0:T(8,128)(2,1)}, bf16[128,8192]{1,0:T(8,128)(2,1)}, u32[]{:S(2)}, u32[]{:S(2)}) collective-permute-start(bf16[128,8192]{1,0:T(8,128)(2,1)} %shard_map.91), channel_id=1, source_target_pairs={{0,16},{16,0},{1,17},{17,1},{2,18},{18,2},{3,19},{19,3},{4,20},{20... | collective-permute-start | bytes 6291464 | tf_op jit(solution)/shard_map/ppermute | solution.py:160
  22.8 12.5 %collective-permute-start.1 = (bf16[5,256,128]{2,1,0:T(8,128)(2,1)S(1)}, bf16[5,256,128]{2,1,0:T(8,128)(2,1)S(1)}, u32[]{:S(2)}, u32[]{:S(2)}) collective-permute-start(bf16[5,256,128]{2,1,0:T(8,128)(2,1)S(1)} %slice.8), channel_id=1, source_target_pairs={{0,128},{128,256},{256,384},{384,0},{1,129},{129,257},{257,385},{3... | collective-permute-start | bytes 983048 | tf_op jit(solution)/shard_map/ppermute | solution.py:160
  24.7 14.4 %collective-permute-start.4 = (bf16[3,256,128]{2,1,0:T(8,128)(2,1)S(1)}, bf16[3,256,128]{2,1,0:T(8,128)(2,1)S(1)}, u32[]{:S(2)}, u32[]{:S(2)}) collective-permute-start(bf16[3,256,128]{2,1,0:T(8,128)(2,1)S(1)} %slice.9), channel_id=1, source_target_pairs={{0,384},{128,0},{256,128},{384,256},{1,385},{129,1},{257,129},{385... | collective-permute-start | bytes 589832 | tf_op jit(solution)/shard_map/ppermute | solution.py:160
  29.8 21.3 %collective-permute-start.3 = (bf16[5,256,128]{2,1,0:T(8,128)(2,1)S(1)}, bf16[5,256,128]{2,1,0:T(8,128)(2,1)S(1)}, u32[]{:S(2)}, u32[]{:S(2)}) collective-permute-start(bf16[5,256,128]{2,1,0:T(8,128)(2,1)S(1)} %slice.8), channel_id=1, source_target_pairs={{0,384},{128,0},{256,128},{384,256},{1,385},{129,1},{257,129},{385... | collective-permute-start | bytes 983048 | tf_op jit(solution)/shard_map/ppermute | solution.py:160
  35.3 20.2 %collective-permute-start.5 = (bf16[5,256,128]{2,1,0:T(8,128)(2,1)S(1)}, bf16[5,256,128]{2,1,0:T(8,128)(2,1)S(1)}, u32[]{:S(2)}, u32[]{:S(2)}) collective-permute-start(bf16[5,256,128]{2,1,0:T(8,128)(2,1)S(1)} %collective-permute-done.1.refs_1_), channel_id=1, source_target_pairs={{0,128},{128,256},{256,384},{384,0},{1,129},{129,257},{257,385},{3... | collective-permute-start | bytes 983048 | tf_op jit(solution)/shard_map/ppermute | solution.py:160
  37.2 14.0 %collective-permute-start.2 = (bf16[3,256,128]{2,1,0:T(8,128)(2,1)S(1)}, bf16[3,256,128]{2,1,0:T(8,128)(2,1)S(1)}, u32[]{:S(2)}, u32[]{:S(2)}) collective-permute-start(bf16[3,256,128]{2,1,0:T(8,128)(2,1)S(1)} %slice.9), channel_id=1, source_target_pairs={{0,128},{128,256},{256,384},{384,0},{1,129},{129,257},{257,385},{3... | collective-permute-start | bytes 589832 | tf_op jit(solution)/shard_map/ppermute | solution.py:160
  39.1 16.3 %collective-permute-start.6 = (bf16[3,256,128]{2,1,0:T(8,128)(2,1)S(1)}, bf16[3,256,128]{2,1,0:T(8,128)(2,1)S(1)}, u32[]{:S(2)}, u32[]{:S(2)}) collective-permute-start(bf16[3,256,128]{2,1,0:T(8,128)(2,1)S(1)} %collective-permute-done.4.refs_4_), channel_id=1, source_target_pairs={{0,384},{128,0},{256,128},{384,256},{1,385},{129,1},{257,129},{385... | collective-permute-start | bytes 589832 | tf_op jit(solution)/shard_map/ppermute | solution.py:160
  51.2 1.6 %copy-start.3 = (bf16[1,128,8192]{2,1,0:T(8,128)(2,1)S(1)}, bf16[1,128,8192]{2,1,0:T(8,128)(2,1)}, u32[]{:S(2)}) copy-start(bf16[1,128,8192]{2,1,0:T(8,128)(2,1)} %param.10) | copy-start | bytes 6291460
  55.4 24.0 %copy-start.4 = (bf16[1,16,16384]{2,1,0:T(8,128)(2,1)S(1)}, bf16[1,16,16384]{2,1,0:T(8,128)(2,1)}, u32[]{:S(2)}) copy-start(bf16[1,16,16384]{2,1,0:T(8,128)(2,1)} %param.17) | copy-start | bytes 1572868
  55.4 24.0 %copy-start.5 = (f32[1,128,128]{2,1,0:T(8,128)S(1)}, f32[1,128,128]{2,1,0:T(8,128)}, u32[]{:S(2)}) copy-start(f32[1,128,128]{2,1,0:T(8,128)} %param.13) | copy-start | bytes 196612
  55.4 24.0 %copy-start.6 = (f32[1,128,128]{2,1,0:T(8,128)S(1)}, f32[1,128,128]{2,1,0:T(8,128)}, u32[]{:S(2)}) copy-start(f32[1,128,128]{2,1,0:T(8,128)} %param.14) | copy-start | bytes 196612
  55.5 24.0 %copy-start.7 = (f32[1,128]{1,0:T(1,128)S(1)}, f32[1,128]{1,0:T(1,128)}, u32[]{:S(2)}) copy-start(f32[1,128]{1,0:T(1,128)} %eig_a.1) | copy-start | bytes 1540
  55.5 24.0 %copy-start.8 = (f32[1,128]{1,0:T(1,128)S(1)}, f32[1,128]{1,0:T(1,128)}, u32[]{:S(2)}) copy-start(f32[1,128]{1,0:T(1,128)} %eig_g.1) | copy-start | bytes 1540
  55.9 3.1 %collective-permute-start.7 = (bf16[2,128,128]{2,1,0:T(8,128)(2,1)S(1)}, bf16[2,128,128]{2,1,0:T(8,128)(2,1)S(1)}, u32[]{:S(2)}, u32[]{:S(2)}) collective-permute-start(bf16[2,128,128]{2,1,0:T(8,128)(2,1)S(1)} %shard_map.94.mine_ref), channel_id=1, source_target_pairs={{0,16},{16,0},{1,17},{17,1},{2,18},{18,2},{3,19},{19,3},{4,20},{20... | collective-permute-start | bytes 196616 | tf_op jit(solution)/shard_map/ppermute | solution.py:160

commit v6 on v5

--- a/solution.py
+++ b/solution.py
@@ -18,10 +18,16 @@
 SMEM = pl.BlockSpec(memory_space=pltpu.SMEM)
 
 
-def pack(in_ref, out_ref, out):
-    for k in range(out.shape[0]):
-        out[k, 0] = in_ref[...]
-        out[k, 1] = out_ref[...]
+def pack(in_ref, out_ref, out, sems):
+    copies = [
+        pltpu.make_async_copy(rows, out.at[k, j], sems.at[k, j])
+        for k in range(out.shape[0])
+        for j, rows in enumerate((in_ref, out_ref))
+    ]
+    for copy in copies:
+        copy.start()
+    for copy in copies:
+        copy.wait()
 
 
 def deal(here_ref, acts_ref, grads_ref, send_ref, sem):
@@ -51,24 +57,29 @@
     return mine, other
 
 
-def begin(pieces, far, here_ref, acts_ref, grads_ref, got_ref, *refs):
+def begin(pieces, later, here_ref, acts_ref, grads_ref, got_ref, *refs):
     rows, (out, ahead) = refs[:-2], refs[-2:]
     zero = jnp.zeros(out.shape[1:], F32)
     out[0], out[1] = products(
         pieces, here_ref, acts_ref, grads_ref, got_ref, rows, zero, zero
     )
-    width = ahead.shape[2]
-    line = lax.rem(here_ref[0] + far, here_ref[2])
-    cols = pl.ds(pl.multiple_of(line * width, width), width)
-    ahead[0] = jnp.where(here_ref[1] == 0, acts_ref[:, cols], grads_ref[:, cols])
-    ahead[1] = got_ref[:, cols]
-
-
-def finish(ahead_ref, low_ref, high_ref, acc_ref, out):
+    depth = rows[0].shape[1]
+    done = 0
+    for step, first, count in later:
+        line = lax.rem(here_ref[0] + step, here_ref[2]) * here_ref[3]
+        cols = pl.ds(pl.multiple_of((line + first) * depth, depth), count * depth)
+        put = pl.ds(done * depth, count * depth)
+        ahead[0, :, put] = jnp.where(here_ref[1] == 0, acts_ref[:, cols], grads_ref[:, cols])
+        ahead[1, :, put] = got_ref[:, cols]
+        done += count
+
+
+def finish(ahead_ref, acc_ref, *refs):
+    rows, out = refs[:-1], refs[-1]
     mine, other = acc_ref[0], acc_ref[1]
-    depth = low_ref.shape[1]
     done = 0
-    for rows_ref in (low_ref, high_ref):
+    for rows_ref in rows:
+        depth = rows_ref.shape[1]
         for k in range(rows_ref.shape[0]):
             cols = pl.ds((done + k) * depth, depth)
             mine = mine + jnp.dot(ahead_ref[0, :, cols], rows_ref[k], preferred_element_type=F32)
@@ -144,9 +155,8 @@
             kernel,
             out_shape=shape,
             in_specs=in_specs,
-            out_specs=jax.tree.map(lambda _: VMEM, shape),
             compiler_params=pltpu.CompilerParams(vmem_limit_bytes=grant),
-            **more,
+            **({"out_specs": jax.tree.map(lambda _: VMEM, shape)} | more),
         )(*args)
 
     def shape(*dims, dtype=BF16):
@@ -159,7 +169,9 @@
         size = lax.axis_size(axis)
         return lax.ppermute(x, axis, [(i, (i + step) % size) for i in range(size)])
 
-    both = call(pack, shape(n_z, 2, depth, rank), [VMEM] * 2, proj_in[0], proj_out[0], grant=None)
+    both = call(pack, shape(n_z, 2, depth, rank), [VMEM] * 2,
+                proj_in[0], proj_out[0], grant=None, out_specs=pl.BlockSpec(memory_space=pl.ANY),
+                scratch_shapes=[pltpu.SemaphoreType.DMA((n_z, 2))])
     line = all_to_all(both.reshape(line_blocks, depth, rank), ("zlo", "core"))
     send = call(
         deal, shape(*local.shape), [SMEM, hbm, hbm], here, local, local_g,
@@ -176,18 +188,20 @@
     far_high = permute(above_high, "y", -1)
 
     below, above, far = n_y - 1, 1, n_y // 2
-    near = {(0, 0): line, (below, 0): below_low, (below, part): below_high,
-            (above, 0): above_low, (above, part): above_high}
+    near = {(0, 0): line, (below, 0): below_low, (above, part): above_high, (below, part): below_high}
+    later = ((above, 0, part), (far, 0, line_blocks))
+    last = (above_low, far_low, far_high)
     cost = pl.CostEstimate(
-        flops=4 * n_tok * rank * local.shape[1] * 3 // 4, bytes_accessed=6 << 20, transcendentals=0
+        flops=4 * n_tok * rank * local.shape[1] * 5 // 8, bytes_accessed=6 << 20, transcendentals=0
     )
     acc, ahead = call(
-        functools.partial(begin, tuple(near), far),
-        (shape(2, n_tok, rank, dtype=F32), shape(2, n_tok, line_blocks * depth)),
+        functools.partial(begin, tuple(near), later),
+        (shape(2, n_tok, rank, dtype=F32),
+         shape(2, n_tok, sum(count for _, _, count in later) * depth)),
         [SMEM] + [VMEM] * (3 + len(near)),
         here, local, local_g, got, *near.values(), cost_estimate=cost,
     )
-    mine = call(finish, shape(2, n_tok, rank), [VMEM] * 4, ahead, far_low, far_high, acc)
+    mine = call(finish, shape(2, n_tok, rank), [VMEM] * (2 + len(last)), ahead, acc, *last)
     grad = call(
         functools.partial(outer, float(tokens)), shape(n_y, rank, rank),
         [SMEM, VMEM, VMEM], here, mine, permute(mine, "core", 1),

time: 109 us -> 109 us (level)
  no operation moved by 1% of the time
where the time goes in v6:
time: 109 us; the launch traced here: 108 us
  blocking collectives  46.6 us (43%)
  starting transfers between devices  30.8 us (28%)
  waiting for transfers between devices  16.4 us (15%)
  Pallas kernels  8.92 us (8%)
  local copies, waits for them, and re-layouts  4.84 us (4%)
    all_to_all x1, blocking collectives, body(): return jnp.sum(lax.all_to_all(sent, LAYER, 0, 0), 0)  27 us
    ppermute x8, starting transfers between devices, permute(): return lax.ppermute(x, axis, [(i, (i + step) % size) for i in range(size)])  21.9 us
    all_to_all x2, blocking collectives, all_to_all(): return lax.all_to_all(x, axis, 0, 0, tiled=True)  19.6 us
    ppermute x8, waiting for transfers between devices, permute(): return lax.ppermute(x, axis, [(i, (i + step) % size) for i in range(size)])  11.6 us
    pallas_call x7, Pallas kernels, call(): pl.pallas_call(kernel, out_shape=shape, in_specs=in_specs, compiler_param...  8.92 us
    all_to_all x1, starting transfers between devices, all_to_all(): return lax.all_to_all(x, axis, 0, 0, tiled=True)  8.87 us
    unnamed x18, local copies, waits for them, and re-layouts  4.81 us
    all_to_all x1, waiting for transfers between devices, all_to_all(): return lax.all_to_all(x, axis, 0, 0, tiled=True)  4.78 us
  transfers between devices with their start and end apart: 9, of which 4 were waited for; matrix products, arithmetic and copies ran while one was open for 0% of the time, Pallas kernels for 4%

profile of v6, /device:TPU:32, one launch (start us, length us, event | category | flops | bytes accessed | tf_op | source)
XLA Modules:
  0.0 108.4 jit_solution(8472056440767843738)
XLA Ops:
  0.0 1.7 %shard_map.92 = bf16[4,2,256,128]{3,2,1,0:T(8,128)(2,1)} custom-call(bf16[256,128]{1,0:T(8,128)(2,1)} %bitcast.22, bf16[256,128]{1,0:T(8,128)(2,1)} %bitcast.23), custom_call_target="tpu_custom_call" | custom-call | tf_op jit(solution)/shard_map/pallas_call | solution.py:154
  1.7 8.9 %all-to-all-start = ((bf16[8,256,128]{2,1,0:T(8,128)(2,1)}), bf16[8,256,128]{2,1,0:T(8,128)(2,1)S(1)}, u32[]{:S(2)}, u32[]{:S(2)}) async-start(bf16[8,256,128]{2,1,0:T(8,128)(2,1)} %bitcast.21), calls=%async_computation | async-start | bytes 1048576 | tf_op jit(solution)/shard_map/all_to_all | solution.py:166
  10.6 0.1 pad_add_fusion.here_ref
  10.7 0.0 copy-start
  10.7 1.6 %copy-done = bf16[1,128,8192]{2,1,0:T(8,128)(2,1)S(1)} copy-done((bf16[1,128,8192]{2,1,0:T(8,128)(2,1)S(1)}, bf16[1,128,8192]{2,1,0:T(8,128)(2,1)}, u32[]{:S(2)}) %copy-start) | copy-done | bytes 2097176
  12.3 0.0 copy-start.2
  12.3 1.6 %copy-done.2 = bf16[1,128,8192]{2,1,0:T(8,128)(2,1)S(1)} copy-done((bf16[1,128,8192]{2,1,0:T(8,128)(2,1)S(1)}, bf16[1,128,8192]{2,1,0:T(8,128)(2,1)}, u32[]{:S(2)}) %copy-start.2) | copy-done | bytes 2097176
  13.9 0.0 copy-start.1
  13.9 2.0 %shard_map.91 = bf16[128,8192]{1,0:T(8,128)(2,1)} custom-call(s32[4]{0:T(128)S(1)} %pad_add_fusion.here_ref, bf16[128,8192]{1,0:T(8,128)(2,1)S(1)} %bitcast.13, bf16[128,8192]{1,0:T(8,128)(2,1)S(1)} %bitcast.15), custom_call_target="tpu_custom_call" | custom-call | tf_op jit(solution)/shard_map/pallas_call | solution.py:154
  15.9 2.0 %collective-permute-start = (bf16[128,8192]{1,0:T(8,128)(2,1)}, bf16[128,8192]{1,0:T(8,128)(2,1)}, u32[]{:S(2)}, u32[]{:S(2)}) collective-permute-start(bf16[128,8192]{1,0:T(8,128)(2,1)} %shard_map.91), channel_id=1, source_target_pairs={{0,16},{16,0},{1,17},{17,1},{2,18},{18,2},{3,19},{19,3},{4,20},{20... | collective-permute-start | bytes 6291464 | tf_op jit(solution)/shard_map/ppermute | solution.py:170
  18.0 4.8 %all-to-all-done.refs_0_ = bf16[8,256,128]{2,1,0:T(8,128)(2,1)S(1)} async-done(((bf16[8,256,128]{2,1,0:T(8,128)(2,1)}), bf16[8,256,128]{2,1,0:T(8,128)(2,1)S(1)}, u32[]{:S(2)}, u32[]{:S(2)}) %all-to-all-start) | async-done | bytes 524320 | tf_op jit(solution)/shard_map/all_to_all | solution.py:166
  22.8 1.9 %collective-permute-start.1 = (bf16[5,256,128]{2,1,0:T(8,128)(2,1)S(1)}, bf16[5,256,128]{2,1,0:T(8,128)(2,1)S(1)}, u32[]{:S(2)}, u32[]{:S(2)}) collective-permute-start(bf16[5,256,128]{2,1,0:T(8,128)(2,1)S(1)} %slice.8), channel_id=1, source_target_pairs={{0,128},{128,256},{256,384},{384,0},{1,129},{129,257},{257,385},{3... | collective-permute-start | bytes 983048 | tf_op jit(solution)/shard_map/ppermute | solution.py:170
  24.7 5.1 %collective-permute-start.2 = (bf16[3,256,128]{2,1,0:T(8,128)(2,1)S(1)}, bf16[3,256,128]{2,1,0:T(8,128)(2,1)S(1)}, u32[]{:S(2)}, u32[]{:S(2)}) collective-permute-start(bf16[3,256,128]{2,1,0:T(8,128)(2,1)S(1)} %slice.9), channel_id=1, source_target_pairs={{0,384},{128,0},{256,128},{384,256},{1,385},{129,1},{257,129},{385... | collective-permute-start | bytes 589832 | tf_op jit(solution)/shard_map/ppermute | solution.py:170
  29.9 1.9 %collective-permute-start.4 = (bf16[5,256,128]{2,1,0:T(8,128)(2,1)S(1)}, bf16[5,256,128]{2,1,0:T(8,128)(2,1)S(1)}, u32[]{:S(2)}, u32[]{:S(2)}) collective-permute-start(bf16[5,256,128]{2,1,0:T(8,128)(2,1)S(1)} %slice.8), channel_id=1, source_target_pairs={{0,384},{128,0},{256,128},{384,256},{1,385},{129,1},{257,129},{385... | collective-permute-start | bytes 983048 | tf_op jit(solution)/shard_map/ppermute | solution.py:170
  31.8 3.5 %collective-permute-done.1.refs_1_ = bf16[5,256,128]{2,1,0:T(8,128)(2,1)S(1)} collective-permute-done((bf16[5,256,128]{2,1,0:T(8,128)(2,1)S(1)}, bf16[5,256,128]{2,1,0:T(8,128)(2,1)S(1)}, u32[]{:S(2)}, u32[]{:S(2)}) %collective-permute-start.1) | collective-permute-done | bytes 327712 | tf_op jit(solution)/shard_map/ppermute | solution.py:170
  35.3 1.9 %collective-permute-start.5 = (bf16[5,256,128]{2,1,0:T(8,128)(2,1)S(1)}, bf16[5,256,128]{2,1,0:T(8,128)(2,1)S(1)}, u32[]{:S(2)}, u32[]{:S(2)}) collective-permute-start(bf16[5,256,128]{2,1,0:T(8,128)(2,1)S(1)} %collective-permute-done.1.refs_1_), channel_id=1, source_target_pairs={{0,128},{128,256},{256,384},{384,0},{1,129},{129,257},{257,385},{3... | collective-permute-start | bytes 983048 | tf_op jit(solution)/shard_map/ppermute | solution.py:170
  37.2 1.9 %collective-permute-start.3 = (bf16[3,256,128]{2,1,0:T(8,128)(2,1)S(1)}, bf16[3,256,128]{2,1,0:T(8,128)(2,1)S(1)}, u32[]{:S(2)}, u32[]{:S(2)}) collective-permute-start(bf16[3,256,128]{2,1,0:T(8,128)(2,1)S(1)} %slice.9), channel_id=1, source_target_pairs={{0,128},{128,256},{256,384},{384,0},{1,129},{129,257},{257,385},{3... | collective-permute-start | bytes 589832 | tf_op jit(solution)/shard_map/ppermute | solution.py:170
  39.1 0.0 collective-permute-done.2.refs_2_
  39.2 5.1 %collective-permute-start.6 = (bf16[3,256,128]{2,1,0:T(8,128)(2,1)S(1)}, bf16[3,256,128]{2,1,0:T(8,128)(2,1)S(1)}, u32[]{:S(2)}, u32[]{:S(2)}) collective-permute-start(bf16[3,256,128]{2,1,0:T(8,128)(2,1)S(1)} %collective-permute-done.2.refs_2_), channel_id=1, source_target_pairs={{0,384},{128,0},{256,128},{384,256},{1,385},{129,1},{257,129},{385... | collective-permute-start | bytes 589832 | tf_op jit(solution)/shard_map/ppermute | solution.py:170
  44.3 6.9 %collective-permute-done.3.refs_3_ = bf16[3,256,128]{2,1,0:T(8,128)(2,1)S(1)} collective-permute-done((bf16[3,256,128]{2,1,0:T(8,128)(2,1)S(1)}, bf16[3,256,128]{2,1,0:T(8,128)(2,1)S(1)}, u32[]{:S(2)}, u32[]{:S(2)}) %collective-permute-start.3) | collective-permute-done | bytes 196640 | tf_op jit(solution)/shard_map/ppermute | solution.py:170
  51.2 0.0 collective-permute-done.got_ref
  51.2 0.0 copy-done.1
  51.2 0.0 copy-start.3
  51.2 1.6 %copy-done.3 = bf16[1,128,8192]{2,1,0:T(8,128)(2,1)S(1)} copy-done((bf16[1,128,8192]{2,1,0:T(8,128)(2,1)S(1)}, bf16[1,128,8192]{2,1,0:T(8,128)(2,1)}, u32[]{:S(2)}) %copy-start.3) | copy-done | bytes 2097176
  52.8 2.5 %shard_map.93 = (f32[2,128,128]{2,1,0:T(8,128)S(1)}, bf16[2,128,3328]{2,1,0:T(8,128)(2,1)S(1)}) custom-call(s32[4]{0:T(128)S(1)} %pad_add_fusion.here_ref, bf16[128,8192]{1,0:T(8,128)(2,1)S(1)} %bitcast.14, bf16[128,8192]{1,0:T(8,128)(2,1)S(1)} %bitcast.16, bf16[128,8192]{1,0:T(8,128)(2,1)} %collective-permute-done.got_ref, ...), custom_call_target="tpu_custom_call" | custom-call | flops 335544320 | bytes 6291456 | tf_op jit(solution)/shard_map/pallas_call | solution.py:154
  55.3 0.0 copy-start.4
  55.3 0.0 copy-start.5
  55.3 0.0 copy-start.6
  55.4 0.0 copy-start.7
  55.4 0.0 copy-start.8
  55.4 0.0 collective-permute-done.4.refs_0_
  55.4 0.0 collective-permute-done.6.refs_2_
  55.4 0.0 collective-permute-done.5.refs_1_
  55.4 0.6 shard_map.94.mine_ref
  56.0 1.9 %collective-permute-start.7 = (bf16[2,128,128]{2,1,0:T(8,128)(2,1)S(1)}, bf16[2,128,128]{2,1,0:T(8,128)(2,1)S(1)}, u32[]{:S(2)}, u32[]{:S(2)}) collective-permute-start(bf16[2,128,128]{2,1,0:T(8,128)(2,1)S(1)} %shard_map.94.mine_ref), channel_id=1, source_target_pairs={{0,16},{16,0},{1,17},{17,1},{2,18},{18,2},{3,19},{19,3},{4,20},{20... | collective-permute-start | bytes 196616 | tf_op jit(solution)/shard_map/ppermute | solution.py:170
  57.9 1.2 %collective-permute-done.7.got_ref = bf16[2,128,128]{2,1,0:T(8,128)(2,1)S(1)} collective-permute-done((bf16[2,128,128]{2,1,0:T(8,128)(2,1)S(1)}, bf16[2,128,128]{2,1,0:T(8,128)(2,1)S(1)}, u32[]{:S(2)}, u32[]{:S(2)}) %collective-permute-start.7) | collective-permute-done | bytes 65568 | tf_op jit(solution)/shard_map/ppermute | solution.py:170
  59.2 0.7 shard_map.95
  59.9 8.4 %all_to_all.24.parts_ref = bf16[4,128,128]{2,1,0:T(8,128)(2,1)S(1)} all-to-all(bf16[4,128,128]{2,1,0:T(8,128)(2,1)S(1)} %shard_map.95), channel_id=1, replica_groups=mesh['y'=4,'zlo'=4,'core'=2,'zhi'=4,'x'=4] {'y'}, dimensions={0} | all-to-all | bytes 262144 | tf_op jit(solution)/shard_map/all_to_all | solution.py:166
  68.3 11.2 %all_to_all.25.parts_ref = bf16[4,128,128]{2,1,0:T(8,128)(2,1)S(1)} all-to-all(bf16[4,128,128]{2,1,0:T(8,128)(2,1)S(1)} %shard_map.96), channel_id=1, replica_groups=mesh['y'=4,'zlo'=4,'core'=2,'zhi'=4,'x'=4] {'zlo'}, dimensions={0} | all-to-all | bytes 262144 | tf_op jit(solution)/shard_map/all_to_all | solution.py:166
  79.5 0.0 copy-done.4
  79.5 0.0 copy-done.5
  79.5 0.0 copy-done.6
  79.5 0.0 copy-done.7
  79.5 0.0 copy-done.8
  79.5 1.2 %shard_map.97 = f32[16,16]{1,0:T(8,128)S(1)} custom-call(bf16[4,128,128]{2,1,0:T(8,128)(2,1)S(1)} %all_to_all.25.parts_ref, f32[128,128]{1,0:T(8,128)S(1)} %bitcast.18, f32[128,128]{1,0:T(8,128)S(1)} %bitcast.19, f32[1,128]{1,0:T(1,128)S(1)} %copy-done.7, f32[1,128]{1,0:T(1,128)S(1)} %copy-done.8, bf16[16,16384]{1,0:T(8,128)(2,1)S(1)} %bitcast.17), custom_call_target="tpu_custom_call" | custom-call | tf_op jit(solution)/shard_map/pallas_call | solution.py:154
  80.8 27.0 %all_to_all.26 = f32[16,1,16]{2,1,0:T(1,128)S(1)} all-to-all(f32[16,1,16]{2,1,0:T(1,128)S(1)} %bitcast.20), channel_id=1, replica_groups=mesh['y'=4,'zlo'=4,'core'=2,'zhi'=4,'x'=4] {'zhi','x'}, dimensions={0} | all-to-all | bytes 2048 | tf_op jit(solution)/shard_map/all_to_all | solution.py:214
  107.8 0.5 reduce_sum.9
  (3 shorter events, 0.1 us)
Async XLA Ops:
  1.7 21.0 %all-to-all-start = ((bf16[8,256,128]{2,1,0:T(8,128)(2,1)}), bf16[8,256,128]{2,1,0:T(8,128)(2,1)S(1)}, u32[]{:S(2)}, u32[]{:S(2)}) async-start(bf16[8,256,128]{2,1,0:T(8,128)(2,1)} %bitcast.21), calls=%async_computation | async-start | bytes 1048576 | tf_op jit(solution)/shard_map/all_to_all | solution.py:166
  10.7 1.6 %copy-start = (bf16[1,128,8192]{2,1,0:T(8,128)(2,1)S(1)}, bf16[1,128,8192]{2,1,0:T(8,128)(2,1)}, u32[]{:S(2)}) copy-start(bf16[1,128,8192]{2,1,0:T(8,128)(2,1)} %param.9) | copy-start | bytes 6291460
  12.3 1.6 %copy-start.2 = (bf16[1,128,8192]{2,1,0:T(8,128)(2,1)S(1)}, bf16[1,128,8192]{2,1,0:T(8,128)(2,1)}, u32[]{:S(2)}) copy-start(bf16[1,128,8192]{2,1,0:T(8,128)(2,1)} %param.10) | copy-start | bytes 6291460
  13.9 37.3 %copy-start.1 = (bf16[1,128,8192]{2,1,0:T(8,128)(2,1)S(1)}, bf16[1,128,8192]{2,1,0:T(8,128)(2,1)}, u32[]{:S(2)}) copy-start(bf16[1,128,8192]{2,1,0:T(8,128)(2,1)} %param.9) | copy-start | bytes 6291460
  15.9 35.2 %collective-permute-start = (bf16[128,8192]{1,0:T(8,128)(2,1)}, bf16[128,8192]{1,0:T(8,128)(2,1)}, u32[]{:S(2)}, u32[]{:S(2)}) collective-permute-start(bf16[128,8192]{1,0:T(8,128)(2,1)} %shard_map.91), channel_id=1, source_target_pairs={{0,16},{16,0},{1,17},{17,1},{2,18},{18,2},{3,19},{19,3},{4,20},{20... | collective-permute-start | bytes 6291464 | tf_op jit(solution)/shard_map/ppermute | solution.py:170
  22.8 12.5 %collective-permute-start.1 = (bf16[5,256,128]{2,1,0:T(8,128)(2,1)S(1)}, bf16[5,256,128]{2,1,0:T(8,128)(2,1)S(1)}, u32[]{:S(2)}, u32[]{:S(2)}) collective-permute-start(bf16[5,256,128]{2,1,0:T(8,128)(2,1)S(1)} %slice.8), channel_id=1, source_target_pairs={{0,128},{128,256},{256,384},{384,0},{1,129},{129,257},{257,385},{3... | collective-permute-start | bytes 983048 | tf_op jit(solution)/shard_map/ppermute | solution.py:170
  24.7 14.4 %collective-permute-start.2 = (bf16[3,256,128]{2,1,0:T(8,128)(2,1)S(1)}, bf16[3,256,128]{2,1,0:T(8,128)(2,1)S(1)}, u32[]{:S(2)}, u32[]{:S(2)}) collective-permute-start(bf16[3,256,128]{2,1,0:T(8,128)(2,1)S(1)} %slice.9), channel_id=1, source_target_pairs={{0,384},{128,0},{256,128},{384,256},{1,385},{129,1},{257,129},{385... | collective-permute-start | bytes 589832 | tf_op jit(solution)/shard_map/ppermute | solution.py:170
  29.9 25.5 %collective-permute-start.4 = (bf16[5,256,128]{2,1,0:T(8,128)(2,1)S(1)}, bf16[5,256,128]{2,1,0:T(8,128)(2,1)S(1)}, u32[]{:S(2)}, u32[]{:S(2)}) collective-permute-start(bf16[5,256,128]{2,1,0:T(8,128)(2,1)S(1)} %slice.8), channel_id=1, source_target_pairs={{0,384},{128,0},{256,128},{384,256},{1,385},{129,1},{257,129},{385... | collective-permute-start | bytes 983048 | tf_op jit(solution)/shard_map/ppermute | solution.py:170
  35.3 20.1 %collective-permute-start.5 = (bf16[5,256,128]{2,1,0:T(8,128)(2,1)S(1)}, bf16[5,256,128]{2,1,0:T(8,128)(2,1)S(1)}, u32[]{:S(2)}, u32[]{:S(2)}) collective-permute-start(bf16[5,256,128]{2,1,0:T(8,128)(2,1)S(1)} %collective-permute-done.1.refs_1_), channel_id=1, source_target_pairs={{0,128},{128,256},{256,384},{384,0},{1,129},{129,257},{257,385},{3... | collective-permute-start | bytes 983048 | tf_op jit(solution)/shard_map/ppermute | solution.py:170
  37.2 14.0 %collective-permute-start.3 = (bf16[3,256,128]{2,1,0:T(8,128)(2,1)S(1)}, bf16[3,256,128]{2,1,0:T(8,128)(2,1)S(1)}, u32[]{:S(2)}, u32[]{:S(2)}) collective-permute-start(bf16[3,256,128]{2,1,0:T(8,128)(2,1)S(1)} %slice.9), channel_id=1, source_target_pairs={{0,128},{128,256},{256,384},{384,0},{1,129},{129,257},{257,385},{3... | collective-permute-start | bytes 589832 | tf_op jit(solution)/shard_map/ppermute | solution.py:170
  39.2 16.2 %collective-permute-start.6 = (bf16[3,256,128]{2,1,0:T(8,128)(2,1)S(1)}, bf16[3,256,128]{2,1,0:T(8,128)(2,1)S(1)}, u32[]{:S(2)}, u32[]{:S(2)}) collective-permute-start(bf16[3,256,128]{2,1,0:T(8,128)(2,1)S(1)} %collective-permute-done.2.refs_2_), channel_id=1, source_target_pairs={{0,384},{128,0},{256,128},{384,256},{1,385},{129,1},{257,129},{385... | collective-permute-start | bytes 589832 | tf_op jit(solution)/shard_map/ppermute | solution.py:170
  51.2 1.6 %copy-start.3 = (bf16[1,128,8192]{2,1,0:T(8,128)(2,1)S(1)}, bf16[1,128,8192]{2,1,0:T(8,128)(2,1)}, u32[]{:S(2)}) copy-start(bf16[1,128,8192]{2,1,0:T(8,128)(2,1)} %param.10) | copy-start | bytes 6291460
  55.3 24.2 %copy-start.4 = (bf16[1,16,16384]{2,1,0:T(8,128)(2,1)S(1)}, bf16[1,16,16384]{2,1,0:T(8,128)(2,1)}, u32[]{:S(2)}) copy-start(bf16[1,16,16384]{2,1,0:T(8,128)(2,1)} %param.17) | copy-start | bytes 1572868
  55.3 24.2 %copy-start.5 = (f32[1,128,128]{2,1,0:T(8,128)S(1)}, f32[1,128,128]{2,1,0:T(8,128)}, u32[]{:S(2)}) copy-start(f32[1,128,128]{2,1,0:T(8,128)} %param.13) | copy-start | bytes 196612
  55.3 24.2 %copy-start.6 = (f32[1,128,128]{2,1,0:T(8,128)S(1)}, f32[1,128,128]{2,1,0:T(8,128)}, u32[]{:S(2)}) copy-start(f32[1,128,128]{2,1,0:T(8,128)} %param.14) | copy-start | bytes 196612
  55.4 24.2 %copy-start.7 = (f32[1,128]{1,0:T(1,128)S(1)}, f32[1,128]{1,0:T(1,128)}, u32[]{:S(2)}) copy-start(f32[1,128]{1,0:T(1,128)} %eig_a.1) | copy-start | bytes 1540
  55.4 24.2 %copy-start.8 = (f32[1,128]{1,0:T(1,128)S(1)}, f32[1,128]{1,0:T(1,128)}, u32[]{:S(2)}) copy-start(f32[1,128]{1,0:T(1,128)} %eig_g.1) | copy-start | bytes 1540
  56.0 3.1 %collective-permute-start.7 = (bf16[2,128,128]{2,1,0:T(8,128)(2,1)S(1)}, bf16[2,128,128]{2,1,0:T(8,128)(2,1)S(1)}, u32[]{:S(2)}, u32[]{:S(2)}) collective-permute-start(bf16[2,128,128]{2,1,0:T(8,128)(2,1)S(1)} %shard_map.94.mine_ref), channel_id=1, source_target_pairs={{0,16},{16,0},{1,17},{17,1},{2,18},{18,2},{3,19},{19,3},{4,20},{20... | collective-permute-start | bytes 196616 | tf_op jit(solution)/shard_map/ppermute | solution.py:170

commit v7 on v6

--- a/solution.py
+++ b/solution.py
@@ -44,11 +44,16 @@
         copy.wait()
 
 
+def line_of(here_ref, step):
+    y, core, n_y, line_blocks = (here_ref[k] for k in range(4))
+    return lax.rem(y + jnp.where(core == 0, step, n_y - step), n_y) * line_blocks
+
+
 def products(pieces, here_ref, acts_ref, grads_ref, got_ref, row_refs, mine, other):
     even = here_ref[1] == 0
     for (step, first), rows_ref in zip(pieces, row_refs):
         count, depth, _ = rows_ref.shape
-        line = lax.rem(here_ref[0] + step, here_ref[2]) * here_ref[3]
+        line = line_of(here_ref, step)
         for k in range(count):
             cols = pl.ds(pl.multiple_of((line + (first + k)) * depth, depth), depth)
             keep = jnp.where(even, acts_ref[:, cols], grads_ref[:, cols])
@@ -66,7 +71,7 @@
     depth = rows[0].shape[1]
     done = 0
     for step, first, count in later:
-        line = lax.rem(here_ref[0] + step, here_ref[2]) * here_ref[3]
+        line = line_of(here_ref, step)
         cols = pl.ds(pl.multiple_of((line + first) * depth, depth), count * depth)
         put = pl.ds(done * depth, count * depth)
         ahead[0, :, put] = jnp.where(here_ref[1] == 0, acts_ref[:, cols], grads_ref[:, cols])
@@ -142,7 +147,7 @@
     n_y, n_z = lax.axis_size("y"), lax.axis_size("zlo")
     depth, rank = proj_in.shape[1:]
     line_blocks = 2 * n_z
-    part = 5 * line_blocks // 8
+    part = 3 * line_blocks // 4
     local, local_g = acts[0], grads_out[0]
     n_tok = local.shape[0]
     hbm = pl.BlockSpec(memory_space=pltpu.HBM)
@@ -179,18 +184,26 @@
     )
     got = permute(send, "core", 1)
 
+    def along_y(x, step):
+        moves = [
+            (y * 2 + core, (y + (step if core == 0 else -step)) % n_y * 2 + core)
+            for y in range(n_y)
+            for core in range(2)
+        ]
+        return lax.ppermute(x, ("y", "core"), moves)
+
     low, high = line[:part], line[part:]
-    below_low = permute(low, "y", 1)
-    above_high = permute(high, "y", -1)
-    below_high = permute(high, "y", 1)
-    above_low = permute(low, "y", -1)
-    far_low = permute(below_low, "y", 1)
-    far_high = permute(above_high, "y", -1)
-
-    below, above, far = n_y - 1, 1, n_y // 2
-    near = {(0, 0): line, (below, 0): below_low, (above, part): above_high, (below, part): below_high}
-    later = ((above, 0, part), (far, 0, line_blocks))
-    last = (above_low, far_low, far_high)
+    behind_low = along_y(low, 1)
+    behind_high = along_y(high, 1)
+    ahead_high = along_y(high, -1)
+    ahead_low = along_y(low, -1)
+    far_low = along_y(behind_low, 1)
+    far_high = along_y(ahead_high, -1)
+
+    behind, front, far = n_y - 1, 1, n_y // 2
+    near = {(0, 0): line, (behind, 0): behind_low, (behind, part): behind_high, (front, part): ahead_high}
+    later = ((front, 0, part), (far, 0, line_blocks))
+    last = (ahead_low, far_low, far_high)
     cost = pl.CostEstimate(
         flops=4 * n_tok * rank * local.shape[1] * 5 // 8, bytes_accessed=6 << 20, transcendentals=0
     )
@@ -202,14 +215,24 @@
         here, local, local_g, got, *near.values(), cost_estimate=cost,
     )
     mine = call(finish, shape(2, n_tok, rank), [VMEM] * (2 + len(last)), ahead, acc, *last)
+
+    def at(y, z, core):
+        return (y * n_z + z) * 2 + core
+
+    def exchange(x, core_along_y):
+        other = 1 - core_along_y
+        groups = [[at(y, z, core_along_y) for y in range(n_y)] for z in range(n_z)]
+        groups += [[at(y, z, other) for z in range(n_z)] for y in range(n_y)]
+        return lax.all_to_all(x, CTX, 0, 0, axis_index_groups=groups, tiled=True)
+
     grad = call(
         functools.partial(outer, float(tokens)), shape(n_y, rank, rank),
         [SMEM, VMEM, VMEM], here, mine, permute(mine, "core", 1),
     )
-    grad = call(add_up, shape(n_z, rank, rank), [VMEM], all_to_all(grad, "y"))
+    grad = call(add_up, shape(n_z, rank, rank), [VMEM], exchange(grad, 0))
     sent = call(
         score, shape(n_layer, train_grads.shape[1], dtype=F32), [VMEM] * 6,
-        all_to_all(grad, "zlo"), basis_a[0], basis_g[0], eig_a, eig_g, train_grads[0],
+        exchange(grad, 1), basis_a[0], basis_g[0], eig_a, eig_g, train_grads[0],
     )
     return jnp.sum(lax.all_to_all(sent, LAYER, 0, 0), 0)
 

time: 109 us -> 109 us (level)
  starting transfers between devices: 30.8 us -> 34.4 us
  waiting for transfers between devices: 16.4 us -> 13.9 us
  blocking collectives: 46.6 us -> 45.5 us
    ppermute x0 -> x6, starting transfers between devices: none -> 21.6 us  [along_y(): return lax.ppermute(x, ('y', 'core'), moves)]
    ppermute x8 -> x2, starting transfers between devices: 21.9 us -> 3.95 us  [permute(): return lax.ppermute(x, axis, [(i, (i + step) % size) for i in range(size)])]
    ppermute x8 -> x2, waiting for transfers between devices: 11.6 us -> 1.22 us  [permute(): return lax.ppermute(x, axis, [(i, (i + step) % size) for i in range(size)])]
    ppermute x0 -> x6, waiting for transfers between devices: none -> 7.85 us  [along_y(): return lax.ppermute(x, ('y', 'core'), moves)]
    all_to_all x1, blocking collectives: 27 us -> 25.5 us  [body(): return jnp.sum(lax.all_to_all(sent, LAYER, 0, 0), 0)]
where the time goes in v7:
time: 109 us; the launch traced here: 108 us
  blocking collectives  45.5 us (42%)
  starting transfers between devices  34.4 us (32%)
  waiting for transfers between devices  13.9 us (13%)
  Pallas kernels  8.93 us (8%)
  local copies, waits for them, and re-layouts  4.84 us (4%)
    all_to_all x1, blocking collectives, body(): return jnp.sum(lax.all_to_all(sent, LAYER, 0, 0), 0)  25.5 us
    ppermute x6, starting transfers between devices, along_y(): return lax.ppermute(x, ('y', 'core'), moves)  21.6 us
    all_to_all x2, blocking collectives, exchange(): return lax.all_to_all(x, CTX, 0, 0, axis_index_groups=groups, tiled=True)  20 us
    pallas_call x7, Pallas kernels, call(): pl.pallas_call(kernel, out_shape=shape, in_specs=in_specs, compiler_param...  8.93 us
    all_to_all x1, starting transfers between devices, all_to_all(): return lax.all_to_all(x, axis, 0, 0, tiled=True)  8.87 us
    ppermute x6, waiting for transfers between devices, along_y(): return lax.ppermute(x, ('y', 'core'), moves)  7.85 us
    unnamed x18, local copies, waits for them, and re-layouts  4.8 us
    all_to_all x1, waiting for transfers between devices, all_to_all(): return lax.all_to_all(x, axis, 0, 0, tiled=True)  4.78 us
  transfers between devices with their start and end apart: 9, of which 4 were waited for; matrix products, arithmetic and copies ran while one was open for 0% of the time, Pallas kernels for 4%

profile of v7, /device:TPU:32, one launch (start us, length us, event | category | flops | bytes accessed | tf_op | source)
XLA Modules:
  0.0 108.4 jit_solution(2829856556088916101)
XLA Ops:
  0.0 1.7 %shard_map.92 = bf16[4,2,256,128]{3,2,1,0:T(8,128)(2,1)} custom-call(bf16[256,128]{1,0:T(8,128)(2,1)} %bitcast.22, bf16[256,128]{1,0:T(8,128)(2,1)} %bitcast.23), custom_call_target="tpu_custom_call" | custom-call | tf_op jit(solution)/shard_map/pallas_call | solution.py:159
  1.7 8.9 %all-to-all-start = ((bf16[8,256,128]{2,1,0:T(8,128)(2,1)}), bf16[8,256,128]{2,1,0:T(8,128)(2,1)S(1)}, u32[]{:S(2)}, u32[]{:S(2)}) async-start(bf16[8,256,128]{2,1,0:T(8,128)(2,1)} %bitcast.21), calls=%async_computation | async-start | bytes 1048576 | tf_op jit(solution)/shard_map/all_to_all | solution.py:171
  10.6 0.1 pad_add_fusion.here_ref
  10.7 0.0 copy-start
  10.7 1.6 %copy-done = bf16[1,128,8192]{2,1,0:T(8,128)(2,1)S(1)} copy-done((bf16[1,128,8192]{2,1,0:T(8,128)(2,1)S(1)}, bf16[1,128,8192]{2,1,0:T(8,128)(2,1)}, u32[]{:S(2)}) %copy-start) | copy-done | bytes 2097176
  12.3 0.0 copy-start.2
  12.3 1.6 %copy-done.2 = bf16[1,128,8192]{2,1,0:T(8,128)(2,1)S(1)} copy-done((bf16[1,128,8192]{2,1,0:T(8,128)(2,1)S(1)}, bf16[1,128,8192]{2,1,0:T(8,128)(2,1)}, u32[]{:S(2)}) %copy-start.2) | copy-done | bytes 2097176
  13.9 0.0 copy-start.1
  13.9 2.0 %shard_map.91 = bf16[128,8192]{1,0:T(8,128)(2,1)} custom-call(s32[4]{0:T(128)S(1)} %pad_add_fusion.here_ref, bf16[128,8192]{1,0:T(8,128)(2,1)S(1)} %bitcast.13, bf16[128,8192]{1,0:T(8,128)(2,1)S(1)} %bitcast.15), custom_call_target="tpu_custom_call" | custom-call | tf_op jit(solution)/shard_map/pallas_call | solution.py:159
  15.9 2.0 %collective-permute-start = (bf16[128,8192]{1,0:T(8,128)(2,1)}, bf16[128,8192]{1,0:T(8,128)(2,1)}, u32[]{:S(2)}, u32[]{:S(2)}) collective-permute-start(bf16[128,8192]{1,0:T(8,128)(2,1)} %shard_map.91), channel_id=1, source_target_pairs={{0,16},{16,0},{1,17},{17,1},{2,18},{18,2},{3,19},{19,3},{4,20},{20... | collective-permute-start | bytes 6291464 | tf_op jit(solution)/shard_map/ppermute | solution.py:175
  18.0 4.8 %all-to-all-done.refs_0_ = bf16[8,256,128]{2,1,0:T(8,128)(2,1)S(1)} async-done(((bf16[8,256,128]{2,1,0:T(8,128)(2,1)}), bf16[8,256,128]{2,1,0:T(8,128)(2,1)S(1)}, u32[]{:S(2)}, u32[]{:S(2)}) %all-to-all-start) | async-done | bytes 524320 | tf_op jit(solution)/shard_map/all_to_all | solution.py:171
  22.8 1.9 %collective-permute-start.1 = (bf16[6,256,128]{2,1,0:T(8,128)(2,1)S(1)}, bf16[6,256,128]{2,1,0:T(8,128)(2,1)S(1)}, u32[]{:S(2)}, u32[]{:S(2)}) collective-permute-start(bf16[6,256,128]{2,1,0:T(8,128)(2,1)S(1)} %slice.8), channel_id=1, source_target_pairs={{0,128},{16,400},{128,256},{144,16},{256,384},{272,144},{384,0},{4... | collective-permute-start | bytes 1179656 | tf_op jit(solution)/shard_map/ppermute | solution.py:193
  24.7 5.1 %collective-permute-start.4 = (bf16[6,256,128]{2,1,0:T(8,128)(2,1)S(1)}, bf16[6,256,128]{2,1,0:T(8,128)(2,1)S(1)}, u32[]{:S(2)}, u32[]{:S(2)}) collective-permute-start(bf16[6,256,128]{2,1,0:T(8,128)(2,1)S(1)} %slice.8), channel_id=1, source_target_pairs={{0,384},{16,144},{128,0},{144,272},{256,128},{272,400},{384,256},{... | collective-permute-start | bytes 1179656 | tf_op jit(solution)/shard_map/ppermute | solution.py:193
  29.8 7.3 %collective-permute-done.1.refs_1_ = bf16[6,256,128]{2,1,0:T(8,128)(2,1)S(1)} collective-permute-done((bf16[6,256,128]{2,1,0:T(8,128)(2,1)S(1)}, bf16[6,256,128]{2,1,0:T(8,128)(2,1)S(1)}, u32[]{:S(2)}, u32[]{:S(2)}) %collective-permute-start.1) | collective-permute-done | bytes 393248 | tf_op jit(solution)/shard_map/ppermute | solution.py:193
  37.1 1.9 %collective-permute-start.5 = (bf16[6,256,128]{2,1,0:T(8,128)(2,1)S(1)}, bf16[6,256,128]{2,1,0:T(8,128)(2,1)S(1)}, u32[]{:S(2)}, u32[]{:S(2)}) collective-permute-start(bf16[6,256,128]{2,1,0:T(8,128)(2,1)S(1)} %collective-permute-done.1.refs_1_), channel_id=1, source_target_pairs={{0,128},{16,400},{128,256},{144,16},{256,384},{272,144},{384,0},{4... | collective-permute-start | bytes 1179656 | tf_op jit(solution)/shard_map/ppermute | solution.py:193
  39.0 5.1 %collective-permute-start.3 = (bf16[2,256,128]{2,1,0:T(8,128)(2,1)S(1)}, bf16[2,256,128]{2,1,0:T(8,128)(2,1)S(1)}, u32[]{:S(2)}, u32[]{:S(2)}) collective-permute-start(bf16[2,256,128]{2,1,0:T(8,128)(2,1)S(1)} %slice.9), channel_id=1, source_target_pairs={{0,384},{16,144},{128,0},{144,272},{256,128},{272,400},{384,256},{... | collective-permute-start | bytes 393224 | tf_op jit(solution)/shard_map/ppermute | solution.py:193
  44.2 1.9 %collective-permute-start.2 = (bf16[2,256,128]{2,1,0:T(8,128)(2,1)S(1)}, bf16[2,256,128]{2,1,0:T(8,128)(2,1)S(1)}, u32[]{:S(2)}, u32[]{:S(2)}) collective-permute-start(bf16[2,256,128]{2,1,0:T(8,128)(2,1)S(1)} %slice.9), channel_id=1, source_target_pairs={{0,128},{16,400},{128,256},{144,16},{256,384},{272,144},{384,0},{4... | collective-permute-start | bytes 393224 | tf_op jit(solution)/shard_map/ppermute | solution.py:193
  46.1 0.6 collective-permute-done.3.refs_3_
  46.7 5.6 %collective-permute-start.6 = (bf16[2,256,128]{2,1,0:T(8,128)(2,1)S(1)}, bf16[2,256,128]{2,1,0:T(8,128)(2,1)S(1)}, u32[]{:S(2)}, u32[]{:S(2)}) collective-permute-start(bf16[2,256,128]{2,1,0:T(8,128)(2,1)S(1)} %collective-permute-done.3.refs_3_), channel_id=1, source_target_pairs={{0,384},{16,144},{128,0},{144,272},{256,128},{272,400},{384,256},{... | collective-permute-start | bytes 393224 | tf_op jit(solution)/shard_map/ppermute | solution.py:193
  52.2 0.0 collective-permute-done.2.refs_2_
  52.3 0.0 collective-permute-done.got_ref
  52.3 0.0 copy-done.1
  52.3 0.0 copy-start.3
  52.3 1.6 %copy-done.3 = bf16[1,128,8192]{2,1,0:T(8,128)(2,1)S(1)} copy-done((bf16[1,128,8192]{2,1,0:T(8,128)(2,1)S(1)}, bf16[1,128,8192]{2,1,0:T(8,128)(2,1)}, u32[]{:S(2)}) %copy-start.3) | copy-done | bytes 2097176
  53.9 2.5 %shard_map.93 = (f32[2,128,128]{2,1,0:T(8,128)S(1)}, bf16[2,128,3584]{2,1,0:T(8,128)(2,1)S(1)}) custom-call(s32[4]{0:T(128)S(1)} %pad_add_fusion.here_ref, bf16[128,8192]{1,0:T(8,128)(2,1)S(1)} %bitcast.14, bf16[128,8192]{1,0:T(8,128)(2,1)S(1)} %bitcast.16, bf16[128,8192]{1,0:T(8,128)(2,1)} %collective-permute-done.got_ref, ...), custom_call_target="tpu_custom_call" | custom-call | flops 335544320 | bytes 6291456 | tf_op jit(solution)/shard_map/pallas_call | solution.py:159
  56.4 0.0 copy-start.4
  56.4 0.0 copy-start.5
  56.4 0.0 copy-start.6
  56.4 0.0 copy-start.7
  56.5 0.0 copy-start.8
  56.5 0.0 collective-permute-done.6.refs_2_
  56.5 0.0 collective-permute-done.4.refs_0_
  56.5 0.0 collective-permute-done.5.refs_1_
  56.5 0.6 shard_map.94.mine_ref
  57.1 1.9 %collective-permute-start.7 = (bf16[2,128,128]{2,1,0:T(8,128)(2,1)S(1)}, bf16[2,128,128]{2,1,0:T(8,128)(2,1)S(1)}, u32[]{:S(2)}, u32[]{:S(2)}) collective-permute-start(bf16[2,128,128]{2,1,0:T(8,128)(2,1)S(1)} %shard_map.94.mine_ref), channel_id=1, source_target_pairs={{0,16},{16,0},{1,17},{17,1},{2,18},{18,2},{3,19},{19,3},{4,20},{20... | collective-permute-start | bytes 196616 | tf_op jit(solution)/shard_map/ppermute | solution.py:175
  59.1 1.2 %collective-permute-done.7.got_ref = bf16[2,128,128]{2,1,0:T(8,128)(2,1)S(1)} collective-permute-done((bf16[2,128,128]{2,1,0:T(8,128)(2,1)S(1)}, bf16[2,128,128]{2,1,0:T(8,128)(2,1)S(1)}, u32[]{:S(2)}, u32[]{:S(2)}) %collective-permute-start.7) | collective-permute-done | bytes 65568 | tf_op jit(solution)/shard_map/ppermute | solution.py:175
  60.3 0.7 shard_map.95
  61.0 9.0 %all_to_all.24.parts_ref = bf16[4,128,128]{2,1,0:T(8,128)(2,1)S(1)} all-to-all(bf16[4,128,128]{2,1,0:T(8,128)(2,1)S(1)} %shard_map.95), channel_id=1, replica_groups={{0,128,256,384},{32,160,288,416},{64,192,320,448},{96,224,352,480},{16,..., dimensions={0} | all-to-all | bytes 262144 | tf_op jit(solution)/shard_map/all_to_all | solution.py:226
  70.0 11.0 %all_to_all.25.parts_ref = bf16[4,128,128]{2,1,0:T(8,128)(2,1)S(1)} all-to-all(bf16[4,128,128]{2,1,0:T(8,128)(2,1)S(1)} %shard_map.96), channel_id=1, replica_groups={{16,144,272,400},{48,176,304,432},{80,208,336,464},{112,240,368,496},{0..., dimensions={0} | all-to-all | bytes 262144 | tf_op jit(solution)/shard_map/all_to_all | solution.py:226
  81.0 0.0 copy-done.4
  81.0 0.0 copy-done.5
  81.0 0.0 copy-done.6
  81.0 0.0 copy-done.7
  81.0 0.0 copy-done.8
  81.0 1.2 %shard_map.97 = f32[16,16]{1,0:T(8,128)S(1)} custom-call(bf16[4,128,128]{2,1,0:T(8,128)(2,1)S(1)} %all_to_all.25.parts_ref, f32[128,128]{1,0:T(8,128)S(1)} %bitcast.18, f32[128,128]{1,0:T(8,128)S(1)} %bitcast.19, f32[1,128]{1,0:T(1,128)S(1)} %copy-done.7, f32[1,128]{1,0:T(1,128)S(1)} %copy-done.8, bf16[16,16384]{1,0:T(8,128)(2,1)S(1)} %bitcast.17), custom_call_target="tpu_custom_call" | custom-call | tf_op jit(solution)/shard_map/pallas_call | solution.py:159
  82.3 25.5 %all_to_all.26 = f32[16,1,16]{2,1,0:T(1,128)S(1)} all-to-all(f32[16,1,16]{2,1,0:T(1,128)S(1)} %bitcast.20), channel_id=1, replica_groups=mesh['y'=4,'zlo'=4,'core'=2,'zhi'=4,'x'=4] {'zhi','x'}, dimensions={0} | all-to-all | bytes 2048 | tf_op jit(solution)/shard_map/all_to_all | solution.py:237
  107.8 0.5 reduce_sum.9
  (3 shorter events, 0.1 us)
Async XLA Ops:
  1.7 21.0 %all-to-all-start = ((bf16[8,256,128]{2,1,0:T(8,128)(2,1)}), bf16[8,256,128]{2,1,0:T(8,128)(2,1)S(1)}, u32[]{:S(2)}, u32[]{:S(2)}) async-start(bf16[8,256,128]{2,1,0:T(8,128)(2,1)} %bitcast.21), calls=%async_computation | async-start | bytes 1048576 | tf_op jit(solution)/shard_map/all_to_all | solution.py:171
  10.7 1.6 %copy-start = (bf16[1,128,8192]{2,1,0:T(8,128)(2,1)S(1)}, bf16[1,128,8192]{2,1,0:T(8,128)(2,1)}, u32[]{:S(2)}) copy-start(bf16[1,128,8192]{2,1,0:T(8,128)(2,1)} %param.9) | copy-start | bytes 6291460
  12.3 1.6 %copy-start.2 = (bf16[1,128,8192]{2,1,0:T(8,128)(2,1)S(1)}, bf16[1,128,8192]{2,1,0:T(8,128)(2,1)}, u32[]{:S(2)}) copy-start(bf16[1,128,8192]{2,1,0:T(8,128)(2,1)} %param.10) | copy-start | bytes 6291460
  13.9 38.4 %copy-start.1 = (bf16[1,128,8192]{2,1,0:T(8,128)(2,1)S(1)}, bf16[1,128,8192]{2,1,0:T(8,128)(2,1)}, u32[]{:S(2)}) copy-start(bf16[1,128,8192]{2,1,0:T(8,128)(2,1)} %param.9) | copy-start | bytes 6291460
  15.9 36.3 %collective-permute-start = (bf16[128,8192]{1,0:T(8,128)(2,1)}, bf16[128,8192]{1,0:T(8,128)(2,1)}, u32[]{:S(2)}, u32[]{:S(2)}) collective-permute-start(bf16[128,8192]{1,0:T(8,128)(2,1)} %shard_map.91), channel_id=1, source_target_pairs={{0,16},{16,0},{1,17},{17,1},{2,18},{18,2},{3,19},{19,3},{4,20},{20... | collective-permute-start | bytes 6291464 | tf_op jit(solution)/shard_map/ppermute | solution.py:175
  22.8 14.3 %collective-permute-start.1 = (bf16[6,256,128]{2,1,0:T(8,128)(2,1)S(1)}, bf16[6,256,128]{2,1,0:T(8,128)(2,1)S(1)}, u32[]{:S(2)}, u32[]{:S(2)}) collective-permute-start(bf16[6,256,128]{2,1,0:T(8,128)(2,1)S(1)} %slice.8), channel_id=1, source_target_pairs={{0,128},{16,400},{128,256},{144,16},{256,384},{272,144},{384,0},{4... | collective-permute-start | bytes 1179656 | tf_op jit(solution)/shard_map/ppermute | solution.py:193
  24.7 31.8 %collective-permute-start.4 = (bf16[6,256,128]{2,1,0:T(8,128)(2,1)S(1)}, bf16[6,256,128]{2,1,0:T(8,128)(2,1)S(1)}, u32[]{:S(2)}, u32[]{:S(2)}) collective-permute-start(bf16[6,256,128]{2,1,0:T(8,128)(2,1)S(1)} %slice.8), channel_id=1, source_target_pairs={{0,384},{16,144},{128,0},{144,272},{256,128},{272,400},{384,256},{... | collective-permute-start | bytes 1179656 | tf_op jit(solution)/shard_map/ppermute | solution.py:193
  37.1 19.4 %collective-permute-start.5 = (bf16[6,256,128]{2,1,0:T(8,128)(2,1)S(1)}, bf16[6,256,128]{2,1,0:T(8,128)(2,1)S(1)}, u32[]{:S(2)}, u32[]{:S(2)}) collective-permute-start(bf16[6,256,128]{2,1,0:T(8,128)(2,1)S(1)} %collective-permute-done.1.refs_1_), channel_id=1, source_target_pairs={{0,128},{16,400},{128,256},{144,16},{256,384},{272,144},{384,0},{4... | collective-permute-start | bytes 1179656 | tf_op jit(solution)/shard_map/ppermute | solution.py:193
  39.0 7.6 %collective-permute-start.3 = (bf16[2,256,128]{2,1,0:T(8,128)(2,1)S(1)}, bf16[2,256,128]{2,1,0:T(8,128)(2,1)S(1)}, u32[]{:S(2)}, u32[]{:S(2)}) collective-permute-start(bf16[2,256,128]{2,1,0:T(8,128)(2,1)S(1)} %slice.9), channel_id=1, source_target_pairs={{0,384},{16,144},{128,0},{144,272},{256,128},{272,400},{384,256},{... | collective-permute-start | bytes 393224 | tf_op jit(solution)/shard_map/ppermute | solution.py:193
  44.2 8.1 %collective-permute-start.2 = (bf16[2,256,128]{2,1,0:T(8,128)(2,1)S(1)}, bf16[2,256,128]{2,1,0:T(8,128)(2,1)S(1)}, u32[]{:S(2)}, u32[]{:S(2)}) collective-permute-start(bf16[2,256,128]{2,1,0:T(8,128)(2,1)S(1)} %slice.9), channel_id=1, source_target_pairs={{0,128},{16,400},{128,256},{144,16},{256,384},{272,144},{384,0},{4... | collective-permute-start | bytes 393224 | tf_op jit(solution)/shard_map/ppermute | solution.py:193
  46.7 9.8 %collective-permute-start.6 = (bf16[2,256,128]{2,1,0:T(8,128)(2,1)S(1)}, bf16[2,256,128]{2,1,0:T(8,128)(2,1)S(1)}, u32[]{:S(2)}, u32[]{:S(2)}) collective-permute-start(bf16[2,256,128]{2,1,0:T(8,128)(2,1)S(1)} %collective-permute-done.3.refs_3_), channel_id=1, source_target_pairs={{0,384},{16,144},{128,0},{144,272},{256,128},{272,400},{384,256},{... | collective-permute-start | bytes 393224 | tf_op jit(solution)/shard_map/ppermute | solution.py:193
  52.3 1.6 %copy-start.3 = (bf16[1,128,8192]{2,1,0:T(8,128)(2,1)S(1)}, bf16[1,128,8192]{2,1,0:T(8,128)(2,1)}, u32[]{:S(2)}) copy-start(bf16[1,128,8192]{2,1,0:T(8,128)(2,1)} %param.10) | copy-start | bytes 6291460
  56.4 24.6 %copy-start.4 = (bf16[1,16,16384]{2,1,0:T(8,128)(2,1)S(1)}, bf16[1,16,16384]{2,1,0:T(8,128)(2,1)}, u32[]{:S(2)}) copy-start(bf16[1,16,16384]{2,1,0:T(8,128)(2,1)} %param.17) | copy-start | bytes 1572868
  56.4 24.6 %copy-start.5 = (f32[1,128,128]{2,1,0:T(8,128)S(1)}, f32[1,128,128]{2,1,0:T(8,128)}, u32[]{:S(2)}) copy-start(f32[1,128,128]{2,1,0:T(8,128)} %param.13) | copy-start | bytes 196612
  56.4 24.6 %copy-start.6 = (f32[1,128,128]{2,1,0:T(8,128)S(1)}, f32[1,128,128]{2,1,0:T(8,128)}, u32[]{:S(2)}) copy-start(f32[1,128,128]{2,1,0:T(8,128)} %param.14) | copy-start | bytes 196612
  56.4 24.6 %copy-start.7 = (f32[1,128]{1,0:T(1,128)S(1)}, f32[1,128]{1,0:T(1,128)}, u32[]{:S(2)}) copy-start(f32[1,128]{1,0:T(1,128)} %eig_a.1) | copy-start | bytes 1540
  56.5 24.6 %copy-start.8 = (f32[1,128]{1,0:T(1,128)S(1)}, f32[1,128]{1,0:T(1,128)}, u32[]{:S(2)}) copy-start(f32[1,128]{1,0:T(1,128)} %eig_g.1) | copy-start | bytes 1540
  57.1 3.1 %collective-permute-start.7 = (bf16[2,128,128]{2,1,0:T(8,128)(2,1)S(1)}, bf16[2,128,128]{2,1,0:T(8,128)(2,1)S(1)}, u32[]{:S(2)}, u32[]{:S(2)}) collective-permute-start(bf16[2,128,128]{2,1,0:T(8,128)(2,1)S(1)} %shard_map.94.mine_ref), channel_id=1, source_target_pairs={{0,16},{16,0},{1,17},{17,1},{2,18},{18,2},{3,19},{19,3},{4,20},{20... | collective-permute-start | bytes 196616 | tf_op jit(solution)/shard_map/ppermute | solution.py:175

commit v8 on v7

--- a/solution.py
+++ b/solution.py
@@ -138,16 +138,18 @@
     total = jnp.zeros((train_ref.shape[0], rank), F32)
     for i in range(rank):
         total = total + train_ref[:, i * rank:(i + 1) * rank].astype(F32) * precond[i:i + 1, :]
-    out[...] = dot(jnp.ones((out.shape[0], rank), F32), total, nt)
+    for k in range(out.shape[0]):
+        out[k] = dot(jnp.ones((1, rank), F32), total, nt)
 
 
 def body(acts, grads_out, proj_in, proj_out, basis_a, basis_g, eig_a, eig_g, train_grads):
     tokens = acts.shape[1] * lax.axis_size(CTX)
-    n_layer = lax.axis_size(LAYER)
+    n_zhi, n_x = lax.axis_size("zhi"), lax.axis_size("x")
+    n_train = train_grads.shape[1]
     n_y, n_z = lax.axis_size("y"), lax.axis_size("zlo")
     depth, rank = proj_in.shape[1:]
     line_blocks = 2 * n_z
-    part = 3 * line_blocks // 4
+    part = 5 * line_blocks // 8
     local, local_g = acts[0], grads_out[0]
     n_tok = local.shape[0]
     hbm = pl.BlockSpec(memory_space=pltpu.HBM)
@@ -215,26 +217,20 @@
         here, local, local_g, got, *near.values(), cost_estimate=cost,
     )
     mine = call(finish, shape(2, n_tok, rank), [VMEM] * (2 + len(last)), ahead, acc, *last)
-
-    def at(y, z, core):
-        return (y * n_z + z) * 2 + core
-
-    def exchange(x, core_along_y):
-        other = 1 - core_along_y
-        groups = [[at(y, z, core_along_y) for y in range(n_y)] for z in range(n_z)]
-        groups += [[at(y, z, other) for z in range(n_z)] for y in range(n_y)]
-        return lax.all_to_all(x, CTX, 0, 0, axis_index_groups=groups, tiled=True)
-
     grad = call(
         functools.partial(outer, float(tokens)), shape(n_y, rank, rank),
         [SMEM, VMEM, VMEM], here, mine, permute(mine, "core", 1),
     )
-    grad = call(add_up, shape(n_z, rank, rank), [VMEM], exchange(grad, 0))
+    grad = call(add_up, shape(n_z, rank, rank), [VMEM], all_to_all(grad, "y"))
     sent = call(
-        score, shape(n_layer, train_grads.shape[1], dtype=F32), [VMEM] * 6,
-        exchange(grad, 1), basis_a[0], basis_g[0], eig_a, eig_g, train_grads[0],
-    )
-    return jnp.sum(lax.all_to_all(sent, LAYER, 0, 0), 0)
+        score, shape(n_zhi, 1, n_train, dtype=F32), [VMEM] * 6,
+        all_to_all(grad, "zlo"), basis_a[0], basis_g[0], eig_a, eig_g, train_grads[0],
+    )
+    sent = call(
+        add_up, shape(n_x, 1, n_train, dtype=F32), [VMEM],
+        all_to_all(sent, "zhi"),
+    )
+    return jnp.sum(all_to_all(sent, "x"), (0, 1))
 
 
 def solution(mesh):

time: 109 us -> 111 us (1.018)
  blocking collectives: 45.5 us -> 50.4 us
  starting transfers between devices: 34.4 us -> 30.8 us
    all_to_all x3 -> x4, blocking collectives: 45.5 us -> 50.4 us  [all_to_all(): return lax.all_to_all(x, axis, 0, 0, tiled=True)]
    ppermute x6, starting transfers between devices: 21.6 us -> 17.9 us  [along_y(): return lax.ppermute(x, ('y', 'core'), moves)]
    ppermute x6, waiting for transfers between devices: 7.85 us -> 9 us  [along_y(): return lax.ppermute(x, ('y', 'core'), moves)]
    pallas_call x7 -> x8, Pallas kernels: 8.93 us -> 8.93 us  [call(): pl.pallas_call(kernel, out_shape=shape, in_specs=in_specs, compiler_param...]
where the time goes in v8:
time: 111 us
  blocking collectives  50.4 us (45%)
  starting transfers between devices  30.8 us (28%)
  waiting for transfers between devices  15 us (14%)
  Pallas kernels  8.93 us (8%)
  local copies, waits for them, and re-layouts  4.84 us (4%)
    all_to_all x4, blocking collectives, all_to_all(): return lax.all_to_all(x, axis, 0, 0, tiled=True)  50.4 us
    ppermute x6, starting transfers between devices, along_y(): return lax.ppermute(x, ('y', 'core'), moves)  17.9 us
    ppermute x6, waiting for transfers between devices, along_y(): return lax.ppermute(x, ('y', 'core'), moves)  9 us
    pallas_call x8, Pallas kernels, call(): pl.pallas_call(kernel, out_shape=shape, in_specs=in_specs, compiler_param...  8.93 us
    all_to_all x1, starting transfers between devices, all_to_all(): return lax.all_to_all(x, axis, 0, 0, tiled=True)  8.87 us
    unnamed x18, local copies, waits for them, and re-layouts  4.81 us
    all_to_all x1, waiting for transfers between devices, all_to_all(): return lax.all_to_all(x, axis, 0, 0, tiled=True)  4.78 us
    ppermute x2, starting transfers between devices, permute(): return lax.ppermute(x, axis, [(i, (i + step) % size) for i in range(size)])  3.95 us
  transfers between devices with their start and end apart: 9, of which 4 were waited for; matrix products, arithmetic and copies ran while one was open for 0% of the time, Pallas kernels for 4%

profile of v8, /device:TPU:32, one launch (start us, length us, event | category | flops | bytes accessed | tf_op | source)
XLA Modules:
  0.0 110.7 jit_solution(12670461250627886869)
XLA Ops:
  0.0 1.7 %shard_map.92 = bf16[4,2,256,128]{3,2,1,0:T(8,128)(2,1)} custom-call(bf16[256,128]{1,0:T(8,128)(2,1)} %bitcast.18, bf16[256,128]{1,0:T(8,128)(2,1)} %bitcast.19), custom_call_target="tpu_custom_call" | custom-call | tf_op jit(solution)/shard_map/pallas_call | solution.py:161
  1.7 8.9 %all-to-all-start = ((bf16[8,256,128]{2,1,0:T(8,128)(2,1)}), bf16[8,256,128]{2,1,0:T(8,128)(2,1)S(1)}, u32[]{:S(2)}, u32[]{:S(2)}) async-start(bf16[8,256,128]{2,1,0:T(8,128)(2,1)} %bitcast.17), calls=%async_computation | async-start | bytes 1048576 | tf_op jit(solution)/shard_map/all_to_all | solution.py:173
  10.6 0.1 pad_add_fusion.here_ref
  10.7 0.0 copy-start
  10.7 1.6 %copy-done = bf16[1,128,8192]{2,1,0:T(8,128)(2,1)S(1)} copy-done((bf16[1,128,8192]{2,1,0:T(8,128)(2,1)S(1)}, bf16[1,128,8192]{2,1,0:T(8,128)(2,1)}, u32[]{:S(2)}) %copy-start) | copy-done | bytes 2097176
  12.3 0.0 copy-start.2
  12.3 1.6 %copy-done.2 = bf16[1,128,8192]{2,1,0:T(8,128)(2,1)S(1)} copy-done((bf16[1,128,8192]{2,1,0:T(8,128)(2,1)S(1)}, bf16[1,128,8192]{2,1,0:T(8,128)(2,1)}, u32[]{:S(2)}) %copy-start.2) | copy-done | bytes 2097176
  13.9 0.0 copy-start.1
  13.9 2.0 %shard_map.91 = bf16[128,8192]{1,0:T(8,128)(2,1)} custom-call(s32[4]{0:T(128)S(1)} %pad_add_fusion.here_ref, bf16[128,8192]{1,0:T(8,128)(2,1)S(1)} %bitcast.10, bf16[128,8192]{1,0:T(8,128)(2,1)S(1)} %bitcast.12), custom_call_target="tpu_custom_call" | custom-call | tf_op jit(solution)/shard_map/pallas_call | solution.py:161
  15.9 2.0 %collective-permute-start = (bf16[128,8192]{1,0:T(8,128)(2,1)}, bf16[128,8192]{1,0:T(8,128)(2,1)}, u32[]{:S(2)}, u32[]{:S(2)}) collective-permute-start(bf16[128,8192]{1,0:T(8,128)(2,1)} %shard_map.91), channel_id=1, source_target_pairs={{0,16},{16,0},{1,17},{17,1},{2,18},{18,2},{3,19},{19,3},{4,20},{20... | collective-permute-start | bytes 6291464 | tf_op jit(solution)/shard_map/ppermute | solution.py:177
  18.0 4.8 %all-to-all-done.refs_0_ = bf16[8,256,128]{2,1,0:T(8,128)(2,1)S(1)} async-done(((bf16[8,256,128]{2,1,0:T(8,128)(2,1)}), bf16[8,256,128]{2,1,0:T(8,128)(2,1)S(1)}, u32[]{:S(2)}, u32[]{:S(2)}) %all-to-all-start) | async-done | bytes 524320 | tf_op jit(solution)/shard_map/all_to_all | solution.py:173
  22.8 1.9 %collective-permute-start.1 = (bf16[5,256,128]{2,1,0:T(8,128)(2,1)S(1)}, bf16[5,256,128]{2,1,0:T(8,128)(2,1)S(1)}, u32[]{:S(2)}, u32[]{:S(2)}) collective-permute-start(bf16[5,256,128]{2,1,0:T(8,128)(2,1)S(1)} %slice.8), channel_id=1, source_target_pairs={{0,128},{16,400},{128,256},{144,16},{256,384},{272,144},{384,0},{4... | collective-permute-start | bytes 983048 | tf_op jit(solution)/shard_map/ppermute | solution.py:195
  24.7 5.1 %collective-permute-start.3 = (bf16[3,256,128]{2,1,0:T(8,128)(2,1)S(1)}, bf16[3,256,128]{2,1,0:T(8,128)(2,1)S(1)}, u32[]{:S(2)}, u32[]{:S(2)}) collective-permute-start(bf16[3,256,128]{2,1,0:T(8,128)(2,1)S(1)} %slice.9), channel_id=1, source_target_pairs={{0,384},{16,144},{128,0},{144,272},{256,128},{272,400},{384,256},{... | collective-permute-start | bytes 589832 | tf_op jit(solution)/shard_map/ppermute | solution.py:195
  29.9 1.9 %collective-permute-start.4 = (bf16[5,256,128]{2,1,0:T(8,128)(2,1)S(1)}, bf16[5,256,128]{2,1,0:T(8,128)(2,1)S(1)}, u32[]{:S(2)}, u32[]{:S(2)}) collective-permute-start(bf16[5,256,128]{2,1,0:T(8,128)(2,1)S(1)} %slice.8), channel_id=1, source_target_pairs={{0,384},{16,144},{128,0},{144,272},{256,128},{272,400},{384,256},{... | collective-permute-start | bytes 983048 | tf_op jit(solution)/shard_map/ppermute | solution.py:195
  31.8 3.9 %collective-permute-done.1.refs_1_ = bf16[5,256,128]{2,1,0:T(8,128)(2,1)S(1)} collective-permute-done((bf16[5,256,128]{2,1,0:T(8,128)(2,1)S(1)}, bf16[5,256,128]{2,1,0:T(8,128)(2,1)S(1)}, u32[]{:S(2)}, u32[]{:S(2)}) %collective-permute-start.1) | collective-permute-done | bytes 327712 | tf_op jit(solution)/shard_map/ppermute | solution.py:195
  35.7 1.9 %collective-permute-start.5 = (bf16[5,256,128]{2,1,0:T(8,128)(2,1)S(1)}, bf16[5,256,128]{2,1,0:T(8,128)(2,1)S(1)}, u32[]{:S(2)}, u32[]{:S(2)}) collective-permute-start(bf16[5,256,128]{2,1,0:T(8,128)(2,1)S(1)} %collective-permute-done.1.refs_1_), channel_id=1, source_target_pairs={{0,128},{16,400},{128,256},{144,16},{256,384},{272,144},{384,0},{4... | collective-permute-start | bytes 983048 | tf_op jit(solution)/shard_map/ppermute | solution.py:195
  37.6 1.9 %collective-permute-start.2 = (bf16[3,256,128]{2,1,0:T(8,128)(2,1)S(1)}, bf16[3,256,128]{2,1,0:T(8,128)(2,1)S(1)}, u32[]{:S(2)}, u32[]{:S(2)}) collective-permute-start(bf16[3,256,128]{2,1,0:T(8,128)(2,1)S(1)} %slice.9), channel_id=1, source_target_pairs={{0,128},{16,400},{128,256},{144,16},{256,384},{272,144},{384,0},{4... | collective-permute-start | bytes 589832 | tf_op jit(solution)/shard_map/ppermute | solution.py:195
  39.5 0.0 collective-permute-done.3.refs_3_
  39.5 5.1 %collective-permute-start.6 = (bf16[3,256,128]{2,1,0:T(8,128)(2,1)S(1)}, bf16[3,256,128]{2,1,0:T(8,128)(2,1)S(1)}, u32[]{:S(2)}, u32[]{:S(2)}) collective-permute-start(bf16[3,256,128]{2,1,0:T(8,128)(2,1)S(1)} %collective-permute-done.3.refs_3_), channel_id=1, source_target_pairs={{0,384},{16,144},{128,0},{144,272},{256,128},{272,400},{384,256},{... | collective-permute-start | bytes 589832 | tf_op jit(solution)/shard_map/ppermute | solution.py:195
  44.7 5.1 %collective-permute-done.2.refs_2_ = bf16[3,256,128]{2,1,0:T(8,128)(2,1)S(1)} collective-permute-done((bf16[3,256,128]{2,1,0:T(8,128)(2,1)S(1)}, bf16[3,256,128]{2,1,0:T(8,128)(2,1)S(1)}, u32[]{:S(2)}, u32[]{:S(2)}) %collective-permute-start.2) | collective-permute-done | bytes 196640 | tf_op jit(solution)/shard_map/ppermute | solution.py:195
  49.8 0.0 collective-permute-done.got_ref
  49.8 0.0 copy-done.1
  49.8 0.0 copy-start.3
  49.8 1.6 %copy-done.3 = bf16[1,128,8192]{2,1,0:T(8,128)(2,1)S(1)} copy-done((bf16[1,128,8192]{2,1,0:T(8,128)(2,1)S(1)}, bf16[1,128,8192]{2,1,0:T(8,128)(2,1)}, u32[]{:S(2)}) %copy-start.3) | copy-done | bytes 2097176
  51.4 2.5 %shard_map.93 = (f32[2,128,128]{2,1,0:T(8,128)S(1)}, bf16[2,128,3328]{2,1,0:T(8,128)(2,1)S(1)}) custom-call(s32[4]{0:T(128)S(1)} %pad_add_fusion.here_ref, bf16[128,8192]{1,0:T(8,128)(2,1)S(1)} %bitcast.11, bf16[128,8192]{1,0:T(8,128)(2,1)S(1)} %bitcast.13, bf16[128,8192]{1,0:T(8,128)(2,1)} %collective-permute-done.got_ref, ...), custom_call_target="tpu_custom_call" | custom-call | flops 335544320 | bytes 6291456 | tf_op jit(solution)/shard_map/pallas_call | solution.py:161
  53.9 0.0 copy-start.4
  54.0 0.0 copy-start.5
  54.0 0.0 copy-start.6
  54.0 0.0 copy-start.7
  54.0 0.0 copy-start.8
  54.0 0.0 collective-permute-done.4.refs_0_
  54.0 0.0 collective-permute-done.6.refs_2_
  54.0 0.0 collective-permute-done.5.refs_1_
  54.0 0.6 shard_map.94.mine_ref
  54.6 1.9 %collective-permute-start.7 = (bf16[2,128,128]{2,1,0:T(8,128)(2,1)S(1)}, bf16[2,128,128]{2,1,0:T(8,128)(2,1)S(1)}, u32[]{:S(2)}, u32[]{:S(2)}) collective-permute-start(bf16[2,128,128]{2,1,0:T(8,128)(2,1)S(1)} %shard_map.94.mine_ref), channel_id=1, source_target_pairs={{0,16},{16,0},{1,17},{17,1},{2,18},{18,2},{3,19},{19,3},{4,20},{20... | collective-permute-start | bytes 196616 | tf_op jit(solution)/shard_map/ppermute | solution.py:177
  56.6 1.2 %collective-permute-done.7.got_ref = bf16[2,128,128]{2,1,0:T(8,128)(2,1)S(1)} collective-permute-done((bf16[2,128,128]{2,1,0:T(8,128)(2,1)S(1)}, bf16[2,128,128]{2,1,0:T(8,128)(2,1)S(1)}, u32[]{:S(2)}, u32[]{:S(2)}) %collective-permute-start.7) | collective-permute-done | bytes 65568 | tf_op jit(solution)/shard_map/ppermute | solution.py:177
  57.8 0.7 shard_map.95
  58.5 8.4 %all_to_all.25.parts_ref = bf16[4,128,128]{2,1,0:T(8,128)(2,1)S(1)} all-to-all(bf16[4,128,128]{2,1,0:T(8,128)(2,1)S(1)} %shard_map.95), channel_id=1, replica_groups=mesh['y'=4,'zlo'=4,'core'=2,'zhi'=4,'x'=4] {'y'}, dimensions={0} | all-to-all | bytes 262144 | tf_op jit(solution)/shard_map/all_to_all | solution.py:173
  66.9 10.7 %all_to_all.26.parts_ref = bf16[4,128,128]{2,1,0:T(8,128)(2,1)S(1)} all-to-all(bf16[4,128,128]{2,1,0:T(8,128)(2,1)S(1)} %shard_map.96), channel_id=1, replica_groups=mesh['y'=4,'zlo'=4,'core'=2,'zhi'=4,'x'=4] {'zlo'}, dimensions={0} | all-to-all | bytes 262144 | tf_op jit(solution)/shard_map/all_to_all | solution.py:173
  77.6 0.0 copy-done.4
  77.6 0.0 copy-done.5
  77.6 0.0 copy-done.6
  77.6 0.0 copy-done.7
  77.7 0.0 copy-done.8
  77.7 1.2 %shard_map.97 = f32[4,1,16]{2,1,0:T(1,128)S(1)} custom-call(bf16[4,128,128]{2,1,0:T(8,128)(2,1)S(1)} %all_to_all.26.parts_ref, f32[128,128]{1,0:T(8,128)S(1)} %bitcast.15, f32[128,128]{1,0:T(8,128)S(1)} %bitcast.16, f32[1,128]{1,0:T(1,128)S(1)} %copy-done.7, f32[1,128]{1,0:T(1,128)S(1)} %copy-done.8, bf16[16,16384]{1,0:T(8,128)(2,1)S(1)} %bitcast.14), custom_call_target="tpu_custom_call" | custom-call | tf_op jit(solution)/shard_map/pallas_call | solution.py:161
  78.9 21.9 %all_to_all.27.parts_ref = f32[4,1,16]{2,1,0:T(1,128)S(1)} all-to-all(f32[4,1,16]{2,1,0:T(1,128)S(1)} %shard_map.97), channel_id=1, replica_groups=mesh['y'=4,'zlo'=4,'core'=2,'zhi'=4,'x'=4] {'zhi'}, dimensions={0} | all-to-all | bytes 512 | tf_op jit(solution)/shard_map/all_to_all | solution.py:173
  100.8 9.4 %all_to_all.28 = f32[4,1,16]{2,1,0:T(1,128)S(1)} all-to-all(f32[4,1,16]{2,1,0:T(1,128)S(1)} %shard_map.98), channel_id=1, replica_groups=mesh['y'=4,'zlo'=4,'core'=2,'zhi'=4,'x'=4] {'x'}, dimensions={0} | all-to-all | bytes 512 | tf_op jit(solution)/shard_map/all_to_all | solution.py:173
  110.2 0.5 reduce_sum.9
  (4 shorter events, 0.1 us)
Async XLA Ops:
  1.7 21.0 %all-to-all-start = ((bf16[8,256,128]{2,1,0:T(8,128)(2,1)}), bf16[8,256,128]{2,1,0:T(8,128)(2,1)S(1)}, u32[]{:S(2)}, u32[]{:S(2)}) async-start(bf16[8,256,128]{2,1,0:T(8,128)(2,1)} %bitcast.17), calls=%async_computation | async-start | bytes 1048576 | tf_op jit(solution)/shard_map/all_to_all | solution.py:173
  10.7 1.6 %copy-start = (bf16[1,128,8192]{2,1,0:T(8,128)(2,1)S(1)}, bf16[1,128,8192]{2,1,0:T(8,128)(2,1)}, u32[]{:S(2)}) copy-start(bf16[1,128,8192]{2,1,0:T(8,128)(2,1)} %param.9) | copy-start | bytes 6291460
  12.3 1.6 %copy-start.2 = (bf16[1,128,8192]{2,1,0:T(8,128)(2,1)S(1)}, bf16[1,128,8192]{2,1,0:T(8,128)(2,1)}, u32[]{:S(2)}) copy-start(bf16[1,128,8192]{2,1,0:T(8,128)(2,1)} %param.10) | copy-start | bytes 6291460
  13.9 35.9 %copy-start.1 = (bf16[1,128,8192]{2,1,0:T(8,128)(2,1)S(1)}, bf16[1,128,8192]{2,1,0:T(8,128)(2,1)}, u32[]{:S(2)}) copy-start(bf16[1,128,8192]{2,1,0:T(8,128)(2,1)} %param.9) | copy-start | bytes 6291460
  15.9 33.9 %collective-permute-start = (bf16[128,8192]{1,0:T(8,128)(2,1)}, bf16[128,8192]{1,0:T(8,128)(2,1)}, u32[]{:S(2)}, u32[]{:S(2)}) collective-permute-start(bf16[128,8192]{1,0:T(8,128)(2,1)} %shard_map.91), channel_id=1, source_target_pairs={{0,16},{16,0},{1,17},{17,1},{2,18},{18,2},{3,19},{19,3},{4,20},{20... | collective-permute-start | bytes 6291464 | tf_op jit(solution)/shard_map/ppermute | solution.py:177
  22.8 12.9 %collective-permute-start.1 = (bf16[5,256,128]{2,1,0:T(8,128)(2,1)S(1)}, bf16[5,256,128]{2,1,0:T(8,128)(2,1)S(1)}, u32[]{:S(2)}, u32[]{:S(2)}) collective-permute-start(bf16[5,256,128]{2,1,0:T(8,128)(2,1)S(1)} %slice.8), channel_id=1, source_target_pairs={{0,128},{16,400},{128,256},{144,16},{256,384},{272,144},{384,0},{4... | collective-permute-start | bytes 983048 | tf_op jit(solution)/shard_map/ppermute | solution.py:195
  24.7 14.8 %collective-permute-start.3 = (bf16[3,256,128]{2,1,0:T(8,128)(2,1)S(1)}, bf16[3,256,128]{2,1,0:T(8,128)(2,1)S(1)}, u32[]{:S(2)}, u32[]{:S(2)}) collective-permute-start(bf16[3,256,128]{2,1,0:T(8,128)(2,1)S(1)} %slice.9), channel_id=1, source_target_pairs={{0,384},{16,144},{128,0},{144,272},{256,128},{272,400},{384,256},{... | collective-permute-start | bytes 589832 | tf_op jit(solution)/shard_map/ppermute | solution.py:195
  29.9 24.1 %collective-permute-start.4 = (bf16[5,256,128]{2,1,0:T(8,128)(2,1)S(1)}, bf16[5,256,128]{2,1,0:T(8,128)(2,1)S(1)}, u32[]{:S(2)}, u32[]{:S(2)}) collective-permute-start(bf16[5,256,128]{2,1,0:T(8,128)(2,1)S(1)} %slice.8), channel_id=1, source_target_pairs={{0,384},{16,144},{128,0},{144,272},{256,128},{272,400},{384,256},{... | collective-permute-start | bytes 983048 | tf_op jit(solution)/shard_map/ppermute | solution.py:195
  35.7 18.3 %collective-permute-start.5 = (bf16[5,256,128]{2,1,0:T(8,128)(2,1)S(1)}, bf16[5,256,128]{2,1,0:T(8,128)(2,1)S(1)}, u32[]{:S(2)}, u32[]{:S(2)}) collective-permute-start(bf16[5,256,128]{2,1,0:T(8,128)(2,1)S(1)} %collective-permute-done.1.refs_1_), channel_id=1, source_target_pairs={{0,128},{16,400},{128,256},{144,16},{256,384},{272,144},{384,0},{4... | collective-permute-start | bytes 983048 | tf_op jit(solution)/shard_map/ppermute | solution.py:195
  37.6 12.2 %collective-permute-start.2 = (bf16[3,256,128]{2,1,0:T(8,128)(2,1)S(1)}, bf16[3,256,128]{2,1,0:T(8,128)(2,1)S(1)}, u32[]{:S(2)}, u32[]{:S(2)}) collective-permute-start(bf16[3,256,128]{2,1,0:T(8,128)(2,1)S(1)} %slice.9), channel_id=1, source_target_pairs={{0,128},{16,400},{128,256},{144,16},{256,384},{272,144},{384,0},{4... | collective-permute-start | bytes 589832 | tf_op jit(solution)/shard_map/ppermute | solution.py:195
  39.5 14.5 %collective-permute-start.6 = (bf16[3,256,128]{2,1,0:T(8,128)(2,1)S(1)}, bf16[3,256,128]{2,1,0:T(8,128)(2,1)S(1)}, u32[]{:S(2)}, u32[]{:S(2)}) collective-permute-start(bf16[3,256,128]{2,1,0:T(8,128)(2,1)S(1)} %collective-permute-done.3.refs_3_), channel_id=1, source_target_pairs={{0,384},{16,144},{128,0},{144,272},{256,128},{272,400},{384,256},{... | collective-permute-start | bytes 589832 | tf_op jit(solution)/shard_map/ppermute | solution.py:195
  49.8 1.6 %copy-start.3 = (bf16[1,128,8192]{2,1,0:T(8,128)(2,1)S(1)}, bf16[1,128,8192]{2,1,0:T(8,128)(2,1)}, u32[]{:S(2)}) copy-start(bf16[1,128,8192]{2,1,0:T(8,128)(2,1)} %param.10) | copy-start | bytes 6291460
  53.9 23.7 %copy-start.4 = (bf16[1,16,16384]{2,1,0:T(8,128)(2,1)S(1)}, bf16[1,16,16384]{2,1,0:T(8,128)(2,1)}, u32[]{:S(2)}) copy-start(bf16[1,16,16384]{2,1,0:T(8,128)(2,1)} %param.17) | copy-start | bytes 1572868
  54.0 23.7 %copy-start.5 = (f32[1,128,128]{2,1,0:T(8,128)S(1)}, f32[1,128,128]{2,1,0:T(8,128)}, u32[]{:S(2)}) copy-start(f32[1,128,128]{2,1,0:T(8,128)} %param.13) | copy-start | bytes 196612
  54.0 23.7 %copy-start.6 = (f32[1,128,128]{2,1,0:T(8,128)S(1)}, f32[1,128,128]{2,1,0:T(8,128)}, u32[]{:S(2)}) copy-start(f32[1,128,128]{2,1,0:T(8,128)} %param.14) | copy-start | bytes 196612
  54.0 23.7 %copy-start.7 = (f32[1,128]{1,0:T(1,128)S(1)}, f32[1,128]{1,0:T(1,128)}, u32[]{:S(2)}) copy-start(f32[1,128]{1,0:T(1,128)} %eig_a.1) | copy-start | bytes 1540
  54.0 23.7 %copy-start.8 = (f32[1,128]{1,0:T(1,128)S(1)}, f32[1,128]{1,0:T(1,128)}, u32[]{:S(2)}) copy-start(f32[1,128]{1,0:T(1,128)} %eig_g.1) | copy-start | bytes 1540
  54.6 3.1 %collective-permute-start.7 = (bf16[2,128,128]{2,1,0:T(8,128)(2,1)S(1)}, bf16[2,128,128]{2,1,0:T(8,128)(2,1)S(1)}, u32[]{:S(2)}, u32[]{:S(2)}) collective-permute-start(bf16[2,128,128]{2,1,0:T(8,128)(2,1)S(1)} %shard_map.94.mine_ref), channel_id=1, source_target_pairs={{0,16},{16,0},{1,17},{17,1},{2,18},{18,2},{3,19},{19,3},{4,20},{20... | collective-permute-start | bytes 196616 | tf_op jit(solution)/shard_map/ppermute | solution.py:177

commit v9 on v7

--- a/solution.py
+++ b/solution.py
@@ -95,7 +95,8 @@
 
 def outer(tokens, here_ref, mine_ref, got_ref, out):
     even = here_ref[1] == 0
-    total = jnp.zeros(out.shape[1:], F32)
+    rank = out.shape[2]
+    total = jnp.zeros((rank, rank), F32)
     for k in range(2):
         mine, got = mine_ref[k].astype(F32), got_ref[1 - k].astype(F32)
         proj_g = jnp.where(even, got, mine).astype(BF16)
@@ -104,23 +105,22 @@
             proj_g, proj_a, (((0,), (0,)), ((), ())), preferred_element_type=F32
         )
     total = (total / tokens).astype(out.dtype)
+    half = jnp.where(even, total[:out.shape[1]], total[out.shape[1]:])
     for k in range(out.shape[0]):
-        out[k] = total
+        out[k] = half
 
 
 def add_up(parts_ref, out):
     total = parts_ref[0].astype(F32)
     for k in range(1, parts_ref.shape[0]):
         total = total + parts_ref[k].astype(F32)
-    total = total.astype(out.dtype)
-    for k in range(out.shape[0]):
-        out[k] = total
-
-
-def score(parts_ref, basis_a, basis_g, eig_a, eig_g, train_ref, out):
-    grad = parts_ref[0].astype(F32)
-    for k in range(1, parts_ref.shape[0]):
-        grad = grad + parts_ref[k].astype(F32)
+    out[...] = total
+
+
+def score(here_ref, mine_ref, got_ref, basis_a, basis_g, eig_a, eig_g, train_ref, out):
+    even = here_ref[1] == 0
+    mine, got = mine_ref[...], got_ref[...]
+    grad = jnp.concatenate([jnp.where(even, mine, got), jnp.where(even, got, mine)], 0)
     rot_a, rot_g = basis_a[...], basis_g[...]
     dot = functools.partial(
         lax.dot_general, precision=HIGHEST, preferred_element_type=F32
@@ -147,7 +147,7 @@
     n_y, n_z = lax.axis_size("y"), lax.axis_size("zlo")
     depth, rank = proj_in.shape[1:]
     line_blocks = 2 * n_z
-    part = 3 * line_blocks // 4
+    part = 5 * line_blocks // 8
     local, local_g = acts[0], grads_out[0]
     n_tok = local.shape[0]
     hbm = pl.BlockSpec(memory_space=pltpu.HBM)
@@ -215,24 +215,18 @@
         here, local, local_g, got, *near.values(), cost_estimate=cost,
     )
     mine = call(finish, shape(2, n_tok, rank), [VMEM] * (2 + len(last)), ahead, acc, *last)
-
-    def at(y, z, core):
-        return (y * n_z + z) * 2 + core
-
-    def exchange(x, core_along_y):
-        other = 1 - core_along_y
-        groups = [[at(y, z, core_along_y) for y in range(n_y)] for z in range(n_z)]
-        groups += [[at(y, z, other) for z in range(n_z)] for y in range(n_y)]
-        return lax.all_to_all(x, CTX, 0, 0, axis_index_groups=groups, tiled=True)
-
-    grad = call(
-        functools.partial(outer, float(tokens)), shape(n_y, rank, rank),
+    parts = call(
+        functools.partial(outer, float(tokens)), shape(n_y * n_z, rank // 2, rank),
         [SMEM, VMEM, VMEM], here, mine, permute(mine, "core", 1),
     )
-    grad = call(add_up, shape(n_z, rank, rank), [VMEM], exchange(grad, 0))
+    rows = call(
+        add_up, shape(rank // 2, rank, dtype=F32), [VMEM],
+        all_to_all(parts, ("y", "zlo")),
+    )
     sent = call(
-        score, shape(n_layer, train_grads.shape[1], dtype=F32), [VMEM] * 6,
-        exchange(grad, 1), basis_a[0], basis_g[0], eig_a, eig_g, train_grads[0],
+        score, shape(n_layer, train_grads.shape[1], dtype=F32), [SMEM] + [VMEM] * 7,
+        here, rows, permute(rows, "core", 1),
+        basis_a[0], basis_g[0], eig_a, eig_g, train_grads[0],
     )
     return jnp.sum(lax.all_to_all(sent, LAYER, 0, 0), 0)
 

time: 109 us -> 108 us (level)
  the two profiles are of different devices: /device:TPU:32 before, /device:TPU:1 now
where the time goes in v9:
time: 108 us
  starting transfers between devices  39.8 us (37%)
  blocking collectives  37.9 us (35%)
  waiting for transfers between devices  14.6 us (14%)
  Pallas kernels  9.52 us (9%)
  local copies, waits for them, and re-layouts  4.84 us (4%)
    all_to_all x1, blocking collectives, body(): return jnp.sum(lax.all_to_all(sent, LAYER, 0, 0), 0)  25.4 us
    ppermute x6, starting transfers between devices, along_y(): return lax.ppermute(x, ('y', 'core'), moves)  16.1 us
    ppermute x3, starting transfers between devices, permute(): return lax.ppermute(x, axis, [(i, (i + step) % size) for i in range(size)])  13.5 us
    all_to_all x1, blocking collectives, all_to_all(): return lax.all_to_all(x, axis, 0, 0, tiled=True)  12.5 us
    all_to_all x1, starting transfers between devices, all_to_all(): return lax.all_to_all(x, axis, 0, 0, tiled=True)  10.2 us
    pallas_call x7, Pallas kernels, call(): pl.pallas_call(kernel, out_shape=shape, in_specs=in_specs, compiler_param...  9.52 us
    all_to_all x1, waiting for transfers between devices, all_to_all(): return lax.all_to_all(x, axis, 0, 0, tiled=True)  7.05 us
    ppermute x6, waiting for transfers between devices, along_y(): return lax.ppermute(x, ('y', 'core'), moves)  5.82 us
  transfers between devices with their start and end apart: 10, of which 5 were waited for; matrix products, arithmetic and copies ran while one was open for 0% of the time, Pallas kernels for 4%

profile of v9, /device:TPU:1, one launch (start us, length us, event | category | flops | bytes accessed | tf_op | source)
XLA Modules:
  0.0 107.5 jit_solution(16253186003573878110)
XLA Ops:
  0.0 1.7 %shard_map.92 = bf16[4,2,256,128]{3,2,1,0:T(8,128)(2,1)} custom-call(bf16[256,128]{1,0:T(8,128)(2,1)} %bitcast.22, bf16[256,128]{1,0:T(8,128)(2,1)} %bitcast.23), custom_call_target="tpu_custom_call" | custom-call | tf_op jit(solution)/shard_map/pallas_call | solution.py:159
  1.8 10.2 %all-to-all-start = ((bf16[8,256,128]{2,1,0:T(8,128)(2,1)}), bf16[8,256,128]{2,1,0:T(8,128)(2,1)S(1)}, u32[]{:S(2)}, u32[]{:S(2)}) async-start(bf16[8,256,128]{2,1,0:T(8,128)(2,1)} %bitcast.21), calls=%async_computation | async-start | bytes 1048576 | tf_op jit(solution)/shard_map/all_to_all | solution.py:171
  12.0 0.1 pad_add_fusion.here_ref
  12.1 0.0 copy-start
  12.1 1.6 %copy-done = bf16[1,128,8192]{2,1,0:T(8,128)(2,1)S(1)} copy-done((bf16[1,128,8192]{2,1,0:T(8,128)(2,1)S(1)}, bf16[1,128,8192]{2,1,0:T(8,128)(2,1)}, u32[]{:S(2)}) %copy-start) | copy-done | bytes 2097176
  13.7 0.0 copy-start.2
  13.7 1.6 %copy-done.2 = bf16[1,128,8192]{2,1,0:T(8,128)(2,1)S(1)} copy-done((bf16[1,128,8192]{2,1,0:T(8,128)(2,1)S(1)}, bf16[1,128,8192]{2,1,0:T(8,128)(2,1)}, u32[]{:S(2)}) %copy-start.2) | copy-done | bytes 2097176
  15.3 0.0 copy-start.1
  15.3 2.0 %shard_map.91 = bf16[128,8192]{1,0:T(8,128)(2,1)} custom-call(s32[4]{0:T(128)S(1)} %pad_add_fusion.here_ref, bf16[128,8192]{1,0:T(8,128)(2,1)S(1)} %bitcast.13, bf16[128,8192]{1,0:T(8,128)(2,1)S(1)} %bitcast.15), custom_call_target="tpu_custom_call" | custom-call | tf_op jit(solution)/shard_map/pallas_call | solution.py:159
  17.3 2.0 %collective-permute-start = (bf16[128,8192]{1,0:T(8,128)(2,1)}, bf16[128,8192]{1,0:T(8,128)(2,1)}, u32[]{:S(2)}, u32[]{:S(2)}) collective-permute-start(bf16[128,8192]{1,0:T(8,128)(2,1)} %shard_map.91), channel_id=1, source_target_pairs={{0,16},{16,0},{1,17},{17,1},{2,18},{18,2},{3,19},{19,3},{4,20},{20... | collective-permute-start | bytes 6291464 | tf_op jit(solution)/shard_map/ppermute | solution.py:175
  19.3 7.0 %all-to-all-done.refs_0_ = bf16[8,256,128]{2,1,0:T(8,128)(2,1)S(1)} async-done(((bf16[8,256,128]{2,1,0:T(8,128)(2,1)}), bf16[8,256,128]{2,1,0:T(8,128)(2,1)S(1)}, u32[]{:S(2)}, u32[]{:S(2)}) %all-to-all-start) | async-done | bytes 524320 | tf_op jit(solution)/shard_map/all_to_all | solution.py:171
  26.4 1.9 %collective-permute-start.1 = (bf16[5,256,128]{2,1,0:T(8,128)(2,1)S(1)}, bf16[5,256,128]{2,1,0:T(8,128)(2,1)S(1)}, u32[]{:S(2)}, u32[]{:S(2)}) collective-permute-start(bf16[5,256,128]{2,1,0:T(8,128)(2,1)S(1)} %slice.8), channel_id=1, source_target_pairs={{0,128},{16,400},{128,256},{144,16},{256,384},{272,144},{384,0},{4... | collective-permute-start | bytes 983048 | tf_op jit(solution)/shard_map/ppermute | solution.py:193
  28.4 3.4 %collective-permute-start.3 = (bf16[3,256,128]{2,1,0:T(8,128)(2,1)S(1)}, bf16[3,256,128]{2,1,0:T(8,128)(2,1)S(1)}, u32[]{:S(2)}, u32[]{:S(2)}) collective-permute-start(bf16[3,256,128]{2,1,0:T(8,128)(2,1)S(1)} %slice.9), channel_id=1, source_target_pairs={{0,384},{16,144},{128,0},{144,272},{256,128},{272,400},{384,256},{... | collective-permute-start | bytes 589832 | tf_op jit(solution)/shard_map/ppermute | solution.py:193
  31.7 1.9 %collective-permute-start.4 = (bf16[5,256,128]{2,1,0:T(8,128)(2,1)S(1)}, bf16[5,256,128]{2,1,0:T(8,128)(2,1)S(1)}, u32[]{:S(2)}, u32[]{:S(2)}) collective-permute-start(bf16[5,256,128]{2,1,0:T(8,128)(2,1)S(1)} %slice.8), channel_id=1, source_target_pairs={{0,384},{16,144},{128,0},{144,272},{256,128},{272,400},{384,256},{... | collective-permute-start | bytes 983048 | tf_op jit(solution)/shard_map/ppermute | solution.py:193
  33.7 1.0 collective-permute-done.1.refs_1_
  34.7 3.6 %collective-permute-start.5 = (bf16[5,256,128]{2,1,0:T(8,128)(2,1)S(1)}, bf16[5,256,128]{2,1,0:T(8,128)(2,1)S(1)}, u32[]{:S(2)}, u32[]{:S(2)}) collective-permute-start(bf16[5,256,128]{2,1,0:T(8,128)(2,1)S(1)} %collective-permute-done.1.refs_1_), channel_id=1, source_target_pairs={{0,128},{16,400},{128,256},{144,16},{256,384},{272,144},{384,0},{4... | collective-permute-start | bytes 983048 | tf_op jit(solution)/shard_map/ppermute | solution.py:193
  38.3 1.9 %collective-permute-start.2 = (bf16[3,256,128]{2,1,0:T(8,128)(2,1)S(1)}, bf16[3,256,128]{2,1,0:T(8,128)(2,1)S(1)}, u32[]{:S(2)}, u32[]{:S(2)}) collective-permute-start(bf16[3,256,128]{2,1,0:T(8,128)(2,1)S(1)} %slice.9), channel_id=1, source_target_pairs={{0,128},{16,400},{128,256},{144,16},{256,384},{272,144},{384,0},{4... | collective-permute-start | bytes 589832 | tf_op jit(solution)/shard_map/ppermute | solution.py:193
  40.2 0.0 collective-permute-done.3.refs_3_
  40.2 3.4 %collective-permute-start.6 = (bf16[3,256,128]{2,1,0:T(8,128)(2,1)S(1)}, bf16[3,256,128]{2,1,0:T(8,128)(2,1)S(1)}, u32[]{:S(2)}, u32[]{:S(2)}) collective-permute-start(bf16[3,256,128]{2,1,0:T(8,128)(2,1)S(1)} %collective-permute-done.3.refs_3_), channel_id=1, source_target_pairs={{0,384},{16,144},{128,0},{144,272},{256,128},{272,400},{384,256},{... | collective-permute-start | bytes 589832 | tf_op jit(solution)/shard_map/ppermute | solution.py:193
  43.6 4.8 %collective-permute-done.2.refs_2_ = bf16[3,256,128]{2,1,0:T(8,128)(2,1)S(1)} collective-permute-done((bf16[3,256,128]{2,1,0:T(8,128)(2,1)S(1)}, bf16[3,256,128]{2,1,0:T(8,128)(2,1)S(1)}, u32[]{:S(2)}, u32[]{:S(2)}) %collective-permute-start.2) | collective-permute-done | bytes 196640 | tf_op jit(solution)/shard_map/ppermute | solution.py:193
  48.4 0.0 collective-permute-done.got_ref
  48.4 0.0 copy-done.1
  48.4 0.0 copy-start.3
  48.4 1.6 %copy-done.3 = bf16[1,128,8192]{2,1,0:T(8,128)(2,1)S(1)} copy-done((bf16[1,128,8192]{2,1,0:T(8,128)(2,1)S(1)}, bf16[1,128,8192]{2,1,0:T(8,128)(2,1)}, u32[]{:S(2)}) %copy-start.3) | copy-done | bytes 2097176
  50.0 2.5 %shard_map.93 = (f32[2,128,128]{2,1,0:T(8,128)S(1)}, bf16[2,128,3328]{2,1,0:T(8,128)(2,1)S(1)}) custom-call(s32[4]{0:T(128)S(1)} %pad_add_fusion.here_ref, bf16[128,8192]{1,0:T(8,128)(2,1)S(1)} %bitcast.14, bf16[128,8192]{1,0:T(8,128)(2,1)S(1)} %bitcast.16, bf16[128,8192]{1,0:T(8,128)(2,1)} %collective-permute-done.got_ref, ...), custom_call_target="tpu_custom_call" | custom-call | flops 335544320 | bytes 6291456 | tf_op jit(solution)/shard_map/pallas_call | solution.py:159
  52.5 0.0 copy-start.4
  52.5 0.0 copy-start.5
  52.6 0.0 copy-start.6
  52.6 0.0 copy-start.7
  52.6 0.0 copy-start.8
  52.6 0.0 collective-permute-done.4.refs_0_
  52.6 0.0 collective-permute-done.6.refs_2_
  52.6 0.0 collective-permute-done.5.refs_1_
  52.6 0.6 shard_map.94.mine_ref
  53.2 7.7 %collective-permute-start.7 = (bf16[2,128,128]{2,1,0:T(8,128)(2,1)S(1)}, bf16[2,128,128]{2,1,0:T(8,128)(2,1)S(1)}, u32[]{:S(2)}, u32[]{:S(2)}) collective-permute-start(bf16[2,128,128]{2,1,0:T(8,128)(2,1)S(1)} %shard_map.94.mine_ref), channel_id=1, source_target_pairs={{0,16},{16,0},{1,17},{17,1},{2,18},{18,2},{3,19},{19,3},{4,20},{20... | collective-permute-start | bytes 196616 | tf_op jit(solution)/shard_map/ppermute | solution.py:175
  60.9 0.9 collective-permute-done.7.got_ref
  61.8 0.8 shard_map.95
  62.6 12.5 %all_to_all.19.parts_ref = bf16[16,64,128]{2,1,0:T(8,128)(2,1)S(1)} all-to-all(bf16[16,64,128]{2,1,0:T(8,128)(2,1)S(1)} %shard_map.95), channel_id=1, replica_groups=mesh['y'=4,'zlo'=4,'core'=2,'zhi'=4,'x'=4] {'y','zlo'}, dimensions={0} | all-to-all | bytes 524288 | tf_op jit(solution)/shard_map/all_to_all | solution.py:171
  75.1 3.8 %collective-permute-start.8 = (f32[64,128]{1,0:T(8,128)S(1)}, f32[64,128]{1,0:T(8,128)S(1)}, u32[]{:S(2)}, u32[]{:S(2)}) collective-permute-start(f32[64,128]{1,0:T(8,128)S(1)} %shard_map.96.mine_ref), channel_id=1, source_target_pairs={{0,16},{16,0},{1,17},{17,1},{2,18},{18,2},{3,19},{19,3},{4,20},{20... | collective-permute-start | bytes 98312 | tf_op jit(solution)/shard_map/ppermute | solution.py:175
  79.0 0.8 collective-permute-done.8.got_ref
  79.8 0.0 copy-done.4
  79.8 0.0 copy-done.5
  79.8 0.0 copy-done.6
  79.8 0.0 copy-done.7
  79.8 0.0 copy-done.8
  79.8 1.8 %shard_map.97 = f32[16,16]{1,0:T(8,128)S(1)} custom-call(s32[4]{0:T(128)S(1)} %pad_add_fusion.here_ref, f32[64,128]{1,0:T(8,128)S(1)} %shard_map.96.mine_ref, f32[64,128]{1,0:T(8,128)S(1)} %collective-permute-done.8.got_ref, f32[128,128]{1,0:T(8,128)S(1)} %bitcast.18, f32[128,128]{1,0:T(8,128)S(1)} %bitcast.19, f32[1,128]{1,0:T(1,128)S(1)} %copy-done.7, ...), custom_call_target="tpu_custom_call" | custom-call | tf_op jit(solution)/shard_map/pallas_call | solution.py:159
  81.6 25.4 %all_to_all.20 = f32[16,1,16]{2,1,0:T(1,128)S(1)} all-to-all(f32[16,1,16]{2,1,0:T(1,128)S(1)} %bitcast.20), channel_id=1, replica_groups=mesh['y'=4,'zlo'=4,'core'=2,'zhi'=4,'x'=4] {'zhi','x'}, dimensions={0} | all-to-all | bytes 2048 | tf_op jit(solution)/shard_map/all_to_all | solution.py:231
  107.0 0.5 reduce_sum.9
  (3 shorter events, 0.1 us)
Async XLA Ops:
  1.8 24.6 %all-to-all-start = ((bf16[8,256,128]{2,1,0:T(8,128)(2,1)}), bf16[8,256,128]{2,1,0:T(8,128)(2,1)S(1)}, u32[]{:S(2)}, u32[]{:S(2)}) async-start(bf16[8,256,128]{2,1,0:T(8,128)(2,1)} %bitcast.21), calls=%async_computation | async-start | bytes 1048576 | tf_op jit(solution)/shard_map/all_to_all | solution.py:171
  12.1 1.6 %copy-start = (bf16[1,128,8192]{2,1,0:T(8,128)(2,1)S(1)}, bf16[1,128,8192]{2,1,0:T(8,128)(2,1)}, u32[]{:S(2)}) copy-start(bf16[1,128,8192]{2,1,0:T(8,128)(2,1)} %param.9) | copy-start | bytes 6291460
  13.7 1.6 %copy-start.2 = (bf16[1,128,8192]{2,1,0:T(8,128)(2,1)S(1)}, bf16[1,128,8192]{2,1,0:T(8,128)(2,1)}, u32[]{:S(2)}) copy-start(bf16[1,128,8192]{2,1,0:T(8,128)(2,1)} %param.10) | copy-start | bytes 6291460
  15.3 33.1 %copy-start.1 = (bf16[1,128,8192]{2,1,0:T(8,128)(2,1)S(1)}, bf16[1,128,8192]{2,1,0:T(8,128)(2,1)}, u32[]{:S(2)}) copy-start(bf16[1,128,8192]{2,1,0:T(8,128)(2,1)} %param.9) | copy-start | bytes 6291460
  17.3 31.1 %collective-permute-start = (bf16[128,8192]{1,0:T(8,128)(2,1)}, bf16[128,8192]{1,0:T(8,128)(2,1)}, u32[]{:S(2)}, u32[]{:S(2)}) collective-permute-start(bf16[128,8192]{1,0:T(8,128)(2,1)} %shard_map.91), channel_id=1, source_target_pairs={{0,16},{16,0},{1,17},{17,1},{2,18},{18,2},{3,19},{19,3},{4,20},{20... | collective-permute-start | bytes 6291464 | tf_op jit(solution)/shard_map/ppermute | solution.py:175
  26.4 8.2 %collective-permute-start.1 = (bf16[5,256,128]{2,1,0:T(8,128)(2,1)S(1)}, bf16[5,256,128]{2,1,0:T(8,128)(2,1)S(1)}, u32[]{:S(2)}, u32[]{:S(2)}) collective-permute-start(bf16[5,256,128]{2,1,0:T(8,128)(2,1)S(1)} %slice.8), channel_id=1, source_target_pairs={{0,128},{16,400},{128,256},{144,16},{256,384},{272,144},{384,0},{4... | collective-permute-start | bytes 983048 | tf_op jit(solution)/shard_map/ppermute | solution.py:193
  28.4 11.8 %collective-permute-start.3 = (bf16[3,256,128]{2,1,0:T(8,128)(2,1)S(1)}, bf16[3,256,128]{2,1,0:T(8,128)(2,1)S(1)}, u32[]{:S(2)}, u32[]{:S(2)}) collective-permute-start(bf16[3,256,128]{2,1,0:T(8,128)(2,1)S(1)} %slice.9), channel_id=1, source_target_pairs={{0,384},{16,144},{128,0},{144,272},{256,128},{272,400},{384,256},{... | collective-permute-start | bytes 589832 | tf_op jit(solution)/shard_map/ppermute | solution.py:193
  31.7 20.9 %collective-permute-start.4 = (bf16[5,256,128]{2,1,0:T(8,128)(2,1)S(1)}, bf16[5,256,128]{2,1,0:T(8,128)(2,1)S(1)}, u32[]{:S(2)}, u32[]{:S(2)}) collective-permute-start(bf16[5,256,128]{2,1,0:T(8,128)(2,1)S(1)} %slice.8), channel_id=1, source_target_pairs={{0,384},{16,144},{128,0},{144,272},{256,128},{272,400},{384,256},{... | collective-permute-start | bytes 983048 | tf_op jit(solution)/shard_map/ppermute | solution.py:193
  34.7 18.0 %collective-permute-start.5 = (bf16[5,256,128]{2,1,0:T(8,128)(2,1)S(1)}, bf16[5,256,128]{2,1,0:T(8,128)(2,1)S(1)}, u32[]{:S(2)}, u32[]{:S(2)}) collective-permute-start(bf16[5,256,128]{2,1,0:T(8,128)(2,1)S(1)} %collective-permute-done.1.refs_1_), channel_id=1, source_target_pairs={{0,128},{16,400},{128,256},{144,16},{256,384},{272,144},{384,0},{4... | collective-permute-start | bytes 983048 | tf_op jit(solution)/shard_map/ppermute | solution.py:193
  38.3 10.1 %collective-permute-start.2 = (bf16[3,256,128]{2,1,0:T(8,128)(2,1)S(1)}, bf16[3,256,128]{2,1,0:T(8,128)(2,1)S(1)}, u32[]{:S(2)}, u32[]{:S(2)}) collective-permute-start(bf16[3,256,128]{2,1,0:T(8,128)(2,1)S(1)} %slice.9), channel_id=1, source_target_pairs={{0,128},{16,400},{128,256},{144,16},{256,384},{272,144},{384,0},{4... | collective-permute-start | bytes 589832 | tf_op jit(solution)/shard_map/ppermute | solution.py:193
  40.2 12.4 %collective-permute-start.6 = (bf16[3,256,128]{2,1,0:T(8,128)(2,1)S(1)}, bf16[3,256,128]{2,1,0:T(8,128)(2,1)S(1)}, u32[]{:S(2)}, u32[]{:S(2)}) collective-permute-start(bf16[3,256,128]{2,1,0:T(8,128)(2,1)S(1)} %collective-permute-done.3.refs_3_), channel_id=1, source_target_pairs={{0,384},{16,144},{128,0},{144,272},{256,128},{272,400},{384,256},{... | collective-permute-start | bytes 589832 | tf_op jit(solution)/shard_map/ppermute | solution.py:193
  48.4 1.6 %copy-start.3 = (bf16[1,128,8192]{2,1,0:T(8,128)(2,1)S(1)}, bf16[1,128,8192]{2,1,0:T(8,128)(2,1)}, u32[]{:S(2)}) copy-start(bf16[1,128,8192]{2,1,0:T(8,128)(2,1)} %param.10) | copy-start | bytes 6291460
  52.5 27.3 %copy-start.4 = (bf16[1,16,16384]{2,1,0:T(8,128)(2,1)S(1)}, bf16[1,16,16384]{2,1,0:T(8,128)(2,1)}, u32[]{:S(2)}) copy-start(bf16[1,16,16384]{2,1,0:T(8,128)(2,1)} %param.17) | copy-start | bytes 1572868
  52.5 27.2 %copy-start.5 = (f32[1,128,128]{2,1,0:T(8,128)S(1)}, f32[1,128,128]{2,1,0:T(8,128)}, u32[]{:S(2)}) copy-start(f32[1,128,128]{2,1,0:T(8,128)} %param.13) | copy-start | bytes 196612
  52.6 27.2 %copy-start.6 = (f32[1,128,128]{2,1,0:T(8,128)S(1)}, f32[1,128,128]{2,1,0:T(8,128)}, u32[]{:S(2)}) copy-start(f32[1,128,128]{2,1,0:T(8,128)} %param.14) | copy-start | bytes 196612
  52.6 27.2 %copy-start.7 = (f32[1,128]{1,0:T(1,128)S(1)}, f32[1,128]{1,0:T(1,128)}, u32[]{:S(2)}) copy-start(f32[1,128]{1,0:T(1,128)} %eig_a.1) | copy-start | bytes 1540
  52.6 27.2 %copy-start.8 = (f32[1,128]{1,0:T(1,128)S(1)}, f32[1,128]{1,0:T(1,128)}, u32[]{:S(2)}) copy-start(f32[1,128]{1,0:T(1,128)} %eig_g.1) | copy-start | bytes 1540
  53.2 8.5 %collective-permute-start.7 = (bf16[2,128,128]{2,1,0:T(8,128)(2,1)S(1)}, bf16[2,128,128]{2,1,0:T(8,128)(2,1)S(1)}, u32[]{:S(2)}, u32[]{:S(2)}) collective-permute-start(bf16[2,128,128]{2,1,0:T(8,128)(2,1)S(1)} %shard_map.94.mine_ref), channel_id=1, source_target_pairs={{0,16},{16,0},{1,17},{17,1},{2,18},{18,2},{3,19},{19,3},{4,20},{20... | collective-permute-start | bytes 196616 | tf_op jit(solution)/shard_map/ppermute | solution.py:175
  75.1 4.6 %collective-permute-start.8 = (f32[64,128]{1,0:T(8,128)S(1)}, f32[64,128]{1,0:T(8,128)S(1)}, u32[]{:S(2)}, u32[]{:S(2)}) collective-permute-start(f32[64,128]{1,0:T(8,128)S(1)} %shard_map.96.mine_ref), channel_id=1, source_target_pairs={{0,16},{16,0},{1,17},{17,1},{2,18},{18,2},{3,19},{19,3},{4,20},{20... | collective-permute-start | bytes 98312 | tf_op jit(solution)/shard_map/ppermute | solution.py:175

commit v10 on v7

--- a/solution.py
+++ b/solution.py
@@ -147,7 +147,7 @@
     n_y, n_z = lax.axis_size("y"), lax.axis_size("zlo")
     depth, rank = proj_in.shape[1:]
     line_blocks = 2 * n_z
-    part = 3 * line_blocks // 4
+    part = line_blocks // 2
     local, local_g = acts[0], grads_out[0]
     n_tok = local.shape[0]
     hbm = pl.BlockSpec(memory_space=pltpu.HBM)
@@ -215,24 +215,14 @@
         here, local, local_g, got, *near.values(), cost_estimate=cost,
     )
     mine = call(finish, shape(2, n_tok, rank), [VMEM] * (2 + len(last)), ahead, acc, *last)
-
-    def at(y, z, core):
-        return (y * n_z + z) * 2 + core
-
-    def exchange(x, core_along_y):
-        other = 1 - core_along_y
-        groups = [[at(y, z, core_along_y) for y in range(n_y)] for z in range(n_z)]
-        groups += [[at(y, z, other) for z in range(n_z)] for y in range(n_y)]
-        return lax.all_to_all(x, CTX, 0, 0, axis_index_groups=groups, tiled=True)
-
     grad = call(
         functools.partial(outer, float(tokens)), shape(n_y, rank, rank),
         [SMEM, VMEM, VMEM], here, mine, permute(mine, "core", 1),
     )
-    grad = call(add_up, shape(n_z, rank, rank), [VMEM], exchange(grad, 0))
+    grad = call(add_up, shape(n_z, rank, rank), [VMEM], all_to_all(grad, "y"))
     sent = call(
         score, shape(n_layer, train_grads.shape[1], dtype=F32), [VMEM] * 6,
-        exchange(grad, 1), basis_a[0], basis_g[0], eig_a, eig_g, train_grads[0],
+        all_to_all(grad, "zlo"), basis_a[0], basis_g[0], eig_a, eig_g, train_grads[0],
     )
     return jnp.sum(lax.all_to_all(sent, LAYER, 0, 0), 0)
 

time: 109 us -> 103 us (0.945)
  waiting for transfers between devices: 13.9 us -> 6.61 us
  blocking collectives: 45.5 us -> 47.4 us
    ppermute x6, waiting for transfers between devices: 7.85 us -> 0.6 us  [along_y(): return lax.ppermute(x, ('y', 'core'), moves)]
    all_to_all x1, blocking collectives: 25.5 us -> 26.9 us  [body(): return jnp.sum(lax.all_to_all(sent, LAYER, 0, 0), 0)]
  transfers between devices with their start and end apart: 9 -> 9, of which waited for: 4 -> 3; matrix products, arithmetic and copies ran while one was open for 0% -> 0% of each run, Pallas kernels for 4% -> 4%
where the time goes in v10:
time: 103 us
  blocking collectives  47.4 us (46%)
  starting transfers between devices  34 us (33%)
  Pallas kernels  8.91 us (9%)
  waiting for transfers between devices  6.61 us (6%)
  local copies, waits for them, and re-layouts  4.84 us (5%)
    all_to_all x1, blocking collectives, body(): return jnp.sum(lax.all_to_all(sent, LAYER, 0, 0), 0)  26.9 us
    ppermute x6, starting transfers between devices, along_y(): return lax.ppermute(x, ('y', 'core'), moves)  21.2 us
    all_to_all x2, blocking collectives, all_to_all(): return lax.all_to_all(x, axis, 0, 0, tiled=True)  20.5 us
    pallas_call x7, Pallas kernels, call(): pl.pallas_call(kernel, out_shape=shape, in_specs=in_specs, compiler_param...  8.91 us
    all_to_all x1, starting transfers between devices, all_to_all(): return lax.all_to_all(x, axis, 0, 0, tiled=True)  8.87 us
    unnamed x18, local copies, waits for them, and re-layouts  4.8 us
    all_to_all x1, waiting for transfers between devices, all_to_all(): return lax.all_to_all(x, axis, 0, 0, tiled=True)  4.79 us
    ppermute x2, starting transfers between devices, permute(): return lax.ppermute(x, axis, [(i, (i + step) % size) for i in range(size)])  3.95 us
  transfers between devices with their start and end apart: 9, of which 3 were waited for; matrix products, arithmetic and copies ran while one was open for 0% of the time, Pallas kernels for 4%

profile of v10, /device:TPU:32, one launch (start us, length us, event | category | flops | bytes accessed | tf_op | source)
XLA Modules:
  0.0 102.6 jit_solution(8570061622558216347)
XLA Ops:
  0.0 1.7 %shard_map.92 = bf16[4,2,256,128]{3,2,1,0:T(8,128)(2,1)} custom-call(bf16[256,128]{1,0:T(8,128)(2,1)} %bitcast.22, bf16[256,128]{1,0:T(8,128)(2,1)} %bitcast.23), custom_call_target="tpu_custom_call" | custom-call | tf_op jit(solution)/shard_map/pallas_call | solution.py:159
  1.8 8.9 %all-to-all-start = ((bf16[8,256,128]{2,1,0:T(8,128)(2,1)}), bf16[8,256,128]{2,1,0:T(8,128)(2,1)S(1)}, u32[]{:S(2)}, u32[]{:S(2)}) async-start(bf16[8,256,128]{2,1,0:T(8,128)(2,1)} %bitcast.21), calls=%async_computation | async-start | bytes 1048576 | tf_op jit(solution)/shard_map/all_to_all | solution.py:171
  10.6 0.1 pad_add_fusion.here_ref
  10.7 0.0 copy-start
  10.7 1.6 %copy-done = bf16[1,128,8192]{2,1,0:T(8,128)(2,1)S(1)} copy-done((bf16[1,128,8192]{2,1,0:T(8,128)(2,1)S(1)}, bf16[1,128,8192]{2,1,0:T(8,128)(2,1)}, u32[]{:S(2)}) %copy-start) | copy-done | bytes 2097176
  12.3 0.0 copy-start.2
  12.3 1.6 %copy-done.2 = bf16[1,128,8192]{2,1,0:T(8,128)(2,1)S(1)} copy-done((bf16[1,128,8192]{2,1,0:T(8,128)(2,1)S(1)}, bf16[1,128,8192]{2,1,0:T(8,128)(2,1)}, u32[]{:S(2)}) %copy-start.2) | copy-done | bytes 2097176
  13.9 0.0 copy-start.1
  13.9 2.0 %shard_map.91 = bf16[128,8192]{1,0:T(8,128)(2,1)} custom-call(s32[4]{0:T(128)S(1)} %pad_add_fusion.here_ref, bf16[128,8192]{1,0:T(8,128)(2,1)S(1)} %bitcast.13, bf16[128,8192]{1,0:T(8,128)(2,1)S(1)} %bitcast.15), custom_call_target="tpu_custom_call" | custom-call | tf_op jit(solution)/shard_map/pallas_call | solution.py:159
  15.9 2.0 %collective-permute-start = (bf16[128,8192]{1,0:T(8,128)(2,1)}, bf16[128,8192]{1,0:T(8,128)(2,1)}, u32[]{:S(2)}, u32[]{:S(2)}) collective-permute-start(bf16[128,8192]{1,0:T(8,128)(2,1)} %shard_map.91), channel_id=1, source_target_pairs={{0,16},{16,0},{1,17},{17,1},{2,18},{18,2},{3,19},{19,3},{4,20},{20... | collective-permute-start | bytes 6291464 | tf_op jit(solution)/shard_map/ppermute | solution.py:175
  18.0 4.8 %all-to-all-done.refs_0_ = bf16[8,256,128]{2,1,0:T(8,128)(2,1)S(1)} async-done(((bf16[8,256,128]{2,1,0:T(8,128)(2,1)}), bf16[8,256,128]{2,1,0:T(8,128)(2,1)S(1)}, u32[]{:S(2)}, u32[]{:S(2)}) %all-to-all-start) | async-done | bytes 524320 | tf_op jit(solution)/shard_map/all_to_all | solution.py:171
  22.8 1.9 %collective-permute-start.1 = (bf16[4,256,128]{2,1,0:T(8,128)(2,1)S(1)}, bf16[4,256,128]{2,1,0:T(8,128)(2,1)S(1)}, u32[]{:S(2)}, u32[]{:S(2)}) collective-permute-start(bf16[4,256,128]{2,1,0:T(8,128)(2,1)S(1)} %get-tuple-element.10), channel_id=1, source_target_pairs={{0,128},{16,400},{128,256},{144,16},{256,384},{272,144},{384,0},{4... | collective-permute-start | bytes 786440 | tf_op jit(solution)/shard_map/ppermute | solution.py:193
  24.7 5.1 %collective-permute-start.3 = (bf16[4,256,128]{2,1,0:T(8,128)(2,1)S(1)}, bf16[4,256,128]{2,1,0:T(8,128)(2,1)S(1)}, u32[]{:S(2)}, u32[]{:S(2)}) collective-permute-start(bf16[4,256,128]{2,1,0:T(8,128)(2,1)S(1)} %get-tuple-element.9), channel_id=1, source_target_pairs={{0,384},{16,144},{128,0},{144,272},{256,128},{272,400},{384,256},{... | collective-permute-start | bytes 786440 | tf_op jit(solution)/shard_map/ppermute | solution.py:193
  29.9 1.9 %collective-permute-start.2 = (bf16[4,256,128]{2,1,0:T(8,128)(2,1)S(1)}, bf16[4,256,128]{2,1,0:T(8,128)(2,1)S(1)}, u32[]{:S(2)}, u32[]{:S(2)}) collective-permute-start(bf16[4,256,128]{2,1,0:T(8,128)(2,1)S(1)} %get-tuple-element.9), channel_id=1, source_target_pairs={{0,128},{16,400},{128,256},{144,16},{256,384},{272,144},{384,0},{4... | collective-permute-start | bytes 786440 | tf_op jit(solution)/shard_map/ppermute | solution.py:193
  31.8 5.1 %collective-permute-start.4 = (bf16[4,256,128]{2,1,0:T(8,128)(2,1)S(1)}, bf16[4,256,128]{2,1,0:T(8,128)(2,1)S(1)}, u32[]{:S(2)}, u32[]{:S(2)}) collective-permute-start(bf16[4,256,128]{2,1,0:T(8,128)(2,1)S(1)} %get-tuple-element.10), channel_id=1, source_target_pairs={{0,384},{16,144},{128,0},{144,272},{256,128},{272,400},{384,256},{... | collective-permute-start | bytes 786440 | tf_op jit(solution)/shard_map/ppermute | solution.py:193
  36.9 0.0 collective-permute-done.1.refs_1_
  36.9 1.9 %collective-permute-start.5 = (bf16[4,256,128]{2,1,0:T(8,128)(2,1)S(1)}, bf16[4,256,128]{2,1,0:T(8,128)(2,1)S(1)}, u32[]{:S(2)}, u32[]{:S(2)}) collective-permute-start(bf16[4,256,128]{2,1,0:T(8,128)(2,1)S(1)} %collective-permute-done.1.refs_1_), channel_id=1, source_target_pairs={{0,128},{16,400},{128,256},{144,16},{256,384},{272,144},{384,0},{4... | collective-permute-start | bytes 786440 | tf_op jit(solution)/shard_map/ppermute | solution.py:193
  38.9 0.0 collective-permute-done.3.refs_3_
  38.9 5.1 %collective-permute-start.6 = (bf16[4,256,128]{2,1,0:T(8,128)(2,1)S(1)}, bf16[4,256,128]{2,1,0:T(8,128)(2,1)S(1)}, u32[]{:S(2)}, u32[]{:S(2)}) collective-permute-start(bf16[4,256,128]{2,1,0:T(8,128)(2,1)S(1)} %collective-permute-done.3.refs_3_), channel_id=1, source_target_pairs={{0,384},{16,144},{128,0},{144,272},{256,128},{272,400},{384,256},{... | collective-permute-start | bytes 786440 | tf_op jit(solution)/shard_map/ppermute | solution.py:193
  44.0 0.0 collective-permute-done.got_ref
  44.0 0.0 collective-permute-done.2.refs_2_
  44.0 0.0 copy-done.1
  44.1 0.0 copy-start.3
  44.1 1.6 %copy-done.3 = bf16[1,128,8192]{2,1,0:T(8,128)(2,1)S(1)} copy-done((bf16[1,128,8192]{2,1,0:T(8,128)(2,1)S(1)}, bf16[1,128,8192]{2,1,0:T(8,128)(2,1)}, u32[]{:S(2)}) %copy-start.3) | copy-done | bytes 2097176
  45.6 2.6 %shard_map.93 = (f32[2,128,128]{2,1,0:T(8,128)S(1)}, bf16[2,128,3072]{2,1,0:T(8,128)(2,1)S(1)}) custom-call(s32[4]{0:T(128)S(1)} %pad_add_fusion.here_ref, bf16[128,8192]{1,0:T(8,128)(2,1)S(1)} %bitcast.14, bf16[128,8192]{1,0:T(8,128)(2,1)S(1)} %bitcast.16, bf16[128,8192]{1,0:T(8,128)(2,1)} %collective-permute-done.got_ref, ...), custom_call_target="tpu_custom_call" | custom-call | flops 335544320 | bytes 6291456 | tf_op jit(solution)/shard_map/pallas_call | solution.py:159
  48.2 0.0 copy-start.4
  48.2 0.0 copy-start.5
  48.2 0.0 copy-start.6
  48.3 0.0 copy-start.7
  48.3 0.0 copy-start.8
  48.3 0.0 collective-permute-done.4.refs_0_
  48.3 0.6 collective-permute-done.5.refs_1_
  48.9 0.0 collective-permute-done.6.refs_2_
  48.9 0.6 shard_map.94.mine_ref
  49.4 1.9 %collective-permute-start.7 = (bf16[2,128,128]{2,1,0:T(8,128)(2,1)S(1)}, bf16[2,128,128]{2,1,0:T(8,128)(2,1)S(1)}, u32[]{:S(2)}, u32[]{:S(2)}) collective-permute-start(bf16[2,128,128]{2,1,0:T(8,128)(2,1)S(1)} %shard_map.94.mine_ref), channel_id=1, source_target_pairs={{0,16},{16,0},{1,17},{17,1},{2,18},{18,2},{3,19},{19,3},{4,20},{20... | collective-permute-start | bytes 196616 | tf_op jit(solution)/shard_map/ppermute | solution.py:175
  51.4 1.2 %collective-permute-done.7.got_ref = bf16[2,128,128]{2,1,0:T(8,128)(2,1)S(1)} collective-permute-done((bf16[2,128,128]{2,1,0:T(8,128)(2,1)S(1)}, bf16[2,128,128]{2,1,0:T(8,128)(2,1)S(1)}, u32[]{:S(2)}, u32[]{:S(2)}) %collective-permute-start.7) | collective-permute-done | bytes 65568 | tf_op jit(solution)/shard_map/ppermute | solution.py:175
  52.6 0.7 shard_map.95
  53.3 9.7 %all_to_all.24.parts_ref = bf16[4,128,128]{2,1,0:T(8,128)(2,1)S(1)} all-to-all(bf16[4,128,128]{2,1,0:T(8,128)(2,1)S(1)} %shard_map.95), channel_id=1, replica_groups=mesh['y'=4,'zlo'=4,'core'=2,'zhi'=4,'x'=4] {'y'}, dimensions={0} | all-to-all | bytes 262144 | tf_op jit(solution)/shard_map/all_to_all | solution.py:171
  63.1 10.8 %all_to_all.25.parts_ref = bf16[4,128,128]{2,1,0:T(8,128)(2,1)S(1)} all-to-all(bf16[4,128,128]{2,1,0:T(8,128)(2,1)S(1)} %shard_map.96), channel_id=1, replica_groups=mesh['y'=4,'zlo'=4,'core'=2,'zhi'=4,'x'=4] {'zlo'}, dimensions={0} | all-to-all | bytes 262144 | tf_op jit(solution)/shard_map/all_to_all | solution.py:171
  73.9 0.0 copy-done.4
  73.9 0.0 copy-done.5
  73.9 0.0 copy-done.6
  73.9 0.0 copy-done.7
  73.9 0.0 copy-done.8
  73.9 1.2 %shard_map.97 = f32[16,16]{1,0:T(8,128)S(1)} custom-call(bf16[4,128,128]{2,1,0:T(8,128)(2,1)S(1)} %all_to_all.25.parts_ref, f32[128,128]{1,0:T(8,128)S(1)} %bitcast.18, f32[128,128]{1,0:T(8,128)S(1)} %bitcast.19, f32[1,128]{1,0:T(1,128)S(1)} %copy-done.7, f32[1,128]{1,0:T(1,128)S(1)} %copy-done.8, bf16[16,16384]{1,0:T(8,128)(2,1)S(1)} %bitcast.17), custom_call_target="tpu_custom_call" | custom-call | tf_op jit(solution)/shard_map/pallas_call | solution.py:159
  75.1 26.9 %all_to_all.26 = f32[16,1,16]{2,1,0:T(1,128)S(1)} all-to-all(f32[16,1,16]{2,1,0:T(1,128)S(1)} %bitcast.20), channel_id=1, replica_groups=mesh['y'=4,'zlo'=4,'core'=2,'zhi'=4,'x'=4] {'zhi','x'}, dimensions={0} | all-to-all | bytes 2048 | tf_op jit(solution)/shard_map/all_to_all | solution.py:227
  102.0 0.5 reduce_sum.9
  (2 shorter events, 0.1 us)
Async XLA Ops:
  1.8 21.0 %all-to-all-start = ((bf16[8,256,128]{2,1,0:T(8,128)(2,1)}), bf16[8,256,128]{2,1,0:T(8,128)(2,1)S(1)}, u32[]{:S(2)}, u32[]{:S(2)}) async-start(bf16[8,256,128]{2,1,0:T(8,128)(2,1)} %bitcast.21), calls=%async_computation | async-start | bytes 1048576 | tf_op jit(solution)/shard_map/all_to_all | solution.py:171
  10.7 1.6 %copy-start = (bf16[1,128,8192]{2,1,0:T(8,128)(2,1)S(1)}, bf16[1,128,8192]{2,1,0:T(8,128)(2,1)}, u32[]{:S(2)}) copy-start(bf16[1,128,8192]{2,1,0:T(8,128)(2,1)} %param.9) | copy-start | bytes 6291460
  12.3 1.6 %copy-start.2 = (bf16[1,128,8192]{2,1,0:T(8,128)(2,1)S(1)}, bf16[1,128,8192]{2,1,0:T(8,128)(2,1)}, u32[]{:S(2)}) copy-start(bf16[1,128,8192]{2,1,0:T(8,128)(2,1)} %param.10) | copy-start | bytes 6291460
  13.9 30.2 %copy-start.1 = (bf16[1,128,8192]{2,1,0:T(8,128)(2,1)S(1)}, bf16[1,128,8192]{2,1,0:T(8,128)(2,1)}, u32[]{:S(2)}) copy-start(bf16[1,128,8192]{2,1,0:T(8,128)(2,1)} %param.9) | copy-start | bytes 6291460
  15.9 28.1 %collective-permute-start = (bf16[128,8192]{1,0:T(8,128)(2,1)}, bf16[128,8192]{1,0:T(8,128)(2,1)}, u32[]{:S(2)}, u32[]{:S(2)}) collective-permute-start(bf16[128,8192]{1,0:T(8,128)(2,1)} %shard_map.91), channel_id=1, source_target_pairs={{0,16},{16,0},{1,17},{17,1},{2,18},{18,2},{3,19},{19,3},{4,20},{20... | collective-permute-start | bytes 6291464 | tf_op jit(solution)/shard_map/ppermute | solution.py:175
  22.8 14.1 %collective-permute-start.1 = (bf16[4,256,128]{2,1,0:T(8,128)(2,1)S(1)}, bf16[4,256,128]{2,1,0:T(8,128)(2,1)S(1)}, u32[]{:S(2)}, u32[]{:S(2)}) collective-permute-start(bf16[4,256,128]{2,1,0:T(8,128)(2,1)S(1)} %get-tuple-element.10), channel_id=1, source_target_pairs={{0,128},{16,400},{128,256},{144,16},{256,384},{272,144},{384,0},{4... | collective-permute-start | bytes 786440 | tf_op jit(solution)/shard_map/ppermute | solution.py:193
  24.7 14.2 %collective-permute-start.3 = (bf16[4,256,128]{2,1,0:T(8,128)(2,1)S(1)}, bf16[4,256,128]{2,1,0:T(8,128)(2,1)S(1)}, u32[]{:S(2)}, u32[]{:S(2)}) collective-permute-start(bf16[4,256,128]{2,1,0:T(8,128)(2,1)S(1)} %get-tuple-element.9), channel_id=1, source_target_pairs={{0,384},{16,144},{128,0},{144,272},{256,128},{272,400},{384,256},{... | collective-permute-start | bytes 786440 | tf_op jit(solution)/shard_map/ppermute | solution.py:193
  29.9 14.2 %collective-permute-start.2 = (bf16[4,256,128]{2,1,0:T(8,128)(2,1)S(1)}, bf16[4,256,128]{2,1,0:T(8,128)(2,1)S(1)}, u32[]{:S(2)}, u32[]{:S(2)}) collective-permute-start(bf16[4,256,128]{2,1,0:T(8,128)(2,1)S(1)} %get-tuple-element.9), channel_id=1, source_target_pairs={{0,128},{16,400},{128,256},{144,16},{256,384},{272,144},{384,0},{4... | collective-permute-start | bytes 786440 | tf_op jit(solution)/shard_map/ppermute | solution.py:193
  31.8 16.5 %collective-permute-start.4 = (bf16[4,256,128]{2,1,0:T(8,128)(2,1)S(1)}, bf16[4,256,128]{2,1,0:T(8,128)(2,1)S(1)}, u32[]{:S(2)}, u32[]{:S(2)}) collective-permute-start(bf16[4,256,128]{2,1,0:T(8,128)(2,1)S(1)} %get-tuple-element.10), channel_id=1, source_target_pairs={{0,384},{16,144},{128,0},{144,272},{256,128},{272,400},{384,256},{... | collective-permute-start | bytes 786440 | tf_op jit(solution)/shard_map/ppermute | solution.py:193
  36.9 11.9 %collective-permute-start.5 = (bf16[4,256,128]{2,1,0:T(8,128)(2,1)S(1)}, bf16[4,256,128]{2,1,0:T(8,128)(2,1)S(1)}, u32[]{:S(2)}, u32[]{:S(2)}) collective-permute-start(bf16[4,256,128]{2,1,0:T(8,128)(2,1)S(1)} %collective-permute-done.1.refs_1_), channel_id=1, source_target_pairs={{0,128},{16,400},{128,256},{144,16},{256,384},{272,144},{384,0},{4... | collective-permute-start | bytes 786440 | tf_op jit(solution)/shard_map/ppermute | solution.py:193
  38.9 10.0 %collective-permute-start.6 = (bf16[4,256,128]{2,1,0:T(8,128)(2,1)S(1)}, bf16[4,256,128]{2,1,0:T(8,128)(2,1)S(1)}, u32[]{:S(2)}, u32[]{:S(2)}) collective-permute-start(bf16[4,256,128]{2,1,0:T(8,128)(2,1)S(1)} %collective-permute-done.3.refs_3_), channel_id=1, source_target_pairs={{0,384},{16,144},{128,0},{144,272},{256,128},{272,400},{384,256},{... | collective-permute-start | bytes 786440 | tf_op jit(solution)/shard_map/ppermute | solution.py:193
  44.1 1.6 %copy-start.3 = (bf16[1,128,8192]{2,1,0:T(8,128)(2,1)S(1)}, bf16[1,128,8192]{2,1,0:T(8,128)(2,1)}, u32[]{:S(2)}) copy-start(bf16[1,128,8192]{2,1,0:T(8,128)(2,1)} %param.10) | copy-start | bytes 6291460
  48.2 25.6 %copy-start.4 = (bf16[1,16,16384]{2,1,0:T(8,128)(2,1)S(1)}, bf16[1,16,16384]{2,1,0:T(8,128)(2,1)}, u32[]{:S(2)}) copy-start(bf16[1,16,16384]{2,1,0:T(8,128)(2,1)} %param.17) | copy-start | bytes 1572868
  48.2 25.6 %copy-start.5 = (f32[1,128,128]{2,1,0:T(8,128)S(1)}, f32[1,128,128]{2,1,0:T(8,128)}, u32[]{:S(2)}) copy-start(f32[1,128,128]{2,1,0:T(8,128)} %param.13) | copy-start | bytes 196612
  48.2 25.6 %copy-start.6 = (f32[1,128,128]{2,1,0:T(8,128)S(1)}, f32[1,128,128]{2,1,0:T(8,128)}, u32[]{:S(2)}) copy-start(f32[1,128,128]{2,1,0:T(8,128)} %param.14) | copy-start | bytes 196612
  48.3 25.6 %copy-start.7 = (f32[1,128]{1,0:T(1,128)S(1)}, f32[1,128]{1,0:T(1,128)}, u32[]{:S(2)}) copy-start(f32[1,128]{1,0:T(1,128)} %eig_a.1) | copy-start | bytes 1540
  48.3 25.6 %copy-start.8 = (f32[1,128]{1,0:T(1,128)S(1)}, f32[1,128]{1,0:T(1,128)}, u32[]{:S(2)}) copy-start(f32[1,128]{1,0:T(1,128)} %eig_g.1) | copy-start | bytes 1540
  49.4 3.1 %collective-permute-start.7 = (bf16[2,128,128]{2,1,0:T(8,128)(2,1)S(1)}, bf16[2,128,128]{2,1,0:T(8,128)(2,1)S(1)}, u32[]{:S(2)}, u32[]{:S(2)}) collective-permute-start(bf16[2,128,128]{2,1,0:T(8,128)(2,1)S(1)} %shard_map.94.mine_ref), channel_id=1, source_target_pairs={{0,16},{16,0},{1,17},{17,1},{2,18},{18,2},{3,19},{19,3},{4,20},{20... | collective-permute-start | bytes 196616 | tf_op jit(solution)/shard_map/ppermute | solution.py:175
